TPU v7x, 256 devices: a whole 4x4x8 slice. The times are simulated.
256 devices in a mesh: dp: 16 (over x, y), expert: 16 (over z, core).
Axes of the slice: x: 4, y: 4, z: 8, core: 2. Of those that a mesh axis runs over, the one named last changes fastest.
Arguments:
- hidden_in: bfloat16 [256, 2, 2880], P(('expert', 'dp')), may hold values from -6 to 6
- queries: bfloat16 [256, 2, 4096], P(('expert', 'dp')), may hold values from -2 to 2
- new_keys: bfloat16 [256, 2, 512], P(('expert', 'dp')), may hold values from -2 to 2
- new_values: bfloat16 [256, 2, 512], P(('expert', 'dp')), may hold values from -6 to 6
- key_cache: bfloat16 [256, 512, 512], P(('expert', 'dp')), may hold values from -2 to 2
- value_cache: bfloat16 [256, 512, 512], P(('expert', 'dp')), may hold values from -6 to 6
- prompt_lengths: int32 [256], P(('expert', 'dp')), may hold values from 64 to 512, as said below
- out_weight: bfloat16 [4096, 2880], P('expert'), may hold values from -0.375 to 0.375
- norm_gain: float32 [2880], replicated, may hold values from 0.1 to 1.9
- expert_ids: int32 [256, 2, 4], P('expert'), may hold values from 0 to 31, all different within a row; in each aligned block of 32 rows (0 to 31, 32 to 63, ..., all dimensions but the last counted through in order) at most 12 rows name the same one
- top_logits: bfloat16 [256, 2, 4], P('expert'), may hold values from -4 to 4
- gate_weight: bfloat16 [32, 2880, 2880], P('expert', None, 'dp'), may hold values from -0.109375 to 0.109375
- up_weight: bfloat16 [32, 2880, 2880], P('expert', None, 'dp'), may hold values from -0.109375 to 0.109375
- down_weight: bfloat16 [32, 2880, 2880], P('expert', 'dp'), may hold values from -0.109375 to 0.109375
Outputs:
- layer_out: bfloat16 [256, 2, 2880], P(('expert', 'dp'))
Inputs may be any that keep to these rules, and one draw needn't show every extreme that they name: `prompt_lengths`: some row has exactly 512 live slots. `expert_ids`: A row names 4 different experts at each position. Over the 16 rows held by one index of the expert axis and both positions, no expert is named more than 12 times, and in some such group one expert is named exactly 12 times.
All inputs are finite; a program needn't handle non-finite values.
Results may differ from a plain program's by a relative error of at most 0.02.
Values may be sent and summed in bfloat16 or wider, within the bound.
No kernel may reach another device: no remote copies, remote signals or barrier semaphores. Data moves between devices by JAX's collectives and lax.ppermute only.
A program may use at most 128 MiB of HBM per device.

v0:
```python
import jax
import jax.numpy as jnp
from jax import lax
from jax.sharding import PartitionSpec as P

HQ = 64
KVH = 8
HD = 64


def attend_single(query_rows, fresh_keys, fresh_values, cache_keys, cache_values, length):
    step_count = query_rows.shape[0]
    cache_len = cache_keys.shape[0]
    keys_all = jnp.concatenate([cache_keys, fresh_keys], axis=0).reshape(
        cache_len + step_count, KVH, HD
    )
    values_all = jnp.concatenate([cache_values, fresh_values], axis=0).reshape(
        cache_len + step_count, KVH, HD
    )
    query_heads = query_rows.reshape(step_count, KVH, HQ // KVH, HD)
    scores = (
        jnp.einsum("sgqe,kge->sgqk", query_heads, keys_all, preferred_element_type=jnp.float32)
        * 0.125
    )
    position = jnp.arange(cache_len + step_count, dtype=jnp.int32)
    step_ids = jnp.arange(step_count, dtype=jnp.int32)
    visible = (position[None, :] < length) | (position[None, :] >= cache_len) & (
        position[None, :] - cache_len <= step_ids[:, None]
    )
    exp_scores = jnp.where(visible[:, None, None, :], jnp.exp(scores), jnp.zeros_like(scores))
    attn_probs = (exp_scores / jnp.sum(exp_scores, axis=-1, keepdims=True)).astype(jnp.bfloat16)
    attended = jnp.einsum(
        "sgqk,kge->sgqe", attn_probs, values_all, preferred_element_type=jnp.float32
    )
    return attended.astype(jnp.bfloat16).reshape(step_count, HQ * HD)


def rms_normed(residual, norm_gain):
    inverse_rms = lax.rsqrt(jnp.mean(residual * residual, axis=-1, keepdims=True) + 1e-05)
    return (residual * inverse_rms * norm_gain).astype(jnp.bfloat16)


def swiglu_act(gate_vals, up_vals):
    return (gate_vals * jax.nn.sigmoid(1.702 * gate_vals) * (up_vals + 1.0)).astype(jnp.bfloat16)


def expert_partials(slot_block, gate_weight, up_weight, down_weight):
    results = []
    for local_expert in range(slot_block.shape[1]):
        row_block = slot_block[:, local_expert].reshape(-1, slot_block.shape[3])
        gate_vals = jnp.dot(
            row_block, gate_weight[local_expert], preferred_element_type=jnp.float32
        )
        up_vals = jnp.dot(row_block, up_weight[local_expert], preferred_element_type=jnp.float32)
        activated = swiglu_act(gate_vals, up_vals)
        partial_out = jnp.dot(
            activated, down_weight[local_expert], preferred_element_type=jnp.float32
        )
        results.append(
            partial_out.reshape(slot_block.shape[0], slot_block.shape[2], slot_block.shape[3])
        )
    return jnp.stack(results, axis=1)


def routing_tables(chosen_ids, chosen_logits, experts_all, capacity):
    flat_ids = chosen_ids.reshape(-1, chosen_ids.shape[-1])
    exp_logits = jnp.exp(chosen_logits.reshape(flat_ids.shape).astype(jnp.float32))
    mix_weights = exp_logits / jnp.sum(exp_logits, axis=-1, keepdims=True)
    labels = jnp.arange(experts_all, dtype=jnp.int32)
    match_int = (flat_ids[:, :, None] == labels[None, None, :]).astype(jnp.int32)
    hits_int = jnp.sum(match_int, axis=1)
    slot_int = jnp.cumsum(hits_int, axis=0) - hits_int
    places = jnp.arange(capacity, dtype=jnp.int32)
    select = (
        hits_int.T[:, None, :] * (slot_int.T[:, None, :] == places[None, :, None]).astype(jnp.int32)
    ).astype(jnp.float32)
    token_slots = jnp.take_along_axis(slot_int, flat_ids, axis=1)
    source_rows = flat_ids * capacity + token_slots
    return (select, source_rows, mix_weights)


def gathered_combine(returned_flat, source_rows, mix_weights):
    picked = jnp.take(returned_flat, source_rows.reshape(-1), axis=0)
    picked = picked.reshape(source_rows.shape[0], source_rows.shape[1], returned_flat.shape[1])
    return jnp.sum(picked * mix_weights[:, :, None], axis=1)


def on_device(
    hidden_in,
    queries,
    new_keys,
    new_values,
    key_cache,
    value_cache,
    prompt_lengths,
    out_weight,
    norm_gain,
    expert_ids,
    top_logits,
    gate_weight,
    up_weight,
    down_weight,
):
    row_dev = hidden_in.shape[0]
    step_count = hidden_in.shape[1]
    model_width = hidden_in.shape[2]
    per_index = gate_weight.shape[0]
    expert_group = lax.axis_size("expert")
    experts_all = per_index * expert_group
    attended = jax.vmap(attend_single)(
        queries, new_keys, new_values, key_cache, value_cache, prompt_lengths
    )
    by_heads = lax.all_to_all(attended, "expert", split_axis=2, concat_axis=0, tiled=True)
    projected = lax.psum_scatter(
        jnp.einsum("rsf,fd->rsd", by_heads, out_weight, preferred_element_type=jnp.float32).astype(
            jnp.bfloat16
        ),
        "expert",
        scatter_dimension=0,
        tiled=True,
    ).astype(jnp.float32)
    residual = hidden_in.astype(jnp.float32) + projected
    normed = rms_normed(residual, norm_gain)
    capacity = row_dev * step_count
    start_row = lax.axis_index("dp") * row_dev
    mine_ids = lax.dynamic_slice_in_dim(expert_ids, start_row, row_dev, 0)
    mine_logits = lax.dynamic_slice_in_dim(top_logits, start_row, row_dev, 0)
    select, source_rows, mix_weights = routing_tables(mine_ids, mine_logits, experts_all, capacity)
    dispatch = jnp.einsum(
        "xct,td->xcd",
        select.astype(jnp.bfloat16),
        normed.reshape(-1, model_width),
        preferred_element_type=jnp.float32,
    )
    dispatch = dispatch.astype(jnp.bfloat16).reshape(expert_group, per_index, capacity, model_width)
    arrived = lax.all_to_all(dispatch, "expert", split_axis=0, concat_axis=0, tiled=True)
    partials = expert_partials(
        lax.all_gather(arrived, "dp", axis=0, tiled=True), gate_weight, up_weight, down_weight
    )
    summed = lax.psum_scatter(
        partials.astype(jnp.bfloat16), "dp", scatter_dimension=0, tiled=True
    ).astype(jnp.float32)
    returned = lax.all_to_all(
        summed.astype(jnp.bfloat16), "expert", split_axis=0, concat_axis=0, tiled=True
    ).astype(summed.dtype)
    moe_flat = gathered_combine(
        returned.reshape(experts_all * capacity, model_width), source_rows, mix_weights
    )
    moe_out = moe_flat.reshape(row_dev, step_count, model_width)
    return (residual + moe_out).astype(jnp.bfloat16)


def solution(mesh):
    placed = (
        P(("expert", "dp"), None, None),
        P(("expert", "dp"), None, None),
        P(("expert", "dp"), None, None),
        P(("expert", "dp"), None, None),
        P(("expert", "dp"), None, None),
        P(("expert", "dp"), None, None),
        P(("expert", "dp")),
        P("expert", None),
        P(),
        P("expert", None, None),
        P("expert", None, None),
        P("expert", None, "dp"),
        P("expert", None, "dp"),
        P("expert", "dp", None),
    )
    return jax.shard_map(
        on_device,
        mesh=mesh,
        in_specs=placed,
        out_specs=P(("expert", "dp"), None, None),
        check_vma=False,
    )
```

profile of v0, /device:TPU:8, one launch (start us, length us, event | category | flops | bytes accessed | tf_op | source)
XLA Modules:
  0.0 471.1 jit_solution(13765269799745457546)
XLA Ops:
  7.4 0.8 reshape.325
  8.2 1.1 pad_maximum_fusion.2
  9.3 0.3 copy.81
  9.6 0.3 copy.80
  9.9 0.3 fusion.39
  10.3 0.3 fusion.10
  10.6 0.1 reshape.327
  10.8 3.8 copy.84
  14.6 0.5 broadcast.314
  15.1 23.5 %reduce.9 = bf16[4096,2]{1,0:T(8,128)(2,1)S(1)} reduce(bf16[4096,1,2]{2,1,0:T(2,128)(2,1)} %bitcast.98, bf16[]{:T(256)} %broadcast.314), dimensions={1}, to_apply=%bitcast.89.reduce_sub_computation | reduce | bytes 32770
  38.6 2.2 reshape.367
  40.8 8.6 %all-to-all-start = ((bf16[16,2,256]{2,1,0:T(2,128)(2,1)}), bf16[16,2,256]{2,1,0:T(2,128)(2,1)S(1)}, u32[]{:S(2)}, u32[]{:S(2)}) async-start(bf16[16,2,256]{2,1,0:T(2,128)(2,1)} %reshape.367), calls=%async_computation | async-start | bytes 32768 | tf_op jit(solution)/shard_map/all_to_all | solution.py:113
  49.4 0.2 dynamic-slice_reduce_fusion
  49.6 0.1 convert_reduce_fusion
  49.8 7.2 %all-to-all-done = bf16[16,2,256]{2,1,0:T(2,128)(2,1)S(1)} async-done(((bf16[16,2,256]{2,1,0:T(2,128)(2,1)}), bf16[16,2,256]{2,1,0:T(2,128)(2,1)S(1)}, u32[]{:S(2)}, u32[]{:S(2)}) %all-to-all-start) | async-done | bytes 16416 | tf_op jit(solution)/shard_map/all_to_all | solution.py:113
  57.0 4.3 reshape.368
  61.3 4.6 copy.85
  65.9 0.5 convolution_convert_fusion.3
  66.5 0.8 copy.86
  67.3 0.0 all-gather.2.cloned.1.call-start
  67.4 0.6 dynamic-slice
  68.0 100.0 %all-reduce.5.cloned.1.call-done = bf16[16,2,2880]{2,1,0:T(2,128)(2,1)} async-done(((bf16[16,2,2880]{2,1,0:T(2,128)(2,1)}), bf16[16,2,2880]{2,1,0:T(2,128)(2,1)}) %all-reduce.5.cloned.1.call-update) | async-done | bytes 184336
  168.0 1.4 multiply_reduce_fusion.1
  169.4 1.6 convolution_convert_fusion.2
  171.1 0.3 copy.101
  171.4 18.9 %all_to_all.28 = bf16[16,2,2,2880]{3,2,1,0:T(2,128)(2,1)} all-to-all(bf16[16,2,2,2880]{3,2,1,0:T(2,128)(2,1)S(1)} %bitcast.101), channel_id=1, replica_groups=mesh['dp'=16,'expert'=16] {'expert'}, dimensions={0} | all-to-all | bytes 737280 | tf_op jit(solution)/shard_map/all_to_all | solution.py:136
  190.3 0.2 all-reduce.7.cloned.1.call-start
  190.5 7.0 %fusion.36 = (bf16[1,2880,180]{1,0,2:T(2,128)(2,1)}, bf16[1,2880,180]{1,0,2:T(2,128)(2,1)}) fusion(bf16[2,2880,180]{1,0,2:T(2,128)(2,1)} %param.25), kind=kLoop, calls=%fused_computation.84 | loop fusion | bytes 4147200 | tf_op jit(solution)/shard_map/slice | solution.py:52
  197.5 4.3 fusion.37
  201.8 4.2 fusion.38
  206.0 47.4 %all-gather.2.cloned.1.call-done = bf16[256,2,2,2880]{3,2,1,0:T(2,128)(2,1)} async-done(((bf16[16,2,2,2880]{3,2,1,0:T(2,128)(2,1)}), bf16[256,2,2,2880]{3,2,1,0:T(2,128)(2,1)}) %all-gather.2.cloned.1.call-update) | async-done | bytes 5898256 | tf_op jit(solution)/shard_map/all_gather | solution.py:138
  253.4 8.2 %fusion.35 = (bf16[256,1,2,2880]{3,2,1,0:T(2,128)(2,1)}, bf16[256,1,2,2880]{3,2,1,0:T(2,128)(2,1)}) fusion(bf16[256,2,2,2880]{3,2,1,0:T(2,128)(2,1)} %all-gather.2.cloned.1.call-done), kind=kLoop, calls=%fused_computation.83 | loop fusion | bytes 11796480 | tf_op jit(solution)/shard_map/slice | solution.py:50
  261.6 7.2 %reshape_squeeze.6 = bf16[512,2880]{1,0:T(8,128)(2,1)} reshape(bf16[256,1,2,2880]{3,2,1,0:T(2,128)(2,1)} %get-tuple-element.7) | data formatting | bytes 5898240 | tf_op jit(solution)/shard_map/reshape;squeeze | solution.py:50
  268.7 7.1 %reshape_squeeze.7 = bf16[512,2880]{1,0:T(8,128)(2,1)} reshape(bf16[256,1,2,2880]{3,2,1,0:T(2,128)(2,1)} %get-tuple-element.8) | data formatting | bytes 5898240 | tf_op jit(solution)/shard_map/reshape;squeeze | solution.py:50
  275.9 3.8 fusion.12
  279.7 0.2 copy-done.8
  279.9 1.2 fusion.7
  281.1 0.1 copy.90
  281.3 0.1 reshape.332
  281.4 3.8 fusion.11
  285.3 0.2 copy-done.7
  285.5 1.2 fusion.8
  286.7 0.1 copy.95
  286.8 0.1 reshape.333
  287.0 2.8 fusion
  289.8 1.0 fusion.1
  290.8 3.0 pad_maximum_fusion
  293.8 15.6 %copy.98 = bf16[256,2,2,2880]{3,2,1,0:T(2,128)(2,1)} copy(bf16[256,2,2,2880]{0,3,2,1:T(8,128)(2,1)} %pad_maximum_fusion) | data formatting | bytes 11796480 | tf_op jit(solution)/shard_map/stack | solution.py:62
  309.5 0.1 reshape.336
  309.5 0.6 copy-done.15
  310.1 0.6 dynamic-slice.2
  310.7 0.1 reshape.348
  310.8 0.7 gather_fusion.1
  311.4 0.1 reshape.351
  312.2 0.2 fusion.20
  312.4 126.8 %all-reduce.7.cloned.1.call-done = bf16[256,2,2,2880]{3,2,1,0:T(2,128)(2,1)} async-done(((bf16[256,2,2,2880]{3,2,1,0:T(2,128)(2,1)}), bf16[256,2,2,2880]{3,2,1,0:T(2,128)(2,1)}) %all-reduce.7.cloned.1.call-update) | async-done | bytes 5898256
  439.2 2.0 constant_dynamic-slice_fusion
  441.1 7.1 %all-to-all-start.2 = ((bf16[16,2,2,2880]{3,2,1,0:T(2,128)(2,1)}), bf16[16,2,2,2880]{3,2,1,0:T(2,128)(2,1)S(1)}, u32[]{:S(2)}, u32[]{:S(2)}) async-start(bf16[16,2,2,2880]{3,2,1,0:T(2,128)(2,1)} %constant_dynamic-slice_fusion), calls=%async_computation.2 | async-start | bytes 753664 | tf_op jit(solution)/shard_map/all_to_all | solution.py:143
  448.3 0.1 broadcast_divide_fusion
  448.4 13.3 %all-to-all-done.2 = bf16[16,2,2,2880]{3,2,1,0:T(2,128)(2,1)S(1)} async-done(((bf16[16,2,2,2880]{3,2,1,0:T(2,128)(2,1)}), bf16[16,2,2,2880]{3,2,1,0:T(2,128)(2,1)S(1)}, u32[]{:S(2)}, u32[]{:S(2)}) %all-to-all-start.2) | async-done | bytes 368672 | tf_op jit(solution)/shard_map/all_to_all | solution.py:143
  461.6 0.3 reshape.339
  461.9 0.6 gather_fusion
  462.5 0.1 multiply_reduce_fusion
  462.7 1.9 fusion.17
  (49 shorter events, 0.3 us)
Async XLA Ops:
  6.5 59.4 %copy-start = (bf16[256,2880]{0,1:T(8,128)(2,1)S(1)}, bf16[256,2880]{0,1:T(8,128)(2,1)}, u32[]{:S(2)}) copy-start(bf16[256,2880]{0,1:T(8,128)(2,1)} %param.21) | copy-start | bytes 4423684
  6.5 3.0 copy-start.9
  6.5 3.0 copy-start.13
  15.1 34.3 %copy-start.12 = (s32[16,2,4]{0,2,1:T(4,128)S(1)}, s32[16,2,4]{0,2,1:T(4,128)}, u32[]{:S(2)}) copy-start(s32[16,2,4]{0,2,1:T(4,128)} %param.23) | copy-start | bytes 1540
  40.8 16.2 %all-to-all-start = ((bf16[16,2,256]{2,1,0:T(2,128)(2,1)}), bf16[16,2,256]{2,1,0:T(2,128)(2,1)S(1)}, u32[]{:S(2)}, u32[]{:S(2)}) async-start(bf16[16,2,256]{2,1,0:T(2,128)(2,1)} %reshape.367), calls=%async_computation | async-start | bytes 32768 | tf_op jit(solution)/shard_map/all_to_all | solution.py:113
  49.4 118.6 %all-reduce.5.cloned.1.call-start = ((), (), s32[]{:S(2)}) async-start(), calls=%async_computation.4 | async-start | bytes 376832
  61.3 6.1 %copy-start.16 = (u32[256]{0:T(256)S(1)}, u32[256]{0:T(256)}, u32[]{:S(2)}) copy-start(u32[256]{0:T(256)} %constant.88) | copy-start | bytes 3076
  61.3 106.7 %copy-start.10 = (bf16[1,2,2880]{2,1,0:T(2,128)(2,1)S(1)}, bf16[1,2,2880]{2,1,0:T(2,128)(2,1)}, u32[]{:S(2)}) copy-start(bf16[1,2,2880]{2,1,0:T(2,128)(2,1)} %param.14) | copy-start | bytes 34564
  61.3 108.1 %copy-start.11 = (f32[2880]{0:T(1024)S(1)}, f32[2880]{0:T(1024)}, u32[]{:S(2)}) copy-start(f32[2880]{0:T(1024)} %param.22) | copy-start | bytes 34564
  67.3 186.1 %all-gather.2.cloned.1.call-start = ((), (), s32[]{:S(2)}) async-start(), calls=%async_computation.3 | async-start | bytes 6406144 | tf_op jit(solution)/shard_map/all_gather | solution.py:138
  190.3 248.9 %all-reduce.7.cloned.1.call-start = ((), (), s32[]{:S(2)}) async-start(), calls=%async_computation.5 | async-start | bytes 12058624
  190.5 7.0 %copy-start.2 = (bf16[2,2880,180]{1,0,2:T(2,128)(2,1)S(1)}, bf16[2,2880,180]{1,0,2:T(2,128)(2,1)}, u32[]{:S(2)}) copy-start(bf16[2,2880,180]{1,0,2:T(2,128)(2,1)} %param.26) | copy-start | bytes 6220804
  197.5 4.3 copy-start.3
  275.9 3.8 copy-start.6
  275.9 4.0 copy-start.8
  281.4 3.9 copy-start.5
  281.4 4.0 copy-start.7
  286.9 2.8 copy-start.4
  309.4 0.7 copy-start.15
  309.4 2.8 copy-start.14
  310.8 153.8 %copy-start.1 = (bf16[256,2880]{0,1:T(8,128)(2,1)S(1)}, bf16[256,2880]{0,1:T(8,128)(2,1)}, u32[]{:S(2)}) copy-start(bf16[256,2880]{0,1:T(8,128)(2,1)} %param.21) | copy-start | bytes 4423684
  441.1 20.5 %all-to-all-start.2 = ((bf16[16,2,2,2880]{3,2,1,0:T(2,128)(2,1)}), bf16[16,2,2,2880]{3,2,1,0:T(2,128)(2,1)S(1)}, u32[]{:S(2)}, u32[]{:S(2)}) async-start(bf16[16,2,2,2880]{3,2,1,0:T(2,128)(2,1)} %constant_dynamic-slice_fusion), calls=%async_computation.2 | async-start | bytes 753664 | tf_op jit(solution)/shard_map/all_to_all | solution.py:143
Sparse Core Ops, SparseCore 0:
  67.4 100.5 all-reduce.4
  190.4 62.9 all-gather.1
  309.6 129.5 all-reduce.6
where the time goes:
time: 475 us; the launch traced here: 471 us
  waiting for transfers between devices  295 us (62%)
  local copies, waits for them, and re-layouts  78.4 us (17%)
  other arithmetic  31.5 us (7%)
  blocking collectives  18.9 us (4%)
  matrix products  16.7 us (4%)
  starting transfers between devices  16 us (3%)
  between operations  14.9 us (3%)
    unnamed x5, waiting for transfers between devices  227 us
    all_gather x1, waiting for transfers between devices, on_device(): lax.all_gather(arrived, 'dp', axis=0, tiled=True)  47.4 us
    unnamed x1, other arithmetic  23.5 us
    all_to_all x1, blocking collectives, on_device(): lax.all_to_all(dispatch, 'expert', split_axis=0, concat_axis=0, tiled=True)  18.9 us
    another operation x1, local copies, waits for them, and re-layouts, expert_partials(): return jnp.stack(results, axis=1)  15.6 us
    another operation x2, local copies, waits for them, and re-layouts, expert_partials(): row_block = slot_block[:, local_expert].reshape(-1, slot_block.shape[3])  14.3 us
    all_to_all x1, waiting for transfers between devices, on_device(): lax.all_to_all(summed.astype(jnp.bfloat16), 'expert', split_axis=0, conca...  13.3 us
    unnamed x40, local copies, waits for them, and re-layouts  11.2 us
  transfers between devices with their start and end apart: 5, of which 5 were waited for; matrix products, arithmetic and copies ran while one was open for 4% of the time, Pallas kernels for 0%

commit v1 on v0

v1 whole, which is shorter than its diff:
```python
import functools

import jax
import jax.numpy as jnp
from jax import lax
from jax.experimental import pallas as pl
from jax.experimental.pallas import tpu as pltpu
from jax.sharding import Mesh
from jax.sharding import PartitionSpec as P

HQ = 64
KVH = 8
HD = 64
SWAP = [(0, 1), (1, 0)]
F32 = jnp.float32
BF16 = jnp.bfloat16


def params(mib=48):
    return pltpu.CompilerParams(vmem_limit_bytes=mib * 1024 * 1024)


def vmem():
    return pl.BlockSpec(memory_space=pltpu.VMEM)


def smem():
    return pl.BlockSpec(memory_space=pltpu.SMEM)


def attend_kernel(len_ref, q_ref, nk_ref, nv_ref, k_ref, v_ref, out_ref, rows_ref, flat_ref):
    steps = q_ref.shape[1]
    width = KVH * HD
    rows = HQ * steps
    per_group = rows // KVH
    q = q_ref[0].astype(F32) * 0.125
    for h in range(HQ):
        rows_ref[h * steps : (h + 1) * steps, :] = q[:, h * HD : (h + 1) * HD]
    q_rows = rows_ref[...]
    q_pair = jnp.concatenate([q_rows, q_rows], axis=1)
    q_wide = jnp.concatenate([q_pair] * (KVH // 2), axis=1)
    row_id = lax.broadcasted_iota(jnp.int32, (rows, width), 0)
    col_id = lax.broadcasted_iota(jnp.int32, (rows, width), 1)
    in_group = row_id // per_group == col_id // HD
    q_wide = jnp.where(in_group, q_wide, 0.0)
    q_bf = q_wide.astype(BF16)
    scores = lax.dot_general(
        q_bf, k_ref[0], (((1,), (1,)), ((), ())), preferred_element_type=F32
    )
    slot = lax.broadcasted_iota(jnp.int32, scores.shape, 1)
    weights = jnp.where(slot < len_ref[0], jnp.exp(scores), 0.0)
    total = jnp.sum(weights, axis=1, keepdims=True)
    nk = nk_ref[0].astype(F32)
    nv = nv_ref[0].astype(F32)
    step_id = lax.broadcasted_iota(jnp.int32, (rows, 1), 0) % steps
    fresh = []
    for s in range(steps):
        score = jnp.sum(q_wide * nk[s : s + 1, :], axis=1, keepdims=True)
        weight = jnp.where(step_id >= s, jnp.exp(score), 0.0)
        total = total + weight
        fresh.append(weight)
    probs = (weights / total).astype(BF16)
    mixed = jnp.dot(probs, v_ref[0], preferred_element_type=F32)
    for s in range(steps):
        mixed = mixed + (fresh[s] / total).astype(BF16).astype(F32) * nv[s : s + 1, :]
    mixed = jnp.where(in_group, mixed, 0.0)
    folded = mixed[:, :128]
    for i in range(1, width // 128):
        folded = folded + mixed[:, i * 128 : (i + 1) * 128]
    rows_ref[...] = folded[:, :HD] + folded[:, HD:]
    for h in range(HQ):
        flat_ref[:, h * HD : (h + 1) * HD] = rows_ref[h * steps : (h + 1) * steps, :]
    blocks = out_ref.shape[0]
    wide = HQ * HD // blocks
    for b in range(blocks):
        out_ref[b] = flat_ref[:, b * wide : (b + 1) * wide].astype(BF16)


def attend(length, q, nk, nv, k, v, blocks):
    steps = q.shape[1]
    return pl.pallas_call(
        attend_kernel,
        in_specs=[smem()] + [vmem()] * 5,
        out_specs=vmem(),
        out_shape=jax.ShapeDtypeStruct((blocks, steps, HQ * HD // blocks), BF16),
        scratch_shapes=[pltpu.VMEM((HQ * steps, HD), F32), pltpu.VMEM((steps, HQ * HD), F32)],
        compiler_params=params(),
        name="attend",
    )(length, q, nk, nv, k, v)


def norm_kernel(part_ref, hid_ref, gain_ref, route_ref, res_ref, out_ref):
    width = hid_ref.shape[2]
    res = hid_ref[0].astype(F32)
    for i in range(part_ref.shape[0]):
        res = res + part_ref[i].astype(F32)
    res_ref[...] = res
    scale = lax.rsqrt(jnp.sum(res * res, axis=1, keepdims=True) / width + 1e-05)
    normed = (res * scale * gain_ref[...]).astype(BF16).astype(F32)
    full = jnp.concatenate([normed, route_ref[...]], axis=1).astype(BF16)
    for i in range(out_ref.shape[0]):
        out_ref[i] = full


def norm(parts, hidden, gain, route):
    steps, width = hidden.shape[1:]
    copies = parts.shape[0]
    wide = width + route.shape[1]
    return pl.pallas_call(
        norm_kernel,
        in_specs=[vmem()] * 4,
        out_specs=[vmem(), vmem()],
        out_shape=[
            jax.ShapeDtypeStruct((steps, width), F32),
            jax.ShapeDtypeStruct((copies, steps, wide), BF16),
        ],
        compiler_params=params(),
        name="norm",
    )(parts, hidden, gain, route)


def experts_kernel(first_ref, x_ref, g0, g1, u0, u1, d0, d1, out_ref, acc_ref):
    step = pl.program_id(0)
    width = g0.shape[1]
    half = pl.num_programs(0) // 2

    def one(g_ref, u_ref, d_ref, label):
        x = x_ref[:, :width]
        gate = jnp.dot(x, g_ref[0], preferred_element_type=F32)
        up = jnp.dot(x, u_ref[0], preferred_element_type=F32)
        act = gate * jax.nn.sigmoid(1.702 * gate) * (up + 1.0)
        route = x_ref[:, width : width + 8].astype(F32)
        ids = route[:, 0:4]
        expo = jnp.exp(route[:, 4:8])
        chosen = jnp.where(ids == label.astype(F32), expo, 0.0)
        share = jnp.sum(chosen, axis=1, keepdims=True) / jnp.sum(expo, axis=1, keepdims=True)
        mixed = (act * share).astype(BF16)
        return jnp.dot(mixed, d_ref[0], preferred_element_type=F32)

    @pl.when(step == 0)
    def _():
        acc_ref[...] = one(g0, u0, d0, first_ref[0])

    @pl.when((step > 0) & (step < half))
    def _():
        acc_ref[...] += one(g0, u0, d0, first_ref[0] + step)

    @pl.when(step >= half)
    def _():
        acc_ref[...] += one(g1, u1, d1, first_ref[1] + step - half)

    @pl.when(step == pl.num_programs(0) - 1)
    def _():
        out_ref[...] = acc_ref[...].astype(BF16)


def experts(first, x, own, other):
    rows = x.shape[0]
    per, width, hidden = own[0].shape

    def early(i, *_):
        return (jnp.minimum(i, per - 1), 0, 0)

    def late(i, *_):
        return (jnp.maximum(i - per, 0), 0, 0)

    def spec(shape, index):
        return pl.BlockSpec((1,) + shape[1:], index)

    grid_spec = pltpu.PrefetchScalarGridSpec(
        num_scalar_prefetch=1,
        grid=(2 * per,),
        in_specs=[
            pl.BlockSpec(x.shape, lambda i, *_: (0, 0)),
            spec(own[0].shape, early),
            spec(own[0].shape, late),
            spec(own[1].shape, early),
            spec(own[1].shape, late),
            spec(own[2].shape, early),
            spec(own[2].shape, late),
        ],
        out_specs=pl.BlockSpec((rows, width), lambda i, *_: (0, 0)),
        scratch_shapes=[pltpu.VMEM((rows, width), F32)],
    )
    return pl.pallas_call(
        experts_kernel,
        grid_spec=grid_spec,
        out_shape=jax.ShapeDtypeStruct((rows, width), BF16),
        compiler_params=params(),
        name="experts",
    )(first, x, own[0], other[0], own[1], other[1], own[2], other[2])


def exchange(value, axis):
    return lax.all_to_all(value, axis, split_axis=0, concat_axis=0, tiled=True)


def on_device(
    hidden_in,
    queries,
    new_keys,
    new_values,
    key_cache,
    value_cache,
    prompt_lengths,
    out_weight,
    norm_gain,
    expert_ids,
    top_logits,
    gate_weight,
    up_weight,
    down_weight,
):
    rows, steps, width = hidden_in.shape
    nz = lax.axis_size("z")
    ndp = lax.axis_size(("x", "y"))
    z = lax.axis_index("z")
    c = lax.axis_index("c")
    d = lax.axis_index(("x", "y"))
    other_out = lax.ppermute(out_weight, "c", SWAP)
    other = [lax.ppermute(w, "c", SWAP) for w in (gate_weight, up_weight, down_weight)]
    own = [gate_weight, up_weight, down_weight]
    attended = attend(
        prompt_lengths, queries, new_keys, new_values, key_cache, value_cache, nz
    )
    feats = out_weight.shape[0]
    by_heads = exchange(attended, "z").reshape(nz * steps, 2 * feats)
    mine = lax.dynamic_slice_in_dim(by_heads, c * feats, feats, 1)
    theirs = lax.dynamic_slice_in_dim(by_heads, (1 - c) * feats, feats, 1)
    parts = jnp.dot(mine, out_weight, preferred_element_type=F32) + jnp.dot(
        theirs, other_out, preferred_element_type=F32
    )
    parts = exchange(parts.astype(BF16).reshape(nz, steps, width), "z")
    ids = lax.dynamic_index_in_dim(expert_ids, d, 0, False).astype(F32)
    logits = lax.dynamic_index_in_dim(top_logits, d, 0, False).astype(F32)
    route = jnp.pad(jnp.concatenate([ids, logits], axis=1), ((0, 0), (0, 56)))
    residual, sent = norm(parts, hidden_in, norm_gain[None], route)
    column = exchange(sent, "z").reshape(nz * steps, -1)
    copies = jnp.broadcast_to(column[None], (ndp,) + column.shape)
    tokens = exchange(copies, ("x", "y")).reshape(ndp * nz * steps, -1)
    per = gate_weight.shape[0]
    first = jnp.stack([(2 * z + c) * per, (2 * z + 1 - c) * per]).astype(jnp.int32)
    made = experts(first, tokens, own, other)
    back = exchange(made.reshape(ndp, nz * steps, width), ("x", "y"))
    column_sum = jnp.sum(back.astype(F32), axis=0).astype(BF16)
    final = exchange(column_sum.reshape(nz, steps, width), "z")
    out = residual + jnp.sum(final.astype(F32), axis=0)
    return out.astype(BF16)[None]


def solution(mesh):
    shape = dict(mesh.shape)
    side = int(round(shape["dp"] ** 0.5))
    fine = Mesh(
        mesh.devices.reshape(side, shape["dp"] // side, shape["expert"] // 2, 2),
        ("x", "y", "z", "c"),
    )
    row = ("z", "c", "x", "y")
    group = ("z", "c")
    dp = ("x", "y")
    placed = (
        P(row, None, None),
        P(row, None, None),
        P(row, None, None),
        P(row, None, None),
        P(row, None, None),
        P(row, None, None),
        P(row),
        P(group, None),
        P(),
        P(group, None, None),
        P(group, None, None),
        P(group, None, dp),
        P(group, None, dp),
        P(group, dp, None),
    )
    return jax.shard_map(
        on_device,
        mesh=fine,
        in_specs=placed,
        out_specs=P(row, None, None),
        check_vma=False,
    )
```

time: 475 us -> 137 us (0.29)
  waiting for transfers between devices: 295 us -> 15.4 us
  local copies, waits for them, and re-layouts: 78.4 us -> 37.2 us
  other arithmetic: 31.5 us -> 1.21 us
  blocking collectives: 18.9 us -> 46.1 us
  matrix products: 16.7 us -> 2.41 us
  between operations: 14.9 us -> 0.77 us
  Pallas kernels: 0 us -> 12.5 us
    unnamed x5 -> x0, waiting for transfers between devices: 227 us -> none
    all_gather x1 -> x0, waiting for transfers between devices: 47.4 us -> none  [on_device(): lax.all_gather(arrived, 'dp', axis=0, tiled=True)]
    another operation x6 -> x0, local copies, waits for them, and re-layouts: 31 us -> none  [the longest x1 15.6 us: expert_partials(): return jnp.stack(results, axis=1)]
    all_to_all x1 -> x3, blocking collectives: 18.9 us -> 46.1 us  [exchange(): return lax.all_to_all(value, axis, split_axis=0, concat_axis=0, tiled=True)]
    slice x4 -> x0, local copies, waits for them, and re-layouts: 23.7 us -> none  [the longest x1 8.2 us: expert_partials(): row_block = slot_block[:, local_expert].reshape(-1, slot_block.shape[3])]
    unnamed x1 -> x0, other arithmetic: 23.5 us -> none
    ppermute x0 -> x3, local copies, waits for them, and re-layouts: none -> 16.2 us  [on_device(): lax.ppermute(w, 'c', SWAP)]
    dot_general x10 -> x2, matrix products: 16.7 us -> 2.41 us  [the longest x1 1.88 us: on_device(): jnp.dot(mine, out_weight, preferred_element_type=F32)]
  transfers between devices with their start and end apart: 5 -> 7, of which waited for: 5 -> 2; matrix products, arithmetic and copies ran while one was open for 4% -> 26% of each run, Pallas kernels for 0% -> 1%
where the time goes in v1:
time: 137 us; the launch traced here: 136 us
  blocking collectives  46.1 us (34%)
  local copies, waits for them, and re-layouts  37.2 us (27%)
  starting transfers between devices  20.1 us (15%)
  waiting for transfers between devices  15.4 us (11%)
  Pallas kernels  12.5 us (9%)
  matrix products  2.41 us (2%)
    all_to_all x3, blocking collectives, exchange(): return lax.all_to_all(value, axis, split_axis=0, concat_axis=0, tiled=True)  46.1 us
    all_to_all x3, starting transfers between devices, exchange(): return lax.all_to_all(value, axis, split_axis=0, concat_axis=0, tiled=True)  19.4 us
    unnamed x21, local copies, waits for them, and re-layouts  18.9 us
    ppermute x3, local copies, waits for them, and re-layouts, on_device(): lax.ppermute(w, 'c', SWAP)  16.2 us
    all_to_all x3, waiting for transfers between devices, exchange(): return lax.all_to_all(value, axis, split_axis=0, concat_axis=0, tiled=True)  15.4 us
    pallas_call x1, Pallas kernels, experts(): pl.pallas_call(experts_kernel, grid_spec=grid_spec, out_shape=jax.ShapeDt...  10.9 us
  transfers between devices with their start and end apart: 7, of which 2 were waited for; matrix products, arithmetic and copies ran while one was open for 26% of the time, Pallas kernels for 1%

profile of v1, /device:TPU:8, one launch (start us, length us, event | category | flops | bytes accessed | tf_op | source)
XLA Modules:
  0.0 135.6 jit_solution(6908311628486883965)
XLA Ops:
  0.0 0.0 collective-permute-start
  0.7 0.0 copy-start
  0.7 1.0 copy-done
  1.7 0.0 copy-start.1
  1.7 1.0 copy-done.1
  2.7 0.0 copy-start.2
  2.7 0.7 copy-done.2
  3.5 0.0 copy-start.4
  3.5 0.7 copy-done.4
  4.1 0.0 copy-start.5
  4.1 0.7 copy-done.5
  4.8 1.5 %attend.1 = bf16[8,2,512]{2,1,0:T(2,128)(2,1)} custom-call(s32[1]{0:T(128)S(6)} %copy.61.len_ref, bf16[1,2,4096]{2,1,0:T(2,128)(2,1)S(1)} %copy-done.2, bf16[1,2,512]{2,1,0:T(2,128)(2,1)S(1)} %copy-done.4, bf16[1,2,512]{2,1,0:T(2,128)(2,1)S(1)} %copy-done.5, bf16[1,512,512]{2,1,0:T(8,128)(2,1)S(1)} %copy-done, bf16[1,512,512]{2,1,0:T(8,128)(2,1)S(1)} %copy-done.1), custom_call_target="tpu_custom_call" | custom-call | tf_op jit(solution)/shard_map/attend/pallas_call | solution.py:81
  6.3 0.0 copy-start.6
  6.3 0.0 copy-start.7
  6.3 0.0 copy-start.8
  6.3 0.0 copy-start.3
  6.3 8.6 %all-to-all-start = ((bf16[8,2,512]{2,1,0:T(2,128)(2,1)}), bf16[8,2,512]{2,1,0:T(2,128)(2,1)S(1)}, u32[]{:S(2)}, u32[]{:S(2)}) async-start(bf16[8,2,512]{2,1,0:T(2,128)(2,1)} %attend.1), calls=%async_computation | async-start | bytes 32768 | tf_op jit(solution)/shard_map/all_to_all | solution.py:195
  14.9 0.2 collective-permute-start.1
  15.1 0.3 collective-permute-start.2
  15.4 0.2 collective-permute-start.3
  15.6 7.1 %all-to-all-done = bf16[8,2,512]{2,1,0:T(2,128)(2,1)S(1)} async-done(((bf16[8,2,512]{2,1,0:T(2,128)(2,1)}), bf16[8,2,512]{2,1,0:T(2,128)(2,1)S(1)}, u32[]{:S(2)}, u32[]{:S(2)}) %all-to-all-start) | async-done | bytes 16416 | tf_op jit(solution)/shard_map/all_to_all | solution.py:195
  22.7 1.9 %fusion.3 = f32[16,2880]{1,0:T(8,128)S(1)} fusion(bf16[256,2880]{0,1:T(8,128)(2,1)} %param.21, bf16[16,512]{1,0:T(8,128)(2,1)S(1)} %reshape.19, s32[]{:T(128)S(6)} %select_n.12), kind=kOutput, calls=%fused_computation.6 | convolution fusion | flops 23592960 | bytes 1667076 | tf_op jit(solution)/shard_map/dot_general | solution.py:230
  24.6 0.0 collective-permute-done
  24.6 0.5 fusion
  25.2 0.7 reshape.20
  25.9 3.4 %all-to-all-start.1 = ((bf16[8,2,2880]{2,1,0:T(2,128)(2,1)}), bf16[8,2,2880]{2,1,0:T(2,128)(2,1)S(1)}, u32[]{:S(2)}, u32[]{:S(2)}) async-start(bf16[8,2,2880]{2,1,0:T(2,128)(2,1)} %reshape.20), calls=%async_computation.1 | async-start | bytes 188416 | tf_op jit(solution)/shard_map/all_to_all | solution.py:195
  29.2 0.0 copy-done.6
  29.3 0.0 copy-done.7
  29.3 0.0 copy-done.8
  29.3 0.2 convert_reduce_fusion.1
  29.4 0.1 select_maximum_fusion.route_ref
  29.5 8.3 %all-to-all-done.1.part_ref = bf16[8,2,2880]{2,1,0:T(2,128)(2,1)S(1)} async-done(((bf16[8,2,2880]{2,1,0:T(2,128)(2,1)}), bf16[8,2,2880]{2,1,0:T(2,128)(2,1)S(1)}, u32[]{:S(2)}, u32[]{:S(2)}) %all-to-all-start.1) | async-done | bytes 92192 | tf_op jit(solution)/shard_map/all_to_all | solution.py:195
  37.8 0.0 copy-done.3
  37.8 0.1 norm.1
  38.0 11.1 %all_to_all.30 = bf16[8,2,2944]{2,1,0:T(2,128)(2,1)S(1)} all-to-all(bf16[8,2,2944]{2,1,0:T(2,128)(2,1)S(1)} %get-tuple-element.8), channel_id=1, replica_groups=mesh['x'=4,'y'=4,'z'=8,'c'=2] {'z'}, dimensions={0} | all-to-all | bytes 188416 | tf_op jit(solution)/shard_map/all_to_all | solution.py:195
  49.1 1.3 broadcast_in_dim.15
  50.3 7.4 %all-to-all-start.3 = ((bf16[16,16,2944]{2,1,0:T(8,128)(2,1)}), bf16[16,16,2944]{2,1,0:T(8,128)(2,1)}, u32[]{:S(2)}, u32[]{:S(2)}) async-start(bf16[16,16,2944]{2,1,0:T(8,128)(2,1)} %broadcast_in_dim.15), calls=%async_computation.3 | async-start | bytes 3014656 | tf_op jit(solution)/shard_map/all_to_all | solution.py:195
  57.7 1.8 %copy.57.d0 = bf16[2,180,2880]{2,1,0:T(8,128)(2,1)S(1)} copy(bf16[2,180,2880]{2,0,1:T(2,128)(2,1)} %param.27) | data formatting | bytes 4147200 | tf_op args[13]
  59.5 6.5 %copy.53.g0 = bf16[2,2880,180]{2,1,0:T(8,128)(2,1)} copy(bf16[2,2880,180]{1,0,2:T(2,128)(2,1)} %param.25) | data formatting | bytes 4147200 | tf_op args[11]
  66.0 6.5 %copy.55.u0 = bf16[2,2880,180]{2,1,0:T(8,128)(2,1)} copy(bf16[2,2880,180]{1,0,2:T(2,128)(2,1)} %param.26) | data formatting | bytes 4147200 | tf_op args[12]
  72.5 0.1 pad_add_fusion.first_ref
  72.6 0.0 collective-permute-done.1
  72.6 6.5 %copy.54.g1 = bf16[2,2880,180]{2,1,0:T(8,128)(2,1)} copy(bf16[2,2880,180]{1,0,2:T(2,128)(2,1)} %collective-permute-done.1) | data formatting | bytes 4147200 | tf_op jit(solution)/shard_map/ppermute | solution.py:221
  79.0 0.0 collective-permute-done.2
  79.0 6.4 %copy.56.u1 = bf16[2,2880,180]{2,1,0:T(8,128)(2,1)} copy(bf16[2,2880,180]{1,0,2:T(2,128)(2,1)} %collective-permute-done.2) | data formatting | bytes 4147200 | tf_op jit(solution)/shard_map/ppermute | solution.py:221
  85.5 0.0 collective-permute-done.3
  85.5 3.2 %copy.58.d1 = bf16[2,180,2880]{2,1,0:T(8,128)(2,1)} copy(bf16[2,180,2880]{2,0,1:T(2,128)(2,1)} %collective-permute-done.3) | data formatting | bytes 4147200 | tf_op jit(solution)/shard_map/ppermute | solution.py:221
  88.7 0.0 all-to-all-done.3
  88.7 10.9 %experts.1 = bf16[256,2880]{1,0:T(8,128)(2,1)S(1)} custom-call(s32[2]{0:T(128)S(1)} %pad_add_fusion.first_ref, bf16[256,2944]{1,0:T(8,128)(2,1)} %bitcast.2.x_ref, bf16[2,2880,180]{2,1,0:T(8,128)(2,1)} %copy.53.g0, bf16[2,2880,180]{2,1,0:T(8,128)(2,1)} %copy.54.g1, bf16[2,2880,180]{2,1,0:T(8,128)(2,1)} %copy.55.u0, bf16[2,2880,180]{2,1,0:T(8,128)(2,1)} %copy.56.u1, ...), custom_call_target="tpu_custom_call" | custom-call | tf_op jit(solution)/shard_map/experts/pallas_call | solution.py:185
  99.6 24.0 %all_to_all.31 = bf16[16,16,2880]{2,1,0:T(8,128)(2,1)S(1)} all-to-all(bf16[16,16,2880]{2,1,0:T(8,128)(2,1)S(1)} %bitcast.8), channel_id=1, replica_groups=mesh['x'=4,'y'=4,'z'=8,'c'=2] {'x','y'}, dimensions={0} | all-to-all | bytes 2949120 | tf_op jit(solution)/shard_map/all_to_all | solution.py:195
  123.6 0.2 reduce_sum.21
  123.9 11.1 %all_to_all.32 = bf16[8,2,2880]{2,1,0:T(2,128)(2,1)S(1)} all-to-all(bf16[8,2,2880]{2,1,0:T(2,128)(2,1)S(1)} %reshape.23), channel_id=1, replica_groups=mesh['x'=4,'y'=4,'z'=8,'c'=2] {'z'}, dimensions={0} | all-to-all | bytes 184320 | tf_op jit(solution)/shard_map/all_to_all | solution.py:195
  134.9 0.1 convert_reduce_fusion
  135.0 0.6 fusion.1
  (4 shorter events, 0.1 us)
Async XLA Ops:
  0.0 24.6 %collective-permute-start = (bf16[256,2880]{0,1:T(8,128)(2,1)}, bf16[256,2880]{0,1:T(8,128)(2,1)S(1)}, u32[]{:S(2)}, u32[]{:S(2)}) collective-permute-start(bf16[256,2880]{0,1:T(8,128)(2,1)} %param.21), channel_id=1, source_target_pairs={{0,1},{1,0},{2,3},{3,2},{4,5},{5,4},{6,7},{7,6},{8,9},{9,8},{10,11... | collective-permute-start | bytes 4423688 | tf_op jit(solution)/shard_map/ppermute | solution.py:220
  0.7 1.0 copy-start
  1.7 1.0 copy-start.1
  2.7 0.7 copy-start.2
  3.5 0.7 copy-start.4
  4.1 0.7 copy-start.5
  6.3 23.0 %copy-start.6 = (f32[2880]{0:T(1024)S(1)}, f32[2880]{0:T(1024)}, u32[]{:S(2)}) copy-start(f32[2880]{0:T(1024)} %param.22) | copy-start | bytes 34564
  6.3 23.0 %copy-start.7 = (s32[16,2,4]{0,2,1:T(4,128)S(1)}, s32[16,2,4]{0,2,1:T(4,128)}, u32[]{:S(2)}) copy-start(s32[16,2,4]{0,2,1:T(4,128)} %param.23) | copy-start | bytes 1540
  6.3 23.0 %copy-start.8 = (bf16[16,2,4]{0,2,1:T(4,128)(2,1)S(1)}, bf16[16,2,4]{0,2,1:T(4,128)(2,1)}, u32[]{:S(2)}) copy-start(bf16[16,2,4]{0,2,1:T(4,128)(2,1)} %param.24) | copy-start | bytes 772
  6.3 31.5 %copy-start.3 = (bf16[1,2,2880]{2,1,0:T(2,128)(2,1)S(1)}, bf16[1,2,2880]{2,1,0:T(2,128)(2,1)}, u32[]{:S(2)}) copy-start(bf16[1,2,2880]{2,1,0:T(2,128)(2,1)} %hid_ref.1) | copy-start | bytes 34564
  6.3 16.4 %all-to-all-start = ((bf16[8,2,512]{2,1,0:T(2,128)(2,1)}), bf16[8,2,512]{2,1,0:T(2,128)(2,1)S(1)}, u32[]{:S(2)}, u32[]{:S(2)}) async-start(bf16[8,2,512]{2,1,0:T(2,128)(2,1)} %attend.1), calls=%async_computation | async-start | bytes 32768 | tf_op jit(solution)/shard_map/all_to_all | solution.py:195
  14.9 57.7 %collective-permute-start.1 = (bf16[2,2880,180]{1,0,2:T(2,128)(2,1)}, bf16[2,2880,180]{1,0,2:T(2,128)(2,1)}, u32[]{:S(2)}, u32[]{:S(2)}) collective-permute-start(bf16[2,2880,180]{1,0,2:T(2,128)(2,1)} %param.25), channel_id=1, source_target_pairs={{0,1},{1,0},{2,3},{3,2},{4,5},{5,4},{6,7},{7,6},{8,9},{9,8},{10,11... | collective-permute-start | bytes 6220808 | tf_op jit(solution)/shard_map/ppermute | solution.py:221
  15.1 63.9 %collective-permute-start.2 = (bf16[2,2880,180]{1,0,2:T(2,128)(2,1)}, bf16[2,2880,180]{1,0,2:T(2,128)(2,1)}, u32[]{:S(2)}, u32[]{:S(2)}) collective-permute-start(bf16[2,2880,180]{1,0,2:T(2,128)(2,1)} %param.26), channel_id=1, source_target_pairs={{0,1},{1,0},{2,3},{3,2},{4,5},{5,4},{6,7},{7,6},{8,9},{9,8},{10,11... | collective-permute-start | bytes 6220808 | tf_op jit(solution)/shard_map/ppermute | solution.py:221
  15.4 70.1 %collective-permute-start.3 = (bf16[2,180,2880]{2,0,1:T(2,128)(2,1)}, bf16[2,180,2880]{2,0,1:T(2,128)(2,1)}, u32[]{:S(2)}, u32[]{:S(2)}) collective-permute-start(bf16[2,180,2880]{2,0,1:T(2,128)(2,1)} %param.27), channel_id=1, source_target_pairs={{0,1},{1,0},{2,3},{3,2},{4,5},{5,4},{6,7},{7,6},{8,9},{9,8},{10,11... | collective-permute-start | bytes 6220808 | tf_op jit(solution)/shard_map/ppermute | solution.py:221
  25.9 12.0 %all-to-all-start.1 = ((bf16[8,2,2880]{2,1,0:T(2,128)(2,1)}), bf16[8,2,2880]{2,1,0:T(2,128)(2,1)S(1)}, u32[]{:S(2)}, u32[]{:S(2)}) async-start(bf16[8,2,2880]{2,1,0:T(2,128)(2,1)} %reshape.20), calls=%async_computation.1 | async-start | bytes 188416 | tf_op jit(solution)/shard_map/all_to_all | solution.py:195
  50.3 38.4 %all-to-all-start.3 = ((bf16[16,16,2944]{2,1,0:T(8,128)(2,1)}), bf16[16,16,2944]{2,1,0:T(8,128)(2,1)}, u32[]{:S(2)}, u32[]{:S(2)}) async-start(bf16[16,16,2944]{2,1,0:T(8,128)(2,1)} %broadcast_in_dim.15), calls=%async_computation.3 | async-start | bytes 3014656 | tf_op jit(solution)/shard_map/all_to_all | solution.py:195

commit v2 on v1

v2 whole, which is shorter than its diff:
```python
import jax
import jax.numpy as jnp
from jax import lax
from jax.experimental import pallas as pl
from jax.experimental.pallas import tpu as pltpu
from jax.experimental.layout import Layout, with_layout_constraint
from jax.sharding import Mesh
from jax.sharding import PartitionSpec as P

HQ = 64
KVH = 8
HD = 64
SWAP = [(0, 1), (1, 0)]
F32 = jnp.float32
BF16 = jnp.bfloat16


def params(mib):
    return pltpu.CompilerParams(vmem_limit_bytes=mib * 1024 * 1024)


def vmem():
    return pl.BlockSpec(memory_space=pltpu.VMEM)


def hbm():
    return pl.BlockSpec(memory_space=pltpu.HBM)


def stay(*values):
    return [pltpu.with_memory_space_constraint(v, pltpu.HBM) for v in values]


def smem():
    return pl.BlockSpec(memory_space=pltpu.SMEM)


def attend_kernel(
    len_ref, q_hbm, nk_hbm, nv_hbm, k_hbm, v_hbm, out_ref,
    q_ref, nk_ref, nv_ref, k_ref, v_ref, rows_ref, flat_ref, sems,
):
    pairs = (
        (k_hbm, k_ref), (q_hbm, q_ref), (nk_hbm, nk_ref), (nv_hbm, nv_ref), (v_hbm, v_ref),
    )
    copies = [pltpu.make_async_copy(a, b, sems.at[i]) for i, (a, b) in enumerate(pairs)]
    for copy in copies:
        copy.start()
    steps = q_ref.shape[1]
    width = KVH * HD
    rows = HQ * steps
    per_group = rows // KVH
    copies[1].wait()
    q = q_ref[0].astype(F32) * 0.125
    for h in range(HQ):
        rows_ref[h * steps : (h + 1) * steps, :] = q[:, h * HD : (h + 1) * HD]
    q_rows = rows_ref[...]
    q_pair = jnp.concatenate([q_rows, q_rows], axis=1)
    q_wide = jnp.concatenate([q_pair] * (KVH // 2), axis=1)
    row_id = lax.broadcasted_iota(jnp.int32, (rows, width), 0)
    col_id = lax.broadcasted_iota(jnp.int32, (rows, width), 1)
    in_group = row_id // per_group == col_id // HD
    q_wide = jnp.where(in_group, q_wide, 0.0)
    q_bf = q_wide.astype(BF16)
    copies[0].wait()
    scores = lax.dot_general(
        q_bf, k_ref[0], (((1,), (1,)), ((), ())), preferred_element_type=F32
    )
    slot = lax.broadcasted_iota(jnp.int32, scores.shape, 1)
    weights = jnp.where(slot < len_ref[0], jnp.exp(scores), 0.0)
    total = jnp.sum(weights, axis=1, keepdims=True)
    copies[2].wait()
    copies[3].wait()
    nk = nk_ref[0].astype(F32)
    nv = nv_ref[0].astype(F32)
    step_id = lax.broadcasted_iota(jnp.int32, (rows, 1), 0) % steps
    fresh = []
    for s in range(steps):
        score = jnp.sum(q_wide * nk[s : s + 1, :], axis=1, keepdims=True)
        weight = jnp.where(step_id >= s, jnp.exp(score), 0.0)
        total = total + weight
        fresh.append(weight)
    probs = (weights / total).astype(BF16)
    copies[4].wait()
    mixed = jnp.dot(probs, v_ref[0], preferred_element_type=F32)
    for s in range(steps):
        mixed = mixed + (fresh[s] / total).astype(BF16).astype(F32) * nv[s : s + 1, :]
    mixed = jnp.where(in_group, mixed, 0.0)
    folded = mixed[:, :128]
    for i in range(1, width // 128):
        folded = folded + mixed[:, i * 128 : (i + 1) * 128]
    rows_ref[...] = folded[:, :HD] + folded[:, HD:]
    for h in range(HQ):
        flat_ref[:, h * HD : (h + 1) * HD] = rows_ref[h * steps : (h + 1) * steps, :]
    blocks = out_ref.shape[0]
    wide = HQ * HD // blocks
    for b in range(blocks):
        out_ref[b] = flat_ref[:, b * wide : (b + 1) * wide].astype(BF16)


def attend(length, q, nk, nv, k, v, blocks):
    steps = q.shape[1]
    return pl.pallas_call(
        attend_kernel,
        in_specs=[smem()] + [hbm()] * 5,
        out_specs=vmem(),
        out_shape=jax.ShapeDtypeStruct((blocks, steps, HQ * HD // blocks), BF16),
        scratch_shapes=[pltpu.VMEM(a.shape, BF16) for a in (q, nk, nv, k, v)]
        + [
            pltpu.VMEM((HQ * steps, HD), F32),
            pltpu.VMEM((steps, HQ * HD), F32),
            pltpu.SemaphoreType.DMA((5,)),
        ],
        compiler_params=params(12),
        name="attend",
    )(length, *stay(q, nk, nv, k, v))


def project_kernel(
    core_ref, x_ref, own_hbm, other_hbm, out_ref, rows_ref, own_ref, other_ref, sems
):
    copies = [
        pltpu.make_async_copy(own_hbm, own_ref, sems.at[0]),
        pltpu.make_async_copy(other_hbm, other_ref, sems.at[1]),
    ]
    for copy in copies:
        copy.start()
    blocks, steps, _ = x_ref.shape
    for i in range(blocks):
        rows_ref[i * steps : (i + 1) * steps, :] = x_ref[i].astype(F32)
    x = rows_ref[...].astype(BF16)
    feats = own_ref.shape[1]
    low, high = x[:, :feats], x[:, feats:]
    first = core_ref[0] == 0
    mine = jnp.where(first, low, high)
    theirs = jnp.where(first, high, low)
    dims = (((1,), (1,)), ((), ()))
    copies[0].wait()
    part = lax.dot_general(mine, own_ref[...], dims, preferred_element_type=F32)
    copies[1].wait()
    part = part + lax.dot_general(theirs, other_ref[...], dims, preferred_element_type=F32)
    for i in range(blocks):
        out_ref[i] = part[i * steps : (i + 1) * steps, :].astype(BF16)


def project(core, x, own, other):
    blocks, steps, feats = x.shape
    return pl.pallas_call(
        project_kernel,
        in_specs=[smem(), vmem(), hbm(), hbm()],
        out_specs=vmem(),
        out_shape=jax.ShapeDtypeStruct((blocks, steps, own.shape[0]), BF16),
        scratch_shapes=[
            pltpu.VMEM((blocks * steps, feats), F32),
            pltpu.VMEM(own.shape, BF16),
            pltpu.VMEM(own.shape, BF16),
            pltpu.SemaphoreType.DMA((2,)),
        ],
        compiler_params=params(12),
        name="project",
    )(core, x, *stay(own, other))


def norm_kernel(part_ref, hid_ref, gain_ref, route_ref, res_ref, out_ref):
    width = hid_ref.shape[2]
    res = hid_ref[0].astype(F32)
    for i in range(part_ref.shape[0]):
        res = res + part_ref[i].astype(F32)
    res_ref[...] = res
    scale = lax.rsqrt(jnp.sum(res * res, axis=1, keepdims=True) / width + 1e-05)
    normed = (res * scale * gain_ref[...]).astype(BF16).astype(F32)
    full = jnp.concatenate([normed, route_ref[...]], axis=1).astype(BF16)
    for i in range(out_ref.shape[0]):
        out_ref[i] = full


def norm(parts, hidden, gain, route):
    steps, width = hidden.shape[1:]
    copies = parts.shape[0]
    wide = width + route.shape[1]
    return pl.pallas_call(
        norm_kernel,
        in_specs=[vmem()] * 4,
        out_specs=[vmem(), vmem()],
        out_shape=[
            jax.ShapeDtypeStruct((steps, width), F32),
            jax.ShapeDtypeStruct((copies, steps, wide), BF16),
        ],
        compiler_params=params(12),
        name="norm",
    )(parts, hidden, gain, route)


def spread_kernel(x_ref, out_hbm, rows_ref, full_ref, sems):
    blocks, steps, _ = x_ref.shape
    for i in range(blocks):
        rows_ref[i * steps : (i + 1) * steps, :] = x_ref[i].astype(F32)
    full_ref[...] = rows_ref[...].astype(BF16)
    copies = [
        pltpu.make_async_copy(full_ref, out_hbm.at[i], sems.at[i])
        for i in range(out_hbm.shape[0])
    ]
    for copy in copies:
        copy.start()
    for copy in copies:
        copy.wait()


def spread(x, copies):
    blocks, steps, width = x.shape
    return pl.pallas_call(
        spread_kernel,
        in_specs=[vmem()],
        out_specs=hbm(),
        out_shape=jax.ShapeDtypeStruct((copies, blocks * steps, width), BF16),
        scratch_shapes=[
            pltpu.VMEM((blocks * steps, width), F32),
            pltpu.VMEM((blocks * steps, width), BF16),
            pltpu.SemaphoreType.DMA((copies,)),
        ],
        compiler_params=params(12),
        name="spread",
    )(x)


def experts_kernel(
    first_ref, x_ref, g0_hbm, u0_hbm, g1_hbm, u1_hbm, d0_hbm, d1_hbm, out_ref,
    g0, u0, g1, u1, d0, d1, sems,
):
    pairs = (
        (g0_hbm, g0), (u0_hbm, u0), (g1_hbm, g1), (u1_hbm, u1), (d0_hbm, d0), (d1_hbm, d1),
    )
    copies = [pltpu.make_async_copy(a, b, sems.at[i]) for i, (a, b) in enumerate(pairs)]
    for copy in copies:
        copy.start()
    per, _, width = g0.shape
    x = x_ref[:, :width]
    route = x_ref[:, width : width + 8].astype(F32)
    ids = route[:, 0:4]
    expo = jnp.exp(route[:, 4:8])
    total = jnp.sum(expo, axis=1, keepdims=True)
    dims = (((1,), (1,)), ((), ()))
    acts = []
    for side, (g_ref, u_ref) in enumerate(((g0, u0), (g1, u1))):
        copies[2 * side].wait()
        copies[1 + 2 * side].wait()
        for e in range(per):
            gate = lax.dot_general(x, g_ref[e], dims, preferred_element_type=F32)
            up = lax.dot_general(x, u_ref[e], dims, preferred_element_type=F32)
            act = gate * jax.nn.sigmoid(1.702 * gate) * (up + 1.0)
            label = (first_ref[side] + e).astype(F32)
            share = jnp.sum(jnp.where(ids == label, expo, 0.0), axis=1, keepdims=True) / total
            acts.append((act * share).astype(BF16))
    copies[4].wait()
    copies[5].wait()
    chunk = 768
    for start in range(0, width, chunk):
        stop = min(start + chunk, width)
        part = None
        for side, d_ref in enumerate((d0, d1)):
            for e in range(per):
                piece = jnp.dot(
                    acts[side * per + e], d_ref[e, :, start:stop], preferred_element_type=F32
                )
                part = piece if part is None else part + piece
        out_ref[:, start:stop] = part.astype(BF16)


def experts(first, x, own, other):
    width = own[0].shape[2]
    args = (own[0], own[1], other[0], other[1], own[2], other[2])
    return pl.pallas_call(
        experts_kernel,
        in_specs=[smem(), vmem()] + [hbm()] * 6,
        out_specs=vmem(),
        out_shape=jax.ShapeDtypeStruct((x.shape[0], width), BF16),
        scratch_shapes=[pltpu.VMEM(a.shape, BF16) for a in args]
        + [pltpu.SemaphoreType.DMA((len(args),))],
        compiler_params=params(32),
        name="experts",
    )(first, x, *stay(*args))


def row_major(value):
    return with_layout_constraint(value, Layout(major_to_minor=tuple(range(value.ndim))))


def exchange(value, axis):
    return lax.all_to_all(value, axis, split_axis=0, concat_axis=0, tiled=True)


def on_device(
    hidden_in,
    queries,
    new_keys,
    new_values,
    key_cache,
    value_cache,
    prompt_lengths,
    out_weight,
    norm_gain,
    expert_ids,
    top_logits,
    gate_weight,
    up_weight,
    down_weight,
):
    rows, steps, width = hidden_in.shape
    nz = lax.axis_size("z")
    ndp = lax.axis_size(("x", "y"))
    z = lax.axis_index("z")
    c = lax.axis_index("c")
    d = lax.axis_index(("x", "y"))
    out_rows = out_weight.T
    other_out = lax.ppermute(out_rows, "c", SWAP)
    weights = (gate_weight, up_weight, down_weight)
    swapped = [lax.ppermute(w, "c", SWAP) for w in weights]
    attended = attend(
        prompt_lengths, queries, new_keys, new_values, key_cache, value_cache, nz
    )
    attended, gate, up = lax.optimization_barrier((attended, gate_weight, up_weight))
    by_heads = exchange(attended, "z")
    gate, up = row_major(gate.swapaxes(1, 2)), row_major(up.swapaxes(1, 2))
    by_heads, gate, up = lax.optimization_barrier((by_heads, gate, up))
    parts = project(c[None], by_heads, out_rows, other_out)
    parts, down, far_down = lax.optimization_barrier((parts, down_weight, swapped[2]))
    parts = exchange(parts, "z")
    down, far_down = row_major(down), row_major(far_down)
    parts, down, far_down = lax.optimization_barrier((parts, down, far_down))
    ids = lax.dynamic_index_in_dim(expert_ids, d, 0, False).astype(F32)
    logits = lax.dynamic_index_in_dim(top_logits, d, 0, False).astype(F32)
    route = jnp.pad(jnp.concatenate([ids, logits], axis=1), ((0, 0), (0, 56)))
    residual, sent = norm(parts, hidden_in, norm_gain[None], route)
    sent, far_gate, far_up = lax.optimization_barrier((sent, swapped[0], swapped[1]))
    column = exchange(sent, "z")
    far_gate, far_up = row_major(far_gate.swapaxes(1, 2)), row_major(far_up.swapaxes(1, 2))
    column, far_gate, far_up = lax.optimization_barrier((column, far_gate, far_up))
    copies = spread(column, ndp)
    tokens = exchange(copies, ("x", "y")).reshape(ndp * nz * steps, -1)
    own = (gate, up, down)
    other = (far_gate, far_up, far_down)
    per = gate_weight.shape[0]
    first = jnp.stack([(2 * z + c) * per, (2 * z + 1 - c) * per]).astype(jnp.int32)
    made = experts(first, tokens, own, other)
    back = exchange(made.reshape(ndp, nz * steps, width), ("x", "y"))
    column_sum = jnp.sum(back.astype(F32), axis=0).astype(BF16)
    final = exchange(column_sum.reshape(nz, steps, width), "z")
    out = residual + jnp.sum(final.astype(F32), axis=0)
    return out.astype(BF16)[None]


def solution(mesh):
    shape = dict(mesh.shape)
    side = int(round(shape["dp"] ** 0.5))
    fine = Mesh(
        mesh.devices.reshape(side, shape["dp"] // side, shape["expert"] // 2, 2),
        ("x", "y", "z", "c"),
    )
    row = ("z", "c", "x", "y")
    group = ("z", "c")
    dp = ("x", "y")
    placed = (
        P(row, None, None),
        P(row, None, None),
        P(row, None, None),
        P(row, None, None),
        P(row, None, None),
        P(row, None, None),
        P(row),
        P(group, None),
        P(),
        P(group, None, None),
        P(group, None, None),
        P(group, None, dp),
        P(group, None, dp),
        P(group, dp, None),
    )
    return jax.shard_map(
        on_device,
        mesh=fine,
        in_specs=placed,
        out_specs=P(row, None, None),
        check_vma=False,
    )
```

time: 137 us -> 126 us (0.920)
  local copies, waits for them, and re-layouts: 37.2 us -> 16 us
  waiting for transfers between devices: 15.4 us -> 27.7 us
  blocking collectives: 46.1 us -> 37.6 us
  starting transfers between devices: 20.1 us -> 24.8 us
  Pallas kernels: 12.5 us -> 17 us
  matrix products: 2.41 us -> 0 us
    unnamed x21 -> x10, local copies, waits for them, and re-layouts: 18.9 us -> 0.02 us
    ppermute x3 -> x0, local copies, waits for them, and re-layouts: 16.2 us -> none  [on_device(): lax.ppermute(w, 'c', SWAP)]
    all_to_all x3 -> x4, waiting for transfers between devices: 15.4 us -> 27.7 us  [exchange(): return lax.all_to_all(value, axis, split_axis=0, concat_axis=0, tiled=True)]
    optimization_barrier x0 -> x4, local copies, waits for them, and re-layouts: none -> 11.2 us  [the longest x2 6.41 us: on_device(): lax.optimization_barrier((sent, swapped[0], swapped[1]))]
    all_to_all x3 -> x2, blocking collectives: 46.1 us -> 37.6 us  [exchange(): return lax.all_to_all(value, axis, split_axis=0, concat_axis=0, tiled=True)]
    transpose x0 -> x1, local copies, waits for them, and re-layouts: none -> 4.72 us  [on_device(): gate, up = (row_major(gate.swapaxes(1, 2)), row_major(up.swapaxes(1, 2)))]
    all_to_all x3 -> x4, starting transfers between devices: 19.4 us -> 23.8 us  [exchange(): return lax.all_to_all(value, axis, split_axis=0, concat_axis=0, tiled=True)]
    pallas_call x2 -> x4, Pallas kernels: 12.3 us -> 16.2 us  [the longest x1 8.85 us: experts(): pl.pallas_call(experts_kernel, in_specs=[smem(), vmem()] + [hbm()] * 6, o...]
  transfers between devices with their start and end apart: 7 -> 8, of which waited for: 2 -> 4; matrix products, arithmetic and copies ran while one was open for 26% -> 13% of each run, Pallas kernels for 1% -> 5%
where the time goes in v2:
time: 126 us; the launch traced here: 125 us
  blocking collectives  37.6 us (30%)
  waiting for transfers between devices  27.7 us (22%)
  starting transfers between devices  24.8 us (20%)
  Pallas kernels  17 us (13%)
  local copies, waits for them, and re-layouts  16 us (13%)
    all_to_all x2, blocking collectives, exchange(): return lax.all_to_all(value, axis, split_axis=0, concat_axis=0, tiled=True)  37.6 us
    all_to_all x4, waiting for transfers between devices, exchange(): return lax.all_to_all(value, axis, split_axis=0, concat_axis=0, tiled=True)  27.7 us
    all_to_all x4, starting transfers between devices, exchange(): return lax.all_to_all(value, axis, split_axis=0, concat_axis=0, tiled=True)  23.8 us
    pallas_call x1, Pallas kernels, experts(): pl.pallas_call(experts_kernel, in_specs=[smem(), vmem()] + [hbm()] * 6, o...  8.85 us
    optimization_barrier x2, local copies, waits for them, and re-layouts, on_device(): lax.optimization_barrier((sent, swapped[0], swapped[1]))  6.41 us
    optimization_barrier x2, local copies, waits for them, and re-layouts, on_device(): lax.optimization_barrier((parts, down_weight, swapped[2]))  4.82 us
    transpose x1, local copies, waits for them, and re-layouts, on_device(): gate, up = (row_major(gate.swapaxes(1, 2)), row_major(up.swapaxes(1, 2)))  4.72 us
    pallas_call x1, Pallas kernels, project(): pl.pallas_call(project_kernel, in_specs=[smem(), vmem(), hbm(), hbm()], o...  3.37 us
  transfers between devices with their start and end apart: 8, of which 4 were waited for; matrix products, arithmetic and copies ran while one was open for 13% of the time, Pallas kernels for 5%

profile of v2, /device:TPU:8, one launch (start us, length us, event | category | flops | bytes accessed | tf_op | source)
XLA Modules:
  0.0 125.1 jit_solution(5907753747098561720)
XLA Ops:
  0.0 0.0 collective-permute-start.1
  0.0 0.5 collective-permute-start.2
  0.5 0.0 collective-permute-start.3
  0.5 0.5 collective-permute-start
  1.7 2.6 %attend.1 = bf16[8,2,512]{2,1,0:T(2,128)(2,1)} custom-call(s32[1]{0:T(128)S(6)} %copy.67.len_ref, bf16[1,2,4096]{2,1,0:T(2,128)(2,1)} %q_hbm.1, bf16[1,2,512]{2,1,0:T(2,128)(2,1)} %nk_hbm.1, bf16[1,2,512]{2,1,0:T(2,128)(2,1)} %nv_hbm.1, bf16[1,512,512]{2,1,0:T(8,128)(2,1)} %k_hbm.1, bf16[1,512,512]{2,1,0:T(8,128)(2,1)} %v_hbm.1), custom_call_target="tpu_custom_call" | custom-call | tf_op jit(solution)/shard_map/attend/pallas_call | solution.py:102
  4.3 8.5 %all-to-all-start = ((bf16[8,2,512]{2,1,0:T(2,128)(2,1)}), bf16[8,2,512]{2,1,0:T(2,128)(2,1)S(1)}, u32[]{:S(2)}, u32[]{:S(2)}) async-start(bf16[8,2,512]{2,1,0:T(2,128)(2,1)} %attend.1), calls=%async_computation | async-start | bytes 32768 | tf_op jit(solution)/shard_map/all_to_all | solution.py:288
  12.8 4.7 %copy_bitcast_fusion.2 = (bf16[2,180,2880]{2,1,0:T(8,128)(2,1)}, bf16[2,180,2880]{2,1,0:T(8,128)(2,1)}) fusion(bf16[2,2880,180]{1,0,2:T(2,128)(2,1)} %param.26, bf16[2,2880,180]{1,0,2:T(2,128)(2,1)} %param.25), kind=kLoop, calls=%fused_computation.2 | loop fusion | bytes 8294400 | tf_op jit(solution)/shard_map/transpose | solution.py:322
  17.5 0.0 copy-start.2
  17.5 0.0 copy-start.3
  17.5 0.0 copy-start.4
  17.5 0.0 copy-start.1
  17.5 3.1 %all-to-all-done.x_ref = bf16[8,2,512]{2,1,0:T(2,128)(2,1)S(1)} async-done(((bf16[8,2,512]{2,1,0:T(2,128)(2,1)}), bf16[8,2,512]{2,1,0:T(2,128)(2,1)S(1)}, u32[]{:S(2)}, u32[]{:S(2)}) %all-to-all-start) | async-done | bytes 16416 | tf_op jit(solution)/shard_map/all_to_all | solution.py:288
  20.6 0.0 collective-permute-done.other_hbm
  20.6 3.4 %project.1 = bf16[8,2,2880]{2,1,0:T(2,128)(2,1)} custom-call(s32[1]{0:T(128)} %bitcast.core_ref, bf16[8,2,512]{2,1,0:T(2,128)(2,1)S(1)} %all-to-all-done.x_ref, bf16[2880,256]{1,0:T(8,128)(2,1)} %bitcast.23, bf16[2880,256]{1,0:T(8,128)(2,1)} %collective-permute-done.other_hbm), custom_call_target="tpu_custom_call" | custom-call | tf_op jit(solution)/shard_map/project/pallas_call | solution.py:147
  24.0 0.0 collective-permute-done.1
  24.0 4.3 %all-to-all-start.1 = ((bf16[8,2,2880]{2,1,0:T(2,128)(2,1)}), bf16[8,2,2880]{2,1,0:T(2,128)(2,1)S(1)}, u32[]{:S(2)}, u32[]{:S(2)}) async-start(bf16[8,2,2880]{2,1,0:T(2,128)(2,1)} %project.1), calls=%async_computation.1 | async-start | bytes 188416 | tf_op jit(solution)/shard_map/all_to_all | solution.py:288
  28.3 0.0 copy-done.2
  28.3 0.0 copy-done.3
  28.4 0.0 copy-done.4
  28.4 0.2 convert_reduce_fusion.1
  28.5 0.1 select_maximum_fusion.route_ref
  28.6 0.0 copy-done.1
  28.6 1.6 %copy.55.d0_hbm = bf16[2,180,2880]{2,1,0:T(8,128)(2,1)} copy(bf16[2,180,2880]{2,0,1:T(2,128)(2,1)S(1)} %copy-done.1) | data formatting | bytes 4147200 | tf_op jit(solution)/shard_map/optimization_barrier | solution.py:325
  30.2 0.0 copy-start
  30.2 3.2 %copy.56.d1_hbm = bf16[2,180,2880]{2,1,0:T(8,128)(2,1)} copy(bf16[2,180,2880]{2,0,1:T(2,128)(2,1)} %collective-permute-done.1) | data formatting | bytes 4147200 | tf_op jit(solution)/shard_map/optimization_barrier | solution.py:325
  33.4 3.6 %all-to-all-done.1.part_ref = bf16[8,2,2880]{2,1,0:T(2,128)(2,1)S(1)} async-done(((bf16[8,2,2880]{2,1,0:T(2,128)(2,1)}), bf16[8,2,2880]{2,1,0:T(2,128)(2,1)S(1)}, u32[]{:S(2)}, u32[]{:S(2)}) %all-to-all-start.1) | async-done | bytes 92192 | tf_op jit(solution)/shard_map/all_to_all | solution.py:288
  37.0 0.0 copy-done
  37.0 0.8 norm.1
  37.8 0.0 collective-permute-done.2
  37.8 0.0 collective-permute-done.3
  37.8 3.6 %all-to-all-start.2 = ((bf16[8,2,2944]{2,1,0:T(2,128)(2,1)}), bf16[8,2,2944]{2,1,0:T(2,128)(2,1)S(1)}, u32[]{:S(2)}, u32[]{:S(2)}) async-start(bf16[8,2,2944]{2,1,0:T(2,128)(2,1)} %get-tuple-element.35), calls=%async_computation.2 | async-start | bytes 188416 | tf_op jit(solution)/shard_map/all_to_all | solution.py:288
  41.4 3.2 %copy.66 = bf16[2,2880,180]{1,2,0:T(8,128)(2,1)} copy(bf16[2,2880,180]{1,0,2:T(2,128)(2,1)} %collective-permute-done.2) | data formatting | bytes 4147200 | tf_op jit(solution)/shard_map/optimization_barrier | solution.py:333
  44.7 3.2 %copy.65 = bf16[2,2880,180]{1,2,0:T(8,128)(2,1)} copy(bf16[2,2880,180]{1,0,2:T(2,128)(2,1)} %collective-permute-done.3) | data formatting | bytes 4147200 | tf_op jit(solution)/shard_map/optimization_barrier | solution.py:333
  47.8 2.3 %all-to-all-done.2.x_ref = bf16[8,2,2944]{2,1,0:T(2,128)(2,1)S(1)} async-done(((bf16[8,2,2944]{2,1,0:T(2,128)(2,1)}), bf16[8,2,2944]{2,1,0:T(2,128)(2,1)S(1)}, u32[]{:S(2)}, u32[]{:S(2)}) %all-to-all-start.2) | async-done | bytes 94240 | tf_op jit(solution)/shard_map/all_to_all | solution.py:288
  50.1 1.3 %spread.1 = bf16[16,16,2944]{2,1,0:T(8,128)(2,1)} custom-call(bf16[8,2,2944]{2,1,0:T(2,128)(2,1)S(1)} %all-to-all-done.2.x_ref), custom_call_target="tpu_custom_call" | custom-call | tf_op jit(solution)/shard_map/spread/pallas_call | solution.py:210
  51.5 7.4 %all-to-all-start.3 = ((bf16[16,16,2944]{2,1,0:T(8,128)(2,1)}), bf16[16,16,2944]{2,1,0:T(8,128)(2,1)S(1)}, u32[]{:S(2)}, u32[]{:S(2)}) async-start(bf16[16,16,2944]{2,1,0:T(8,128)(2,1)} %spread.1), calls=%async_computation.3 | async-start | bytes 3014656 | tf_op jit(solution)/shard_map/all_to_all | solution.py:288
  58.9 0.1 pad_add_fusion.first_ref
  59.0 18.7 %all-to-all-done.3 = bf16[16,16,2944]{2,1,0:T(8,128)(2,1)S(1)} async-done(((bf16[16,16,2944]{2,1,0:T(8,128)(2,1)}), bf16[16,16,2944]{2,1,0:T(8,128)(2,1)S(1)}, u32[]{:S(2)}, u32[]{:S(2)}) %all-to-all-start.3) | async-done | bytes 1507360 | tf_op jit(solution)/shard_map/all_to_all | solution.py:288
  77.7 8.8 %experts.1 = bf16[256,2880]{1,0:T(8,128)(2,1)S(1)} custom-call(s32[2]{0:T(128)S(1)} %pad_add_fusion.first_ref, bf16[256,2944]{1,0:T(8,128)(2,1)S(1)} %bitcast.18, bf16[2,180,2880]{2,1,0:T(8,128)(2,1)} %get-tuple-element.39.g0_hbm, bf16[2,180,2880]{2,1,0:T(8,128)(2,1)} %get-tuple-element.40.u0_hbm, bf16[2,180,2880]{2,1,0:T(8,128)(2,1)} %bitcast.20, ...), custom_call_target="tpu_custom_call" | custom-call | tf_op jit(solution)/shard_map/experts/pallas_call | solution.py:271
  86.5 24.1 %all_to_all.30 = bf16[16,16,2880]{2,1,0:T(8,128)(2,1)S(1)} all-to-all(bf16[16,16,2880]{2,1,0:T(8,128)(2,1)S(1)} %bitcast.19), channel_id=1, replica_groups=mesh['x'=4,'y'=4,'z'=8,'c'=2] {'x','y'}, dimensions={0} | all-to-all | bytes 2949120 | tf_op jit(solution)/shard_map/all_to_all | solution.py:288
  110.6 0.2 reduce_sum.21
  110.8 13.6 %all_to_all.31 = bf16[8,2,2880]{2,1,0:T(2,128)(2,1)S(1)} all-to-all(bf16[8,2,2880]{2,1,0:T(2,128)(2,1)S(1)} %reshape.14), channel_id=1, replica_groups=mesh['x'=4,'y'=4,'z'=8,'c'=2] {'z'}, dimensions={0} | all-to-all | bytes 184320 | tf_op jit(solution)/shard_map/all_to_all | solution.py:288
  124.4 0.1 convert_reduce_fusion
  124.5 0.6 fusion
  (2 shorter events, 0.1 us)
Async XLA Ops:
  0.0 24.0 %collective-permute-start.1 = (bf16[2,180,2880]{2,0,1:T(2,128)(2,1)}, bf16[2,180,2880]{2,0,1:T(2,128)(2,1)}, u32[]{:S(2)}, u32[]{:S(2)}) collective-permute-start(bf16[2,180,2880]{2,0,1:T(2,128)(2,1)} %param.27), channel_id=1, source_target_pairs={{0,1},{1,0},{2,3},{3,2},{4,5},{5,4},{6,7},{7,6},{8,9},{9,8},{10,11... | collective-permute-start | bytes 6220808 | tf_op jit(solution)/shard_map/ppermute | solution.py:316
  0.0 37.8 %collective-permute-start.2 = (bf16[2,2880,180]{1,0,2:T(2,128)(2,1)}, bf16[2,2880,180]{1,0,2:T(2,128)(2,1)}, u32[]{:S(2)}, u32[]{:S(2)}) collective-permute-start(bf16[2,2880,180]{1,0,2:T(2,128)(2,1)} %param.25), channel_id=1, source_target_pairs={{0,1},{1,0},{2,3},{3,2},{4,5},{5,4},{6,7},{7,6},{8,9},{9,8},{10,11... | collective-permute-start | bytes 6220808 | tf_op jit(solution)/shard_map/ppermute | solution.py:316
  0.5 37.3 %collective-permute-start.3 = (bf16[2,2880,180]{1,0,2:T(2,128)(2,1)}, bf16[2,2880,180]{1,0,2:T(2,128)(2,1)}, u32[]{:S(2)}, u32[]{:S(2)}) collective-permute-start(bf16[2,2880,180]{1,0,2:T(2,128)(2,1)} %param.26), channel_id=1, source_target_pairs={{0,1},{1,0},{2,3},{3,2},{4,5},{5,4},{6,7},{7,6},{8,9},{9,8},{10,11... | collective-permute-start | bytes 6220808 | tf_op jit(solution)/shard_map/ppermute | solution.py:316
  0.5 20.1 %collective-permute-start = (bf16[2880,256]{1,0:T(8,128)(2,1)}, bf16[2880,256]{1,0:T(8,128)(2,1)}, u32[]{:S(2)}, u32[]{:S(2)}) collective-permute-start(bf16[2880,256]{1,0:T(8,128)(2,1)} %bitcast.22), channel_id=1, source_target_pairs={{0,1},{1,0},{2,3},{3,2},{4,5},{5,4},{6,7},{7,6},{8,9},{9,8},{10,11... | collective-permute-start | bytes 4423688 | tf_op jit(solution)/shard_map/ppermute | solution.py:314
  4.3 16.3 %all-to-all-start = ((bf16[8,2,512]{2,1,0:T(2,128)(2,1)}), bf16[8,2,512]{2,1,0:T(2,128)(2,1)S(1)}, u32[]{:S(2)}, u32[]{:S(2)}) async-start(bf16[8,2,512]{2,1,0:T(2,128)(2,1)} %attend.1), calls=%async_computation | async-start | bytes 32768 | tf_op jit(solution)/shard_map/all_to_all | solution.py:288
  17.5 10.8 %copy-start.2 = (f32[2880]{0:T(1024)S(1)}, f32[2880]{0:T(1024)}, u32[]{:S(2)}) copy-start(f32[2880]{0:T(1024)} %param.22) | copy-start | bytes 34564
  17.5 10.8 %copy-start.3 = (s32[16,2,4]{0,2,1:T(4,128)S(1)}, s32[16,2,4]{0,2,1:T(4,128)}, u32[]{:S(2)}) copy-start(s32[16,2,4]{0,2,1:T(4,128)} %param.23) | copy-start | bytes 1540
  17.5 10.8 %copy-start.4 = (bf16[16,2,4]{0,2,1:T(4,128)(2,1)S(1)}, bf16[16,2,4]{0,2,1:T(4,128)(2,1)}, u32[]{:S(2)}) copy-start(bf16[16,2,4]{0,2,1:T(4,128)(2,1)} %param.24) | copy-start | bytes 772
  17.5 11.1 %copy-start.1 = (bf16[2,180,2880]{2,0,1:T(2,128)(2,1)S(1)}, bf16[2,180,2880]{2,0,1:T(2,128)(2,1)}, u32[]{:S(2)}) copy-start(bf16[2,180,2880]{2,0,1:T(2,128)(2,1)} %param.27) | copy-start | bytes 6220804
  24.0 13.0 %all-to-all-start.1 = ((bf16[8,2,2880]{2,1,0:T(2,128)(2,1)}), bf16[8,2,2880]{2,1,0:T(2,128)(2,1)S(1)}, u32[]{:S(2)}, u32[]{:S(2)}) async-start(bf16[8,2,2880]{2,1,0:T(2,128)(2,1)} %project.1), calls=%async_computation.1 | async-start | bytes 188416 | tf_op jit(solution)/shard_map/all_to_all | solution.py:288
  30.2 6.8 %copy-start = (bf16[1,2,2880]{2,1,0:T(2,128)(2,1)S(1)}, bf16[1,2,2880]{2,1,0:T(2,128)(2,1)}, u32[]{:S(2)}) copy-start(bf16[1,2,2880]{2,1,0:T(2,128)(2,1)} %hid_ref.1) | copy-start | bytes 34564
  37.8 12.3 %all-to-all-start.2 = ((bf16[8,2,2944]{2,1,0:T(2,128)(2,1)}), bf16[8,2,2944]{2,1,0:T(2,128)(2,1)S(1)}, u32[]{:S(2)}, u32[]{:S(2)}) async-start(bf16[8,2,2944]{2,1,0:T(2,128)(2,1)} %get-tuple-element.35), calls=%async_computation.2 | async-start | bytes 188416 | tf_op jit(solution)/shard_map/all_to_all | solution.py:288
  51.5 26.2 %all-to-all-start.3 = ((bf16[16,16,2944]{2,1,0:T(8,128)(2,1)}), bf16[16,16,2944]{2,1,0:T(8,128)(2,1)S(1)}, u32[]{:S(2)}, u32[]{:S(2)}) async-start(bf16[16,16,2944]{2,1,0:T(8,128)(2,1)} %spread.1), calls=%async_computation.3 | async-start | bytes 3014656 | tf_op jit(solution)/shard_map/all_to_all | solution.py:288

commit v3 on v2

v3 whole, which is shorter than its diff:
```python
import jax
import jax.numpy as jnp
from jax import lax
from jax.experimental import pallas as pl
from jax.experimental.pallas import tpu as pltpu
from jax.sharding import Mesh
from jax.sharding import PartitionSpec as P

HQ = 64
KVH = 8
HD = 64
SWAP = [(0, 1), (1, 0)]
F32 = jnp.float32
BF16 = jnp.bfloat16


def params(mib):
    return pltpu.CompilerParams(vmem_limit_bytes=mib * 1024 * 1024)


def vmem():
    return pl.BlockSpec(memory_space=pltpu.VMEM)


def hbm():
    return pl.BlockSpec(memory_space=pltpu.HBM)


def stay(*values):
    return [pltpu.with_memory_space_constraint(v, pltpu.HBM) for v in values]


def smem():
    return pl.BlockSpec(memory_space=pltpu.SMEM)


def attend_kernel(
    len_ref, q_hbm, nk_hbm, nv_hbm, k_hbm, v_hbm, out_ref,
    q_ref, nk_ref, nv_ref, k_ref, v_ref, rows_ref, flat_ref, sems,
):
    pairs = (
        (k_hbm, k_ref), (q_hbm, q_ref), (nk_hbm, nk_ref), (nv_hbm, nv_ref), (v_hbm, v_ref),
    )
    copies = [pltpu.make_async_copy(a, b, sems.at[i]) for i, (a, b) in enumerate(pairs)]
    for copy in copies:
        copy.start()
    steps = q_ref.shape[1]
    width = KVH * HD
    rows = HQ * steps
    per_group = rows // KVH
    copies[1].wait()
    q = q_ref[0].astype(F32) * 0.125
    for h in range(HQ):
        rows_ref[h * steps : (h + 1) * steps, :] = q[:, h * HD : (h + 1) * HD]
    q_rows = rows_ref[...]
    q_pair = jnp.concatenate([q_rows, q_rows], axis=1)
    q_wide = jnp.concatenate([q_pair] * (KVH // 2), axis=1)
    row_id = lax.broadcasted_iota(jnp.int32, (rows, width), 0)
    col_id = lax.broadcasted_iota(jnp.int32, (rows, width), 1)
    in_group = row_id // per_group == col_id // HD
    q_wide = jnp.where(in_group, q_wide, 0.0)
    q_bf = q_wide.astype(BF16)
    copies[0].wait()
    scores = lax.dot_general(
        q_bf, k_ref[0], (((1,), (1,)), ((), ())), preferred_element_type=F32
    )
    slot = lax.broadcasted_iota(jnp.int32, scores.shape, 1)
    weights = jnp.where(slot < len_ref[0], jnp.exp(scores), 0.0)
    total = jnp.sum(weights, axis=1, keepdims=True)
    copies[2].wait()
    copies[3].wait()
    nk = nk_ref[0].astype(F32)
    nv = nv_ref[0].astype(F32)
    step_id = lax.broadcasted_iota(jnp.int32, (rows, 1), 0) % steps
    fresh = []
    for s in range(steps):
        score = jnp.sum(q_wide * nk[s : s + 1, :], axis=1, keepdims=True)
        weight = jnp.where(step_id >= s, jnp.exp(score), 0.0)
        total = total + weight
        fresh.append(weight)
    probs = (weights / total).astype(BF16)
    copies[4].wait()
    mixed = jnp.dot(probs, v_ref[0], preferred_element_type=F32)
    for s in range(steps):
        mixed = mixed + (fresh[s] / total).astype(BF16).astype(F32) * nv[s : s + 1, :]
    mixed = jnp.where(in_group, mixed, 0.0)
    folded = mixed[:, :128]
    for i in range(1, width // 128):
        folded = folded + mixed[:, i * 128 : (i + 1) * 128]
    rows_ref[...] = folded[:, :HD] + folded[:, HD:]
    for h in range(HQ):
        flat_ref[:, h * HD : (h + 1) * HD] = rows_ref[h * steps : (h + 1) * steps, :]
    blocks = out_ref.shape[0]
    wide = HQ * HD // blocks
    for b in range(blocks):
        out_ref[b] = flat_ref[:, b * wide : (b + 1) * wide].astype(BF16)


def attend(length, q, nk, nv, k, v, blocks):
    steps = q.shape[1]
    return pl.pallas_call(
        attend_kernel,
        in_specs=[smem()] + [hbm()] * 5,
        out_specs=vmem(),
        out_shape=jax.ShapeDtypeStruct((blocks, steps, HQ * HD // blocks), BF16),
        scratch_shapes=[pltpu.VMEM(a.shape, BF16) for a in (q, nk, nv, k, v)]
        + [
            pltpu.VMEM((HQ * steps, HD), F32),
            pltpu.VMEM((steps, HQ * HD), F32),
            pltpu.SemaphoreType.DMA((5,)),
        ],
        compiler_params=params(12),
        name="attend",
    )(length, *stay(q, nk, nv, k, v))


def project_kernel(
    place_ref, x_ref, hid_ref, route_ref, own_hbm, other_hbm, keep_ref, send_ref,
    rows_ref, own_ref, other_ref, sems,
):
    width, feats = own_ref.shape
    chunk = 640
    cuts = [(start, min(start + chunk, width)) for start in range(0, width, chunk)]
    copies = []
    for i, (start, stop) in enumerate(cuts):
        span = pl.ds(start, stop - start)
        copies.append(
            (
                pltpu.make_async_copy(own_hbm.at[span], own_ref.at[span], sems.at[2 * i]),
                pltpu.make_async_copy(other_hbm.at[span], other_ref.at[span], sems.at[2 * i + 1]),
            )
        )
        copies[-1][0].start()
        copies[-1][1].start()
    blocks, steps, _ = x_ref.shape
    for i in range(blocks):
        rows_ref[i * steps : (i + 1) * steps, :] = x_ref[i].astype(F32)
    x = rows_ref[...].astype(BF16)
    low, high = x[:, :feats], x[:, feats:]
    first = place_ref[1] == 0
    mine = jnp.where(first, low, high)
    theirs = jnp.where(first, high, low)
    extra = jnp.concatenate([hid_ref[0].astype(F32), route_ref[...]], axis=1)
    extra = jnp.concatenate([extra] * blocks, axis=0)
    block = lax.broadcasted_iota(jnp.int32, extra.shape, 0) // steps
    extra = jnp.where(block == place_ref[0], extra, 0.0)
    dims = (((1,), (1,)), ((), ()))
    for (start, stop), (first_copy, second_copy) in zip(cuts, copies):
        first_copy.wait()
        second_copy.wait()
        part = lax.dot_general(mine, own_ref[start:stop], dims, preferred_element_type=F32)
        part = part + lax.dot_general(
            theirs, other_ref[start:stop], dims, preferred_element_type=F32
        )
        part = part + extra[:, start:stop]
        keep_ref[:, start:stop] = part
        send_ref[:, start:stop] = part.astype(BF16)
    keep_ref[:, width:] = extra[:, width:]
    send_ref[:, width:] = extra[:, width:].astype(BF16)


def project(place, x, hidden, route, own, other):
    blocks, steps, feats = x.shape
    wide = own.shape[0] + route.shape[1]
    rows = blocks * steps
    return pl.pallas_call(
        project_kernel,
        in_specs=[smem(), vmem(), vmem(), vmem(), hbm(), hbm()],
        out_specs=[vmem(), vmem()],
        out_shape=[
            jax.ShapeDtypeStruct((rows, wide), F32),
            jax.ShapeDtypeStruct((rows, wide), BF16),
        ],
        scratch_shapes=[
            pltpu.VMEM((rows, feats), F32),
            pltpu.VMEM(own.shape, BF16),
            pltpu.VMEM(own.shape, BF16),
            pltpu.SemaphoreType.DMA((2 * pl.cdiv(own.shape[0], 640),)),
        ],
        compiler_params=params(12),
        name="project",
    )(place, x, hidden, route, *stay(own, other))


def pair_kernel(keep_ref, got_ref, out_ref):
    total = (keep_ref[...] + got_ref[...].astype(F32)).astype(BF16)
    for i in range(out_ref.shape[0]):
        out_ref[i] = total


def pair(keep, got, copies):
    return pl.pallas_call(
        pair_kernel,
        in_specs=[vmem(), vmem()],
        out_specs=vmem(),
        out_shape=jax.ShapeDtypeStruct((copies,) + keep.shape, BF16),
        compiler_params=params(12),
        name="pair",
    )(keep, got)


def norm_kernel(place_ref, part_ref, gain_ref, res_ref, out_ref):
    steps, width = res_ref.shape
    total = part_ref[0].astype(F32)
    for i in range(1, part_ref.shape[0]):
        total = total + part_ref[i].astype(F32)
    res = total[:, :width]
    own = jnp.zeros((steps, width), F32)
    for i in range(res.shape[0] // steps):
        own = own + jnp.where(place_ref[0] == i, res[i * steps : (i + 1) * steps, :], 0.0)
    res_ref[...] = own
    scale = lax.rsqrt(jnp.sum(res * res, axis=1, keepdims=True) / width + 1e-05)
    normed = (res * scale * gain_ref[...]).astype(BF16)
    full = jnp.concatenate([normed.astype(F32), total[:, width:]], axis=1).astype(BF16)
    for i in range(out_ref.shape[0]):
        out_ref[i] = full


def norm(place, parts, gain, copies, steps):
    _, rows, wide = parts.shape
    width = gain.shape[1]
    return pl.pallas_call(
        norm_kernel,
        in_specs=[smem(), vmem(), vmem()],
        out_specs=[vmem(), vmem()],
        out_shape=[
            jax.ShapeDtypeStruct((steps, width), F32),
            jax.ShapeDtypeStruct((copies, rows, wide), BF16),
        ],
        compiler_params=params(12),
        name="norm",
    )(place, parts, gain)


def experts_kernel(
    first_ref, x_ref, g0_hbm, u0_hbm, g1_hbm, u1_hbm, d0_hbm, d1_hbm, out_ref,
    w_ref, d_ref, act_ref, sems,
):
    rows, wide = g0_hbm.shape
    width = out_ref.shape[1]
    part = rows // 2
    pairs = (
        (g0_hbm, w_ref.at[0, pl.ds(0, rows)]), (u0_hbm, w_ref.at[0, pl.ds(rows, rows)]),
        (g1_hbm, w_ref.at[1, pl.ds(0, rows)]), (u1_hbm, w_ref.at[1, pl.ds(rows, rows)]),
        (d0_hbm, d_ref.at[pl.ds(0, rows)]), (d1_hbm, d_ref.at[pl.ds(rows, rows)]),
    )
    copies = [pltpu.make_async_copy(a, b, sems.at[i]) for i, (a, b) in enumerate(pairs)]
    for copy in copies:
        copy.start()
    x = x_ref[...]
    route = x_ref[:, width : width + 8].astype(F32)
    ids = route[:, 0:4]
    expo = jnp.exp(route[:, 4:8])
    total = jnp.sum(expo, axis=1, keepdims=True)
    column = lax.broadcasted_iota(jnp.int32, (x.shape[0], rows), 1)
    dims = (((1,), (1,)), ((), ()))
    for side in range(2):
        shares = []
        for e in range(2):
            label = (first_ref[side] + e).astype(F32)
            shares.append(
                jnp.sum(jnp.where(ids == label, expo, 0.0), axis=1, keepdims=True) / total
            )
        share = jnp.where(column < part, shares[0], shares[1])
        copies[2 * side].wait()
        copies[2 * side + 1].wait()
        both = lax.dot_general(x, w_ref[side], dims, preferred_element_type=F32)
        gate, up = both[:, :rows], both[:, rows:]
        act = gate * jax.nn.sigmoid(1.702 * gate) * (up + 1.0)
        act_ref[:, side * rows : (side + 1) * rows] = (act * share).astype(BF16)
    copies[4].wait()
    copies[5].wait()
    chunk = 768
    for start in range(0, width, chunk):
        stop = min(start + chunk, width)
        out_ref[:, start:stop] = jnp.dot(
            act_ref[...], d_ref[:, start:stop], preferred_element_type=F32
        ).astype(BF16)


def experts(first, x, own, other, width):
    rows, wide = own[0].shape
    args = (own[0], own[1], other[0], other[1], own[2], other[2])
    return pl.pallas_call(
        experts_kernel,
        in_specs=[smem(), vmem()] + [hbm()] * 6,
        out_specs=vmem(),
        out_shape=jax.ShapeDtypeStruct((x.shape[0], width), BF16),
        scratch_shapes=[
            pltpu.VMEM((2, 2 * rows, wide), BF16),
            pltpu.VMEM((2 * rows, wide), BF16),
            pltpu.VMEM((x.shape[0], 2 * rows), BF16),
            pltpu.SemaphoreType.DMA((len(args),)),
        ],
        compiler_params=params(32),
        name="experts",
    )(first, x, *stay(*args[:-1]), args[-1])


def stacked(value):
    per, rows, width = value.shape
    high, wide = rows + -rows % 64, width + -width % 128
    value = jnp.pad(value, ((0, 0), (0, high - rows), (0, wide - width)))
    return value.reshape(per * high, wide)


def exchange(value, axis):
    return lax.all_to_all(value, axis, split_axis=0, concat_axis=0, tiled=True)


def on_device(
    hidden_in,
    queries,
    new_keys,
    new_values,
    key_cache,
    value_cache,
    prompt_lengths,
    out_weight,
    norm_gain,
    expert_ids,
    top_logits,
    gate_weight,
    up_weight,
    down_weight,
):
    steps, width = hidden_in.shape[1:]
    zaxis = ("w", "v")
    dp = ("x", "y")
    nz = lax.axis_size(zaxis)
    ndp = lax.axis_size(dp)
    z = lax.axis_index(zaxis)
    c = lax.axis_index("c")
    d = lax.axis_index(dp)
    per = gate_weight.shape[0]
    out_rows = out_weight.T
    other_out = lax.ppermute(out_rows, "c", SWAP)
    attended = attend(
        prompt_lengths, queries, new_keys, new_values, key_cache, value_cache, nz
    )
    attended, gate = lax.optimization_barrier((attended, gate_weight))
    ids = lax.dynamic_index_in_dim(expert_ids, d, 0, False).astype(F32)
    logits = lax.dynamic_index_in_dim(top_logits, d, 0, False).astype(F32)
    route = jnp.pad(jnp.concatenate([ids, logits], axis=1), ((0, 0), (0, 56)))
    place = jnp.stack([z, c]).astype(jnp.int32)
    first = jnp.stack([(2 * z + c) * per, (2 * z + 1 - c) * per]).astype(jnp.int32)
    by_heads = exchange(attended, zaxis)
    gate = stacked(gate.swapaxes(1, 2))
    by_heads, gate, route, place, first = lax.optimization_barrier(
        (by_heads, gate, route, place, first)
    )
    far_gate = lax.ppermute(gate, "c", SWAP)
    keep, sent = project(place, by_heads, hidden_in, route, out_rows, other_out)
    sent, up = lax.optimization_barrier((sent, up_weight))
    got = lax.ppermute(sent, "v", SWAP)
    up = stacked(up.swapaxes(1, 2))
    got, up = lax.optimization_barrier((got, up))
    far_up = lax.ppermute(up, "c", SWAP)
    quads = pair(keep, got, nz // 2)
    quads, down = lax.optimization_barrier((quads, down_weight))
    parts = exchange(quads, "w")
    down = stacked(down)
    parts, down = lax.optimization_barrier((parts, down))
    far_down = lax.ppermute(down, "c", SWAP)
    residual, copies = norm(place, parts, norm_gain[None], ndp, steps)
    copies, far_gate, far_up, far_down = lax.optimization_barrier(
        (copies, far_gate, far_up, far_down)
    )
    tokens = exchange(copies, dp).reshape(ndp * nz * steps, -1)
    made = experts(first, tokens, (gate, up, down), (far_gate, far_up, far_down), width)
    back = exchange(made.reshape(ndp, nz * steps, width), dp)
    column_sum = jnp.sum(back.astype(F32), axis=0).astype(BF16)
    final = exchange(column_sum.reshape(nz, steps, width), zaxis)
    out = residual + jnp.sum(final.astype(F32), axis=0)
    return out.astype(BF16)[None]


def solution(mesh):
    shape = dict(mesh.shape)
    side = int(round(shape["dp"] ** 0.5))
    fine = Mesh(
        mesh.devices.reshape(side, shape["dp"] // side, shape["expert"] // 4, 2, 2),
        ("x", "y", "w", "v", "c"),
    )
    row = ("w", "v", "c", "x", "y")
    group = ("w", "v", "c")
    dp = ("x", "y")
    placed = (
        P(row, None, None),
        P(row, None, None),
        P(row, None, None),
        P(row, None, None),
        P(row, None, None),
        P(row, None, None),
        P(row),
        P(group, None),
        P(),
        P(group, None, None),
        P(group, None, None),
        P(group, None, dp),
        P(group, None, dp),
        P(group, dp, None),
    )
    return jax.shard_map(
        on_device,
        mesh=fine,
        in_specs=placed,
        out_specs=P(row, None, None),
        check_vma=False,
    )
```

time: 126 us -> 122 us (0.968)
  blocking collectives: 37.6 us -> 64.5 us
  starting transfers between devices: 24.8 us -> 13.2 us
  waiting for transfers between devices: 27.7 us -> 18.4 us
  local copies, waits for them, and re-layouts: 16 us -> 7.13 us
  Pallas kernels: 17 us -> 15.5 us
    all_to_all x2 -> x3, blocking collectives: 37.6 us -> 64.5 us  [exchange(): return lax.all_to_all(value, axis, split_axis=0, concat_axis=0, tiled=True)]
    all_to_all x4 -> x2, waiting for transfers between devices: 27.7 us -> 12.3 us  [exchange(): return lax.all_to_all(value, axis, split_axis=0, concat_axis=0, tiled=True)]
    all_to_all x4 -> x2, starting transfers between devices: 23.8 us -> 11.9 us  [exchange(): return lax.all_to_all(value, axis, split_axis=0, concat_axis=0, tiled=True)]
    optimization_barrier x4 -> x0, local copies, waits for them, and re-layouts: 11.2 us -> none  [the longest x2 6.41 us: on_device(): lax.optimization_barrier((sent, swapped[0], swapped[1]))]
    ppermute x3 -> x4, waiting for transfers between devices: 0.01 us -> 6.04 us  [the longest x1 3.76 us: on_device(): far_down = lax.ppermute(down, 'c', SWAP)]
    transpose x1 -> x0, local copies, waits for them, and re-layouts: 4.72 us -> none  [on_device(): gate, up = (row_major(gate.swapaxes(1, 2)), row_major(up.swapaxes(1, 2)))]
    unnamed x10 -> x11, local copies, waits for them, and re-layouts: 0.02 us -> 3.87 us
    pad x0 -> x3, local copies, waits for them, and re-layouts: none -> 3.21 us  [stacked(): value = jnp.pad(value, ((0, 0), (0, high - rows), (0, wide - width)))]
  transfers between devices with their start and end apart: 8 -> 7, of which waited for: 4 -> 4; matrix products, arithmetic and copies ran while one was open for 13% -> 7% of each run, Pallas kernels for 5% -> 3%
where the time goes in v3:
time: 122 us; the launch traced here: 121 us
  blocking collectives  64.5 us (53%)
  waiting for transfers between devices  18.4 us (15%)
  Pallas kernels  15.5 us (13%)
  starting transfers between devices  13.2 us (11%)
  local copies, waits for them, and re-layouts  7.13 us (6%)
  other arithmetic  1.9 us (2%)
    all_to_all x3, blocking collectives, exchange(): return lax.all_to_all(value, axis, split_axis=0, concat_axis=0, tiled=True)  64.5 us
    all_to_all x2, waiting for transfers between devices, exchange(): return lax.all_to_all(value, axis, split_axis=0, concat_axis=0, tiled=True)  12.3 us
    all_to_all x2, starting transfers between devices, exchange(): return lax.all_to_all(value, axis, split_axis=0, concat_axis=0, tiled=True)  11.9 us
    pallas_call x1, Pallas kernels, experts(): pl.pallas_call(experts_kernel, in_specs=[smem(), vmem()] + [hbm()] * 6, o...  7.95 us
    unnamed x11, local copies, waits for them, and re-layouts  3.87 us
    ppermute x1, waiting for transfers between devices, on_device(): far_down = lax.ppermute(down, 'c', SWAP)  3.76 us
    pallas_call x1, Pallas kernels, project(): pl.pallas_call(project_kernel, in_specs=[smem(), vmem(), vmem(), vmem(),...  3.29 us
    pad x3, local copies, waits for them, and re-layouts, stacked(): value = jnp.pad(value, ((0, 0), (0, high - rows), (0, wide - width)))  3.21 us
  transfers between devices with their start and end apart: 7, of which 4 were waited for; matrix products, arithmetic and copies ran while one was open for 7% of the time, Pallas kernels for 3%

profile of v3, /device:TPU:8, one launch (start us, length us, event | category | flops | bytes accessed | tf_op | source)
XLA Modules:
  0.0 121.4 jit_solution(6598304262680515317)
XLA Ops:
  0.0 0.0 collective-permute-start
  0.7 2.7 %attend.1 = bf16[8,2,512]{2,1,0:T(2,128)(2,1)} custom-call(s32[1]{0:T(128)S(6)} %copy.40.len_ref, bf16[1,2,4096]{2,1,0:T(2,128)(2,1)} %q_hbm.1, bf16[1,2,512]{2,1,0:T(2,128)(2,1)} %nk_hbm.1, bf16[1,2,512]{2,1,0:T(2,128)(2,1)} %nv_hbm.1, bf16[1,512,512]{2,1,0:T(8,128)(2,1)} %k_hbm.1, bf16[1,512,512]{2,1,0:T(8,128)(2,1)} %v_hbm.1), custom_call_target="tpu_custom_call" | custom-call | tf_op jit(solution)/shard_map/attend/pallas_call | solution.py:101
  3.4 8.5 %all-to-all-start = ((bf16[8,2,512]{2,1,0:T(2,128)(2,1)}), bf16[8,2,512]{2,1,0:T(2,128)(2,1)S(1)}, u32[]{:S(2)}, u32[]{:S(2)}) async-start(bf16[8,2,512]{2,1,0:T(2,128)(2,1)} %attend.1), calls=%async_computation | async-start | bytes 32768 | tf_op jit(solution)/shard_map/all_to_all | solution.py:308
  11.8 0.9 convert_reduce_fusion.1
  12.7 0.1 select_maximum_fusion.route_ref
  12.8 0.1 pad_add_fusion
  12.9 1.8 %copy.36 = bf16[2,180,2880]{2,1,0:T(8,128)(2,1)S(1)} copy(bf16[2,180,2880]{2,0,1:T(2,128)(2,1)} %bitcast.20) | data formatting | bytes 4147200
  14.7 0.0 copy-start
  14.7 0.2 pad.14.clone
  14.8 0.0 copy-start.1
  14.9 4.8 %all-to-all-done.x_ref = bf16[8,2,512]{2,1,0:T(2,128)(2,1)S(1)} async-done(((bf16[8,2,512]{2,1,0:T(2,128)(2,1)}), bf16[8,2,512]{2,1,0:T(2,128)(2,1)S(1)}, u32[]{:S(2)}, u32[]{:S(2)}) %all-to-all-start) | async-done | bytes 16416 | tf_op jit(solution)/shard_map/all_to_all | solution.py:308
  19.7 0.0 copy-start.2
  19.7 0.0 collective-permute-done.other_hbm
  19.7 0.0 copy-done
  19.7 3.3 %project.1 = (f32[16,2944]{1,0:T(8,128)S(1)}, bf16[16,2944]{1,0:T(8,128)(2,1)S(1)}) custom-call(s32[2]{0:T(128)S(1)} %get-tuple-element.30.place_ref, bf16[8,2,512]{2,1,0:T(2,128)(2,1)S(1)} %all-to-all-done.x_ref, bf16[1,2,2880]{2,1,0:T(2,128)(2,1)S(1)} %copy-done, f32[2,64]{1,0:T(2,128)S(1)} %select_maximum_fusion.route_ref, bf16[2880,256]{1,0:T(8,128)(2,1)} %bitcast.23, ...), custom_call_target="tpu_custom_call" | custom-call | tf_op jit(solution)/shard_map/project/pallas_call | solution.py:166
  23.0 0.7 collective-permute-start.1
  23.6 0.0 copy-done.2
  23.6 0.2 copy.37
  23.8 1.5 %pad.16.clone = bf16[2,192,2944]{2,1,0:T(8,128)(2,1)} pad(bf16[2,180,2880]{2,1,0:T(8,128)(2,1)S(1)} %copy.37, bf16[]{:T(256)} %constant.30.clone.1), padding=0_0x0_12x0_64 | pad | bytes 4334594 | tf_op jit(solution)/shard_map/jit(_pad)/pad | solution.py:303
  25.4 2.3 %collective-permute-done.1.got_ref = bf16[16,2944]{1,0:T(8,128)(2,1)S(1)} collective-permute-done((bf16[16,2944]{1,0:T(8,128)(2,1)S(1)}, bf16[16,2944]{1,0:T(8,128)(2,1)S(1)}, u32[]{:S(2)}, u32[]{:S(2)}) %collective-permute-start.1) | collective-permute-done | bytes 94240 | tf_op jit(solution)/shard_map/ppermute | solution.py:355
  27.6 0.8 pair.1
  28.4 3.5 %all-to-all-start.1 = ((bf16[4,16,2944]{2,1,0:T(8,128)(2,1)}), bf16[4,16,2944]{2,1,0:T(8,128)(2,1)S(1)}, u32[]{:S(2)}, u32[]{:S(2)}) async-start(bf16[4,16,2944]{2,1,0:T(8,128)(2,1)} %pair.1), calls=%async_computation.1 | async-start | bytes 753664 | tf_op jit(solution)/shard_map/all_to_all | solution.py:308
  31.9 0.0 copy-done.1
  31.9 0.1 collective-permute-start.2
  32.0 1.8 %copy.38 = bf16[2,180,2880]{2,1,0:T(8,128)(2,1)S(1)} copy(bf16[2,180,2880]{2,0,1:T(2,128)(2,1)} %param.27) | data formatting | bytes 4147200
  33.8 0.0 copy-start.3
  33.8 1.5 %pad.17.clone = bf16[2,192,2944]{2,1,0:T(8,128)(2,1)} pad(bf16[2,180,2880]{2,1,0:T(8,128)(2,1)S(1)} %copy.38, bf16[]{:T(256)} %constant.30.clone.1), padding=0_0x0_12x0_64 | pad | bytes 4334594 | tf_op jit(solution)/shard_map/jit(_pad)/pad | solution.py:303
  35.4 0.5 collective-permute-start.3
  35.9 7.5 %all-to-all-done.1.part_ref = bf16[4,16,2944]{2,1,0:T(8,128)(2,1)S(1)} async-done(((bf16[4,16,2944]{2,1,0:T(8,128)(2,1)}), bf16[4,16,2944]{2,1,0:T(8,128)(2,1)S(1)}, u32[]{:S(2)}, u32[]{:S(2)}) %all-to-all-start.1) | async-done | bytes 376864 | tf_op jit(solution)/shard_map/all_to_all | solution.py:308
  43.4 0.0 collective-permute-start.4
  43.4 0.0 copy-done.3
  43.4 0.8 norm.1
  44.2 0.0 collective-permute-done.2.g1_hbm
  44.2 0.0 collective-permute-done.3.u1_hbm
  44.2 3.8 %collective-permute-done.4.d1_hbm = bf16[384,2944]{1,0:T(8,128)(2,1)S(1)} collective-permute-done((bf16[384,2944]{1,0:T(8,128)(2,1)}, bf16[384,2944]{1,0:T(8,128)(2,1)S(1)}, u32[]{:S(2)}, u32[]{:S(2)}) %collective-permute-start.4) | collective-permute-done | bytes 2261024 | tf_op jit(solution)/shard_map/ppermute | solution.py:364
  48.0 28.1 %all_to_all.25 = bf16[16,16,2944]{2,1,0:T(8,128)(2,1)S(1)} all-to-all(bf16[16,16,2944]{2,1,0:T(8,128)(2,1)S(1)} %get-tuple-element.47), channel_id=1, replica_groups=mesh['x'=4,'y'=4,'w'=4,'v'=2,'c'=2] {'x','y'}, dimensions={0} | all-to-all | bytes 3014656 | tf_op jit(solution)/shard_map/all_to_all | solution.py:308
  76.1 7.9 %experts.1 = bf16[256,2880]{1,0:T(8,128)(2,1)S(1)} custom-call(s32[2]{0:T(128)S(1)} %get-tuple-element.42.first_ref, bf16[256,2944]{1,0:T(8,128)(2,1)S(1)} %bitcast.14, bf16[384,2944]{1,0:T(8,128)(2,1)} %bitcast.17, bf16[384,2944]{1,0:T(8,128)(2,1)} %bitcast.8.u0_hbm, bf16[384,2944]{1,0:T(8,128)(2,1)} %collective-permute-done.2.g1_hbm, ...), custom_call_target="tpu_custom_call" | custom-call | tf_op jit(solution)/shard_map/experts/pallas_call | solution.py:284
  84.1 24.5 %all_to_all.26 = bf16[16,16,2880]{2,1,0:T(8,128)(2,1)S(1)} all-to-all(bf16[16,16,2880]{2,1,0:T(8,128)(2,1)S(1)} %bitcast.15), channel_id=1, replica_groups=mesh['x'=4,'y'=4,'w'=4,'v'=2,'c'=2] {'x','y'}, dimensions={0} | all-to-all | bytes 2949120 | tf_op jit(solution)/shard_map/all_to_all | solution.py:308
  108.6 0.2 reduce_sum.21
  108.8 11.8 %all_to_all.27 = bf16[8,2,2880]{2,1,0:T(2,128)(2,1)S(1)} all-to-all(bf16[8,2,2880]{2,1,0:T(2,128)(2,1)S(1)} %reshape.26), channel_id=1, replica_groups=mesh['x'=4,'y'=4,'w'=4,'v'=2,'c'=2] {'w','v'}, dimensions={0} | all-to-all | bytes 184320 | tf_op jit(solution)/shard_map/all_to_all | solution.py:308
  120.7 0.1 convert_reduce_fusion
  120.7 0.6 fusion
  (2 shorter events, 0.0 us)
Async XLA Ops:
  0.0 19.7 %collective-permute-start = (bf16[2880,256]{1,0:T(8,128)(2,1)}, bf16[2880,256]{1,0:T(8,128)(2,1)}, u32[]{:S(2)}, u32[]{:S(2)}) collective-permute-start(bf16[2880,256]{1,0:T(8,128)(2,1)} %bitcast.22), channel_id=1, source_target_pairs={{0,1},{1,0},{2,3},{3,2},{4,5},{5,4},{6,7},{7,6},{8,9},{9,8},{10,11... | collective-permute-start | bytes 4423688 | tf_op jit(solution)/shard_map/ppermute | solution.py:337
  3.4 16.3 %all-to-all-start = ((bf16[8,2,512]{2,1,0:T(2,128)(2,1)}), bf16[8,2,512]{2,1,0:T(2,128)(2,1)S(1)}, u32[]{:S(2)}, u32[]{:S(2)}) async-start(bf16[8,2,512]{2,1,0:T(2,128)(2,1)} %attend.1), calls=%async_computation | async-start | bytes 32768 | tf_op jit(solution)/shard_map/all_to_all | solution.py:308
  14.7 5.0 %copy-start = (bf16[1,2,2880]{2,1,0:T(2,128)(2,1)S(1)}, bf16[1,2,2880]{2,1,0:T(2,128)(2,1)}, u32[]{:S(2)}) copy-start(bf16[1,2,2880]{2,1,0:T(2,128)(2,1)} %hid_ref.1) | copy-start | bytes 34564
  14.8 17.0 %copy-start.1 = (bf16[2,192,2944]{2,1,0:T(8,128)(2,1)}, bf16[2,192,2944]{2,1,0:T(8,128)(2,1)S(1)}, u32[]{:S(2)}) copy-start(bf16[2,192,2944]{2,1,0:T(8,128)(2,1)S(1)} %pad.14.clone) | copy-start | bytes 6782980
  19.7 4.0 %copy-start.2 = (bf16[2,2880,180]{1,0,2:T(2,128)(2,1)S(1)}, bf16[2,2880,180]{1,0,2:T(2,128)(2,1)}, u32[]{:S(2)}) copy-start(bf16[2,2880,180]{1,0,2:T(2,128)(2,1)} %param.26) | copy-start | bytes 6220804
  23.0 4.7 %collective-permute-start.1 = (bf16[16,2944]{1,0:T(8,128)(2,1)S(1)}, bf16[16,2944]{1,0:T(8,128)(2,1)S(1)}, u32[]{:S(2)}, u32[]{:S(2)}) collective-permute-start(bf16[16,2944]{1,0:T(8,128)(2,1)S(1)} %get-tuple-element.35), channel_id=1, source_target_pairs={{0,2},{2,0},{1,3},{3,1},{4,6},{6,4},{5,7},{7,5},{8,10},{10,8},{9,1... | collective-permute-start | bytes 282632 | tf_op jit(solution)/shard_map/ppermute | solution.py:355
  28.4 15.0 %all-to-all-start.1 = ((bf16[4,16,2944]{2,1,0:T(8,128)(2,1)}), bf16[4,16,2944]{2,1,0:T(8,128)(2,1)S(1)}, u32[]{:S(2)}, u32[]{:S(2)}) async-start(bf16[4,16,2944]{2,1,0:T(8,128)(2,1)} %pair.1), calls=%async_computation.1 | async-start | bytes 753664 | tf_op jit(solution)/shard_map/all_to_all | solution.py:308
  31.9 12.3 %collective-permute-start.2 = (bf16[384,2944]{1,0:T(8,128)(2,1)S(1)}, bf16[384,2944]{1,0:T(8,128)(2,1)}, u32[]{:S(2)}, u32[]{:S(2)}) collective-permute-start(bf16[384,2944]{1,0:T(8,128)(2,1)S(1)} %bitcast.16), channel_id=1, source_target_pairs={{0,1},{1,0},{2,3},{3,2},{4,5},{5,4},{6,7},{7,6},{8,9},{9,8},{10,11... | collective-permute-start | bytes 6782984 | tf_op jit(solution)/shard_map/ppermute | solution.py:352
  33.8 9.6 %copy-start.3 = (f32[2880]{0:T(1024)S(1)}, f32[2880]{0:T(1024)}, u32[]{:S(2)}) copy-start(f32[2880]{0:T(1024)} %param.22) | copy-start | bytes 34564
  35.4 8.9 %collective-permute-start.3 = (bf16[384,2944]{1,0:T(8,128)(2,1)}, bf16[384,2944]{1,0:T(8,128)(2,1)}, u32[]{:S(2)}, u32[]{:S(2)}) collective-permute-start(bf16[384,2944]{1,0:T(8,128)(2,1)} %bitcast.8.u0_hbm), channel_id=1, source_target_pairs={{0,1},{1,0},{2,3},{3,2},{4,5},{5,4},{6,7},{7,6},{8,9},{9,8},{10,11... | collective-permute-start | bytes 6782984 | tf_op jit(solution)/shard_map/ppermute | solution.py:358
  43.4 4.6 %collective-permute-start.4 = (bf16[384,2944]{1,0:T(8,128)(2,1)}, bf16[384,2944]{1,0:T(8,128)(2,1)S(1)}, u32[]{:S(2)}, u32[]{:S(2)}) collective-permute-start(bf16[384,2944]{1,0:T(8,128)(2,1)} %bitcast.18), channel_id=1, source_target_pairs={{0,1},{1,0},{2,3},{3,2},{4,5},{5,4},{6,7},{7,6},{8,9},{9,8},{10,11... | collective-permute-start | bytes 6782984 | tf_op jit(solution)/shard_map/ppermute | solution.py:364

commit v4 on v3

--- a/solution.py
+++ b/solution.py
@@ -3,6 +3,7 @@
 from jax import lax
 from jax.experimental import pallas as pl
 from jax.experimental.pallas import tpu as pltpu
+from jax.experimental.layout import Layout, with_layout_constraint
 from jax.sharding import Mesh
 from jax.sharding import PartitionSpec as P
 
@@ -234,74 +235,74 @@
 
 def experts_kernel(
     first_ref, x_ref, g0_hbm, u0_hbm, g1_hbm, u1_hbm, d0_hbm, d1_hbm, out_ref,
-    w_ref, d_ref, act_ref, sems,
+    g0, u0, g1, u1, d0, d1, sems,
 ):
-    rows, wide = g0_hbm.shape
-    width = out_ref.shape[1]
-    part = rows // 2
     pairs = (
-        (g0_hbm, w_ref.at[0, pl.ds(0, rows)]), (u0_hbm, w_ref.at[0, pl.ds(rows, rows)]),
-        (g1_hbm, w_ref.at[1, pl.ds(0, rows)]), (u1_hbm, w_ref.at[1, pl.ds(rows, rows)]),
-        (d0_hbm, d_ref.at[pl.ds(0, rows)]), (d1_hbm, d_ref.at[pl.ds(rows, rows)]),
-    )
-    copies = [pltpu.make_async_copy(a, b, sems.at[i]) for i, (a, b) in enumerate(pairs)]
-    for copy in copies:
-        copy.start()
-    x = x_ref[...]
+        (g0_hbm, g0), (u0_hbm, u0), (g1_hbm, g1), (u1_hbm, u1), (d0_hbm, d0), (d1_hbm, d1),
+    )
+    per, _, width = g0.shape
+    copies = []
+    for i, (a, b) in enumerate(pairs):
+        copies.append(
+            [pltpu.make_async_copy(a.at[e], b.at[e], sems.at[i, e]) for e in range(per)]
+        )
+    for side in (0, 2):
+        for e in range(per):
+            copies[side][e].start()
+            copies[side + 1][e].start()
+    for i in (4, 5):
+        for e in range(per):
+            copies[i][e].start()
+    x = x_ref[:, :width]
     route = x_ref[:, width : width + 8].astype(F32)
     ids = route[:, 0:4]
     expo = jnp.exp(route[:, 4:8])
     total = jnp.sum(expo, axis=1, keepdims=True)
-    column = lax.broadcasted_iota(jnp.int32, (x.shape[0], rows), 1)
     dims = (((1,), (1,)), ((), ()))
-    for side in range(2):
-        shares = []
-        for e in range(2):
+    acts = []
+    for side, (g_ref, u_ref) in enumerate(((g0, u0), (g1, u1))):
+        for e in range(per):
+            copies[2 * side][e].wait()
+            gate = lax.dot_general(x, g_ref[e], dims, preferred_element_type=F32)
+            copies[2 * side + 1][e].wait()
+            up = lax.dot_general(x, u_ref[e], dims, preferred_element_type=F32)
+            act = gate * jax.nn.sigmoid(1.702 * gate) * (up + 1.0)
             label = (first_ref[side] + e).astype(F32)
-            shares.append(
-                jnp.sum(jnp.where(ids == label, expo, 0.0), axis=1, keepdims=True) / total
-            )
-        share = jnp.where(column < part, shares[0], shares[1])
-        copies[2 * side].wait()
-        copies[2 * side + 1].wait()
-        both = lax.dot_general(x, w_ref[side], dims, preferred_element_type=F32)
-        gate, up = both[:, :rows], both[:, rows:]
-        act = gate * jax.nn.sigmoid(1.702 * gate) * (up + 1.0)
-        act_ref[:, side * rows : (side + 1) * rows] = (act * share).astype(BF16)
-    copies[4].wait()
-    copies[5].wait()
+            share = jnp.sum(jnp.where(ids == label, expo, 0.0), axis=1, keepdims=True) / total
+            acts.append((act * share).astype(BF16))
+    for i in (4, 5):
+        for e in range(per):
+            copies[i][e].wait()
     chunk = 768
     for start in range(0, width, chunk):
         stop = min(start + chunk, width)
-        out_ref[:, start:stop] = jnp.dot(
-            act_ref[...], d_ref[:, start:stop], preferred_element_type=F32
-        ).astype(BF16)
-
-
-def experts(first, x, own, other, width):
-    rows, wide = own[0].shape
+        part = None
+        for side, d_ref in enumerate((d0, d1)):
+            for e in range(per):
+                piece = jnp.dot(
+                    acts[side * per + e], d_ref[e, :, start:stop], preferred_element_type=F32
+                )
+                part = piece if part is None else part + piece
+        out_ref[:, start:stop] = part.astype(BF16)
+
+
+def experts(first, x, own, other):
+    width = own[0].shape[2]
     args = (own[0], own[1], other[0], other[1], own[2], other[2])
     return pl.pallas_call(
         experts_kernel,
         in_specs=[smem(), vmem()] + [hbm()] * 6,
         out_specs=vmem(),
         out_shape=jax.ShapeDtypeStruct((x.shape[0], width), BF16),
-        scratch_shapes=[
-            pltpu.VMEM((2, 2 * rows, wide), BF16),
-            pltpu.VMEM((2 * rows, wide), BF16),
-            pltpu.VMEM((x.shape[0], 2 * rows), BF16),
-            pltpu.SemaphoreType.DMA((len(args),)),
-        ],
+        scratch_shapes=[pltpu.VMEM(a.shape, BF16) for a in args]
+        + [pltpu.SemaphoreType.DMA((len(args), own[0].shape[0]))],
         compiler_params=params(32),
         name="experts",
-    )(first, x, *stay(*args[:-1]), args[-1])
-
-
-def stacked(value):
-    per, rows, width = value.shape
-    high, wide = rows + -rows % 64, width + -width % 128
-    value = jnp.pad(value, ((0, 0), (0, high - rows), (0, wide - width)))
-    return value.reshape(per * high, wide)
+    )(first, x, *stay(*args))
+
+
+def row_major(value):
+    return with_layout_constraint(value, Layout(major_to_minor=tuple(range(value.ndim))))
 
 
 def exchange(value, axis):
@@ -335,39 +336,34 @@
     per = gate_weight.shape[0]
     out_rows = out_weight.T
     other_out = lax.ppermute(out_rows, "c", SWAP)
+    weights = [gate_weight, up_weight, down_weight]
+    weights += [lax.ppermute(w, "c", SWAP) for w in weights]
     attended = attend(
         prompt_lengths, queries, new_keys, new_values, key_cache, value_cache, nz
     )
-    attended, gate = lax.optimization_barrier((attended, gate_weight))
     ids = lax.dynamic_index_in_dim(expert_ids, d, 0, False).astype(F32)
     logits = lax.dynamic_index_in_dim(top_logits, d, 0, False).astype(F32)
     route = jnp.pad(jnp.concatenate([ids, logits], axis=1), ((0, 0), (0, 56)))
     place = jnp.stack([z, c]).astype(jnp.int32)
     first = jnp.stack([(2 * z + c) * per, (2 * z + 1 - c) * per]).astype(jnp.int32)
+    gain = norm_gain[None]
+    attended, route, place, first, gain = lax.optimization_barrier(
+        (attended, route, place, first, gain)
+    )
     by_heads = exchange(attended, zaxis)
-    gate = stacked(gate.swapaxes(1, 2))
-    by_heads, gate, route, place, first = lax.optimization_barrier(
-        (by_heads, gate, route, place, first)
-    )
-    far_gate = lax.ppermute(gate, "c", SWAP)
     keep, sent = project(place, by_heads, hidden_in, route, out_rows, other_out)
-    sent, up = lax.optimization_barrier((sent, up_weight))
     got = lax.ppermute(sent, "v", SWAP)
-    up = stacked(up.swapaxes(1, 2))
-    got, up = lax.optimization_barrier((got, up))
-    far_up = lax.ppermute(up, "c", SWAP)
     quads = pair(keep, got, nz // 2)
-    quads, down = lax.optimization_barrier((quads, down_weight))
     parts = exchange(quads, "w")
-    down = stacked(down)
-    parts, down = lax.optimization_barrier((parts, down))
-    far_down = lax.ppermute(down, "c", SWAP)
-    residual, copies = norm(place, parts, norm_gain[None], ndp, steps)
-    copies, far_gate, far_up, far_down = lax.optimization_barrier(
-        (copies, far_gate, far_up, far_down)
-    )
-    tokens = exchange(copies, dp).reshape(ndp * nz * steps, -1)
-    made = experts(first, tokens, (gate, up, down), (far_gate, far_up, far_down), width)
+    residual, copies = norm(place, parts, gain, ndp, steps)
+    copies, *weights = lax.optimization_barrier((copies, *weights))
+    tokens = exchange(copies, dp)
+    relaid = [
+        row_major(w if i % 3 == 2 else w.swapaxes(1, 2)) for i, w in enumerate(weights)
+    ]
+    tokens, *relaid = lax.optimization_barrier((tokens, *relaid))
+    tokens = tokens.reshape(ndp * nz * steps, -1)
+    made = experts(first, tokens, relaid[:3], relaid[3:])
     back = exchange(made.reshape(ndp, nz * steps, width), dp)
     column_sum = jnp.sum(back.astype(F32), axis=0).astype(BF16)
     final = exchange(column_sum.reshape(nz, steps, width), zaxis)

time: 122 us -> 120 us (0.984)
  waiting for transfers between devices: 18.4 us -> 5.24 us
  local copies, waits for them, and re-layouts: 7.13 us -> 18.9 us
  starting transfers between devices: 13.2 us -> 9.12 us
  Pallas kernels: 15.5 us -> 18.8 us
    optimization_barrier x0 -> x6, local copies, waits for them, and re-layouts: none -> 14.5 us  [on_device(): copies, *weights = lax.optimization_barrier((copies, *weights))]
    all_to_all x2 -> x1, waiting for transfers between devices: 12.3 us -> 1.27 us  [exchange(): return lax.all_to_all(value, axis, split_axis=0, concat_axis=0, tiled=True)]
    all_to_all x2 -> x1, starting transfers between devices: 11.9 us -> 7.4 us  [exchange(): return lax.all_to_all(value, axis, split_axis=0, concat_axis=0, tiled=True)]
    ppermute x3, waiting for transfers between devices: 3.76 us -> 0.01 us  [on_device(): weights += [lax.ppermute(w, 'c', SWAP) for w in weights]]
    pallas_call x1, Pallas kernels: 7.95 us -> 11.5 us  [experts(): pl.pallas_call(experts_kernel, in_specs=[smem(), vmem()] + [hbm()] * 6, o...]
    pad x3 -> x0, local copies, waits for them, and re-layouts: 3.21 us -> none  [stacked(): value = jnp.pad(value, ((0, 0), (0, high - rows), (0, wide - width)))]
    ppermute x1, waiting for transfers between devices: 2.28 us -> 3.96 us  [on_device(): got = lax.ppermute(sent, 'v', SWAP)]
    all_to_all x3 -> x4, blocking collectives: 64.5 us -> 64.7 us  [exchange(): return lax.all_to_all(value, axis, split_axis=0, concat_axis=0, tiled=True)]
  transfers between devices with their start and end apart: 7 -> 6, of which waited for: 4 -> 2; matrix products, arithmetic and copies ran while one was open for 7% -> 14% of each run, Pallas kernels for 3% -> 6%
where the time goes in v4:
time: 120 us; the launch traced here: 119 us
  blocking collectives  64.7 us (54%)
  local copies, waits for them, and re-layouts  18.9 us (16%)
  Pallas kernels  18.8 us (16%)
  starting transfers between devices  9.12 us (8%)
  waiting for transfers between devices  5.24 us (4%)
  other arithmetic  1.91 us (2%)
    all_to_all x4, blocking collectives, exchange(): return lax.all_to_all(value, axis, split_axis=0, concat_axis=0, tiled=True)  64.7 us
    optimization_barrier x6, local copies, waits for them, and re-layouts, on_device(): copies, *weights = lax.optimization_barrier((copies, *weights))  14.5 us
    pallas_call x1, Pallas kernels, experts(): pl.pallas_call(experts_kernel, in_specs=[smem(), vmem()] + [hbm()] * 6, o...  11.5 us
    all_to_all x1, starting transfers between devices, exchange(): return lax.all_to_all(value, axis, split_axis=0, concat_axis=0, tiled=True)  7.4 us
    ppermute x1, waiting for transfers between devices, on_device(): got = lax.ppermute(sent, 'v', SWAP)  3.96 us
    unnamed x10, local copies, waits for them, and re-layouts  3.69 us
    pallas_call x1, Pallas kernels, project(): pl.pallas_call(project_kernel, in_specs=[smem(), vmem(), vmem(), vmem(),...  3.2 us
  transfers between devices with their start and end apart: 6, of which 2 were waited for; matrix products, arithmetic and copies ran while one was open for 14% of the time, Pallas kernels for 6%

profile of v4, /device:TPU:8, one launch (start us, length us, event | category | flops | bytes accessed | tf_op | source)
XLA Modules:
  0.0 119.4 jit_solution(11502056181892676717)
XLA Ops:
  0.0 0.0 collective-permute-start
  0.0 0.5 collective-permute-start.2
  0.5 0.0 collective-permute-start.3
  0.5 0.5 collective-permute-start.4
  1.7 0.7 broadcast_in_dim.6.gain_ref
  2.4 2.1 %attend.1 = bf16[8,2,512]{2,1,0:T(2,128)(2,1)S(1)} custom-call(s32[1]{0:T(128)S(6)} %copy.69.len_ref, bf16[1,2,4096]{2,1,0:T(2,128)(2,1)} %q_hbm.1, bf16[1,2,512]{2,1,0:T(2,128)(2,1)} %nk_hbm.1, bf16[1,2,512]{2,1,0:T(2,128)(2,1)} %nv_hbm.1, bf16[1,512,512]{2,1,0:T(8,128)(2,1)} %k_hbm.1, bf16[1,512,512]{2,1,0:T(8,128)(2,1)} %v_hbm.1), custom_call_target="tpu_custom_call" | custom-call | tf_op jit(solution)/shard_map/attend/pallas_call | solution.py:102
  4.5 0.9 convert_reduce_fusion.1
  5.3 0.1 select_maximum_fusion.route_ref
  5.4 0.1 pad_add_fusion
  5.5 16.0 %all_to_all.25.x_ref = bf16[8,2,512]{2,1,0:T(2,128)(2,1)S(1)} all-to-all(bf16[8,2,512]{2,1,0:T(2,128)(2,1)S(1)} %attend.1), channel_id=1, replica_groups=mesh['x'=4,'y'=4,'w'=4,'v'=2,'c'=2] {'w','v'}, dimensions={0} | all-to-all | bytes 32768 | tf_op jit(solution)/shard_map/all_to_all | solution.py:309
  21.5 0.0 collective-permute-done.other_hbm
  21.5 0.0 copy-start
  21.5 0.7 copy-done
  22.2 3.2 %project.1 = (f32[16,2944]{1,0:T(8,128)S(1)}, bf16[16,2944]{1,0:T(8,128)(2,1)S(1)}) custom-call(s32[2]{0:T(128)S(1)} %get-tuple-element.28.place_ref, bf16[8,2,512]{2,1,0:T(2,128)(2,1)S(1)} %all_to_all.25.x_ref, bf16[1,2,2880]{2,1,0:T(2,128)(2,1)S(1)} %copy-done, f32[2,64]{1,0:T(2,128)S(1)} %select_maximum_fusion.route_ref, bf16[2880,256]{1,0:T(8,128)(2,1)} %bitcast.28, ...), custom_call_target="tpu_custom_call" | custom-call | tf_op jit(solution)/shard_map/project/pallas_call | solution.py:167
  25.4 0.7 collective-permute-start.1
  26.1 4.0 %collective-permute-done.1.got_ref = bf16[16,2944]{1,0:T(8,128)(2,1)S(1)} collective-permute-done((bf16[16,2944]{1,0:T(8,128)(2,1)S(1)}, bf16[16,2944]{1,0:T(8,128)(2,1)S(1)}, u32[]{:S(2)}, u32[]{:S(2)}) %collective-permute-start.1) | collective-permute-done | bytes 94240 | tf_op jit(solution)/shard_map/ppermute | solution.py:355
  30.1 13.3 %all_to_all.26.part_ref = bf16[4,16,2944]{2,1,0:T(8,128)(2,1)S(1)} all-to-all(bf16[4,16,2944]{2,1,0:T(8,128)(2,1)S(1)} %pair.1), channel_id=1, replica_groups=mesh['x'=4,'y'=4,'w'=4,'v'=2,'c'=2] {'w'}, dimensions={0} | all-to-all | bytes 753664 | tf_op jit(solution)/shard_map/all_to_all | solution.py:309
  43.4 2.0 %norm.1 = (f32[2,2880]{1,0:T(2,128)S(1)}, bf16[16,16,2944]{2,1,0:T(8,128)(2,1)}) custom-call(s32[2]{0:T(128)S(1)} %get-tuple-element.28.place_ref, bf16[4,16,2944]{2,1,0:T(8,128)(2,1)S(1)} %all_to_all.26.part_ref, f32[1,2880]{1,0:T(1,128)S(1)} %broadcast_in_dim.6.gain_ref), custom_call_target="tpu_custom_call" | custom-call | tf_op jit(solution)/shard_map/norm/pallas_call | solution.py:223
  45.3 0.0 collective-permute-done.2
  45.3 0.0 copy-start.3
  45.4 0.0 collective-permute-done.3
  45.4 0.0 collective-permute-done.4
  45.4 1.4 %copy-done.3 = bf16[2,2880,180]{1,0,2:T(2,128)(2,1)} copy-done((bf16[2,2880,180]{1,0,2:T(2,128)(2,1)}, bf16[2,2880,180]{1,0,2:T(2,128)(2,1)S(1)}, u32[]{:S(2)}) %copy-start.3) | copy-done | bytes 2073624
  46.7 7.4 %all-to-all-start.2 = ((bf16[16,16,2944]{2,1,0:T(8,128)(2,1)}), bf16[16,16,2944]{2,1,0:T(8,128)(2,1)S(1)}, u32[]{:S(2)}, u32[]{:S(2)}) async-start(bf16[16,16,2944]{2,1,0:T(8,128)(2,1)} %get-tuple-element.37), calls=%async_computation.2 | async-start | bytes 3014656 | tf_op jit(solution)/shard_map/all_to_all | solution.py:309
  54.1 0.0 copy-start.1
  54.1 3.3 %copy.68 = bf16[2,2880,180]{1,2,0:T(8,128)(2,1)} copy(bf16[2,2880,180]{1,0,2:T(2,128)(2,1)} %param.25) | data formatting | bytes 4147200 | tf_op jit(solution)/shard_map/optimization_barrier | solution.py:359
  57.5 0.0 copy-done.1
  57.5 0.0 copy-start.2
  57.5 1.6 %copy.67 = bf16[2,2880,180]{1,2,0:T(8,128)(2,1)} copy(bf16[2,2880,180]{1,0,2:T(2,128)(2,1)S(1)} %copy-done.1) | data formatting | bytes 4147200 | tf_op jit(solution)/shard_map/optimization_barrier | solution.py:359
  59.0 0.8 copy-done.2
  59.8 0.0 copy-start.4
  59.8 1.6 %copy.55.d0_hbm = bf16[2,180,2880]{2,1,0:T(8,128)(2,1)} copy(bf16[2,180,2880]{2,0,1:T(2,128)(2,1)S(1)} %copy-done.2) | data formatting | bytes 4147200 | tf_op jit(solution)/shard_map/optimization_barrier | solution.py:359
  61.4 0.8 copy-done.4
  62.2 1.6 %copy.66 = bf16[2,2880,180]{1,2,0:T(8,128)(2,1)} copy(bf16[2,2880,180]{1,0,2:T(2,128)(2,1)S(1)} %copy-done.4) | data formatting | bytes 4147200 | tf_op jit(solution)/shard_map/optimization_barrier | solution.py:359
  63.8 3.2 %copy.65 = bf16[2,2880,180]{1,2,0:T(8,128)(2,1)} copy(bf16[2,2880,180]{1,0,2:T(2,128)(2,1)} %collective-permute-done.3) | data formatting | bytes 4147200 | tf_op jit(solution)/shard_map/optimization_barrier | solution.py:359
  67.1 3.2 %copy.58.d1_hbm = bf16[2,180,2880]{2,1,0:T(8,128)(2,1)} copy(bf16[2,180,2880]{2,0,1:T(2,128)(2,1)} %collective-permute-done.4) | data formatting | bytes 4147200 | tf_op jit(solution)/shard_map/optimization_barrier | solution.py:359
  70.2 1.3 %all-to-all-done.2 = bf16[16,16,2944]{2,1,0:T(8,128)(2,1)S(1)} async-done(((bf16[16,16,2944]{2,1,0:T(8,128)(2,1)}), bf16[16,16,2944]{2,1,0:T(8,128)(2,1)S(1)}, u32[]{:S(2)}, u32[]{:S(2)}) %all-to-all-start.2) | async-done | bytes 1507360 | tf_op jit(solution)/shard_map/all_to_all | solution.py:309
  71.5 11.5 %experts.1 = bf16[256,2880]{1,0:T(8,128)(2,1)S(1)} custom-call(s32[2]{0:T(128)S(1)} %get-tuple-element.35.first_ref, bf16[256,2944]{1,0:T(8,128)(2,1)S(1)} %bitcast.21, bf16[2,180,2880]{2,1,0:T(8,128)(2,1)} %bitcast.23, bf16[2,180,2880]{2,1,0:T(8,128)(2,1)} %bitcast.24, bf16[2,180,2880]{2,1,0:T(8,128)(2,1)} %bitcast.25, bf16[2,180,2880]{2,1,0:T(8,128)(2,1)} %bitcast.26, ...), custom_call_target="tpu_custom_call" | custom-call | tf_op jit(solution)/shard_map/experts/pallas_call | solution.py:292
  83.1 22.7 %all_to_all.27 = bf16[16,16,2880]{2,1,0:T(8,128)(2,1)S(1)} all-to-all(bf16[16,16,2880]{2,1,0:T(8,128)(2,1)S(1)} %bitcast.22), channel_id=1, replica_groups=mesh['x'=4,'y'=4,'w'=4,'v'=2,'c'=2] {'x','y'}, dimensions={0} | all-to-all | bytes 2949120 | tf_op jit(solution)/shard_map/all_to_all | solution.py:309
  105.8 0.2 reduce_sum.21
  106.1 12.7 %all_to_all.28 = bf16[8,2,2880]{2,1,0:T(2,128)(2,1)S(1)} all-to-all(bf16[8,2,2880]{2,1,0:T(2,128)(2,1)S(1)} %reshape.14), channel_id=1, replica_groups=mesh['x'=4,'y'=4,'w'=4,'v'=2,'c'=2] {'w','v'}, dimensions={0} | all-to-all | bytes 184320 | tf_op jit(solution)/shard_map/all_to_all | solution.py:309
  118.7 0.1 convert_reduce_fusion
  118.8 0.6 fusion
  (2 shorter events, 0.1 us)
Async XLA Ops:
  0.0 21.5 %collective-permute-start = (bf16[2880,256]{1,0:T(8,128)(2,1)}, bf16[2880,256]{1,0:T(8,128)(2,1)}, u32[]{:S(2)}, u32[]{:S(2)}) collective-permute-start(bf16[2880,256]{1,0:T(8,128)(2,1)} %bitcast.27), channel_id=1, source_target_pairs={{0,1},{1,0},{2,3},{3,2},{4,5},{5,4},{6,7},{7,6},{8,9},{9,8},{10,11... | collective-permute-start | bytes 4423688 | tf_op jit(solution)/shard_map/ppermute | solution.py:338
  0.0 45.3 %collective-permute-start.2 = (bf16[2,2880,180]{1,0,2:T(2,128)(2,1)}, bf16[2,2880,180]{1,0,2:T(2,128)(2,1)S(1)}, u32[]{:S(2)}, u32[]{:S(2)}) collective-permute-start(bf16[2,2880,180]{1,0,2:T(2,128)(2,1)} %param.25), channel_id=1, source_target_pairs={{0,1},{1,0},{2,3},{3,2},{4,5},{5,4},{6,7},{7,6},{8,9},{9,8},{10,11... | collective-permute-start | bytes 6220808 | tf_op jit(solution)/shard_map/ppermute | solution.py:340
  0.5 44.8 %collective-permute-start.3 = (bf16[2,2880,180]{1,0,2:T(2,128)(2,1)}, bf16[2,2880,180]{1,0,2:T(2,128)(2,1)}, u32[]{:S(2)}, u32[]{:S(2)}) collective-permute-start(bf16[2,2880,180]{1,0,2:T(2,128)(2,1)} %param.26), channel_id=1, source_target_pairs={{0,1},{1,0},{2,3},{3,2},{4,5},{5,4},{6,7},{7,6},{8,9},{9,8},{10,11... | collective-permute-start | bytes 6220808 | tf_op jit(solution)/shard_map/ppermute | solution.py:340
  0.5 44.8 %collective-permute-start.4 = (bf16[2,180,2880]{2,0,1:T(2,128)(2,1)}, bf16[2,180,2880]{2,0,1:T(2,128)(2,1)}, u32[]{:S(2)}, u32[]{:S(2)}) collective-permute-start(bf16[2,180,2880]{2,0,1:T(2,128)(2,1)} %param.27), channel_id=1, source_target_pairs={{0,1},{1,0},{2,3},{3,2},{4,5},{5,4},{6,7},{7,6},{8,9},{9,8},{10,11... | collective-permute-start | bytes 6220808 | tf_op jit(solution)/shard_map/ppermute | solution.py:340
  21.5 0.7 copy-start
  25.4 4.7 %collective-permute-start.1 = (bf16[16,2944]{1,0:T(8,128)(2,1)S(1)}, bf16[16,2944]{1,0:T(8,128)(2,1)S(1)}, u32[]{:S(2)}, u32[]{:S(2)}) collective-permute-start(bf16[16,2944]{1,0:T(8,128)(2,1)S(1)} %get-tuple-element.32), channel_id=1, source_target_pairs={{0,2},{2,0},{1,3},{3,1},{4,6},{6,4},{5,7},{7,5},{8,10},{10,8},{9,1... | collective-permute-start | bytes 282632 | tf_op jit(solution)/shard_map/ppermute | solution.py:355
  45.3 1.4 %copy-start.3 = (bf16[2,2880,180]{1,0,2:T(2,128)(2,1)}, bf16[2,2880,180]{1,0,2:T(2,128)(2,1)S(1)}, u32[]{:S(2)}) copy-start(bf16[2,2880,180]{1,0,2:T(2,128)(2,1)S(1)} %collective-permute-done.2) | copy-start | bytes 6220804
  46.7 24.8 %all-to-all-start.2 = ((bf16[16,16,2944]{2,1,0:T(8,128)(2,1)}), bf16[16,16,2944]{2,1,0:T(8,128)(2,1)S(1)}, u32[]{:S(2)}, u32[]{:S(2)}) async-start(bf16[16,16,2944]{2,1,0:T(8,128)(2,1)} %get-tuple-element.37), calls=%async_computation.2 | async-start | bytes 3014656 | tf_op jit(solution)/shard_map/all_to_all | solution.py:309
  54.1 3.3 %copy-start.1 = (bf16[2,2880,180]{1,0,2:T(2,128)(2,1)S(1)}, bf16[2,2880,180]{1,0,2:T(2,128)(2,1)}, u32[]{:S(2)}) copy-start(bf16[2,2880,180]{1,0,2:T(2,128)(2,1)} %param.26) | copy-start | bytes 6220804
  57.5 2.4 %copy-start.2 = (bf16[2,180,2880]{2,0,1:T(2,128)(2,1)S(1)}, bf16[2,180,2880]{2,0,1:T(2,128)(2,1)}, u32[]{:S(2)}) copy-start(bf16[2,180,2880]{2,0,1:T(2,128)(2,1)} %param.27) | copy-start | bytes 6220804
  59.8 2.4 %copy-start.4 = (bf16[2,2880,180]{1,0,2:T(2,128)(2,1)S(1)}, bf16[2,2880,180]{1,0,2:T(2,128)(2,1)}, u32[]{:S(2)}) copy-start(bf16[2,2880,180]{1,0,2:T(2,128)(2,1)} %copy-done.3) | copy-start | bytes 6220804

commit v5 on v4

--- a/solution.py
+++ b/solution.py
@@ -116,23 +116,31 @@
 
 
 def project_kernel(
-    place_ref, x_ref, hid_ref, route_ref, own_hbm, other_hbm, keep_ref, send_ref,
-    rows_ref, own_ref, other_ref, sems,
+    place_ref, x_ref, hid_hbm, ids_hbm, logits_hbm, own_hbm, other_hbm, keep_ref, send_ref,
+    rows_ref, hid_ref, ids_ref, logits_ref, own_ref, other_ref, sems,
 ):
     width, feats = own_ref.shape
     chunk = 640
     cuts = [(start, min(start + chunk, width)) for start in range(0, width, chunk)]
+    small = [
+        pltpu.make_async_copy(hid_hbm, hid_ref, sems.at[0]),
+        pltpu.make_async_copy(ids_hbm, ids_ref, sems.at[1]),
+        pltpu.make_async_copy(logits_hbm, logits_ref, sems.at[2]),
+    ]
     copies = []
     for i, (start, stop) in enumerate(cuts):
         span = pl.ds(start, stop - start)
         copies.append(
             (
-                pltpu.make_async_copy(own_hbm.at[span], own_ref.at[span], sems.at[2 * i]),
-                pltpu.make_async_copy(other_hbm.at[span], other_ref.at[span], sems.at[2 * i + 1]),
+                pltpu.make_async_copy(own_hbm.at[span], own_ref.at[span], sems.at[2 * i + 3]),
+                pltpu.make_async_copy(other_hbm.at[span], other_ref.at[span], sems.at[2 * i + 4]),
             )
         )
-        copies[-1][0].start()
-        copies[-1][1].start()
+    for copy in small:
+        copy.start()
+    for pair_copies in copies:
+        pair_copies[0].start()
+        pair_copies[1].start()
     blocks, steps, _ = x_ref.shape
     for i in range(blocks):
         rows_ref[i * steps : (i + 1) * steps, :] = x_ref[i].astype(F32)
@@ -141,7 +149,27 @@
     first = place_ref[1] == 0
     mine = jnp.where(first, low, high)
     theirs = jnp.where(first, high, low)
-    extra = jnp.concatenate([hid_ref[0].astype(F32), route_ref[...]], axis=1)
+    for copy in small:
+        copy.wait()
+    spare = keep_ref.shape[1] - width
+    lane = lax.broadcasted_iota(jnp.int32, (1, spare), 1)
+    routes = []
+    for ref in (ids_ref, logits_ref):
+        held = ref[...].astype(F32)
+        row = lax.broadcasted_iota(jnp.int32, held.shape, 2)
+        routes.append(
+            jnp.sum(jnp.where(row == place_ref[2], held, 0.0), axis=2, keepdims=True)
+        )
+    top = routes[0].shape[1]
+    lines = []
+    for s in range(steps):
+        line = jnp.zeros((1, spare), F32)
+        for i, values in enumerate(routes):
+            for k in range(top):
+                line = jnp.where(lane == i * top + k, values[s, k : k + 1, :], line)
+        lines.append(line)
+    route = jnp.concatenate(lines, axis=0)
+    extra = jnp.concatenate([hid_ref[0].astype(F32), route], axis=1)
     extra = jnp.concatenate([extra] * blocks, axis=0)
     block = lax.broadcasted_iota(jnp.int32, extra.shape, 0) // steps
     extra = jnp.where(block == place_ref[0], extra, 0.0)
@@ -160,13 +188,13 @@
     send_ref[:, width:] = extra[:, width:].astype(BF16)
 
 
-def project(place, x, hidden, route, own, other):
+def project(place, x, hidden, ids, logits, own, other):
     blocks, steps, feats = x.shape
-    wide = own.shape[0] + route.shape[1]
+    wide = own.shape[0] + -own.shape[0] % 128
     rows = blocks * steps
     return pl.pallas_call(
         project_kernel,
-        in_specs=[smem(), vmem(), vmem(), vmem(), hbm(), hbm()],
+        in_specs=[smem(), vmem()] + [hbm()] * 5,
         out_specs=[vmem(), vmem()],
         out_shape=[
             jax.ShapeDtypeStruct((rows, wide), F32),
@@ -174,13 +202,16 @@
         ],
         scratch_shapes=[
             pltpu.VMEM((rows, feats), F32),
+            pltpu.VMEM(hidden.shape, BF16),
+            pltpu.VMEM(ids.shape, jnp.int32),
+            pltpu.VMEM(logits.shape, BF16),
             pltpu.VMEM(own.shape, BF16),
             pltpu.VMEM(own.shape, BF16),
-            pltpu.SemaphoreType.DMA((2 * pl.cdiv(own.shape[0], 640),)),
+            pltpu.SemaphoreType.DMA((2 * pl.cdiv(own.shape[0], 640) + 3,)),
         ],
         compiler_params=params(12),
         name="project",
-    )(place, x, hidden, route, *stay(own, other))
+    )(place, x, *stay(hidden, ids, logits, own), other)
 
 
 def pair_kernel(keep_ref, got_ref, out_ref):
@@ -200,21 +231,27 @@
     )(keep, got)
 
 
-def norm_kernel(place_ref, part_ref, gain_ref, res_ref, out_ref):
+def norm_kernel(place_ref, part_ref, gain_ref, res_ref, out_hbm, full_ref, sems):
     steps, width = res_ref.shape
     total = part_ref[0].astype(F32)
     for i in range(1, part_ref.shape[0]):
         total = total + part_ref[i].astype(F32)
     res = total[:, :width]
+    scale = lax.rsqrt(jnp.sum(res * res, axis=1, keepdims=True) / width + 1e-05)
+    normed = (res * scale * gain_ref[...]).astype(BF16)
+    full_ref[...] = jnp.concatenate([normed.astype(F32), total[:, width:]], axis=1).astype(BF16)
+    copies = [
+        pltpu.make_async_copy(full_ref, out_hbm.at[i], sems.at[i])
+        for i in range(out_hbm.shape[0])
+    ]
+    for copy in copies:
+        copy.start()
     own = jnp.zeros((steps, width), F32)
     for i in range(res.shape[0] // steps):
         own = own + jnp.where(place_ref[0] == i, res[i * steps : (i + 1) * steps, :], 0.0)
     res_ref[...] = own
-    scale = lax.rsqrt(jnp.sum(res * res, axis=1, keepdims=True) / width + 1e-05)
-    normed = (res * scale * gain_ref[...]).astype(BF16)
-    full = jnp.concatenate([normed.astype(F32), total[:, width:]], axis=1).astype(BF16)
-    for i in range(out_ref.shape[0]):
-        out_ref[i] = full
+    for copy in copies:
+        copy.wait()
 
 
 def norm(place, parts, gain, copies, steps):
@@ -223,11 +260,12 @@
     return pl.pallas_call(
         norm_kernel,
         in_specs=[smem(), vmem(), vmem()],
-        out_specs=[vmem(), vmem()],
+        out_specs=[vmem(), hbm()],
         out_shape=[
             jax.ShapeDtypeStruct((steps, width), F32),
             jax.ShapeDtypeStruct((copies, rows, wide), BF16),
         ],
+        scratch_shapes=[pltpu.VMEM((rows, wide), BF16), pltpu.SemaphoreType.DMA((copies,))],
         compiler_params=params(12),
         name="norm",
     )(place, parts, gain)
@@ -241,18 +279,9 @@
         (g0_hbm, g0), (u0_hbm, u0), (g1_hbm, g1), (u1_hbm, u1), (d0_hbm, d0), (d1_hbm, d1),
     )
     per, _, width = g0.shape
-    copies = []
-    for i, (a, b) in enumerate(pairs):
-        copies.append(
-            [pltpu.make_async_copy(a.at[e], b.at[e], sems.at[i, e]) for e in range(per)]
-        )
-    for side in (0, 2):
-        for e in range(per):
-            copies[side][e].start()
-            copies[side + 1][e].start()
-    for i in (4, 5):
-        for e in range(per):
-            copies[i][e].start()
+    copies = [pltpu.make_async_copy(a, b, sems.at[i]) for i, (a, b) in enumerate(pairs)]
+    for copy in copies:
+        copy.start()
     x = x_ref[:, :width]
     route = x_ref[:, width : width + 8].astype(F32)
     ids = route[:, 0:4]
@@ -261,18 +290,20 @@
     dims = (((1,), (1,)), ((), ()))
     acts = []
     for side, (g_ref, u_ref) in enumerate(((g0, u0), (g1, u1))):
+        copies[2 * side].wait()
+        gates = [
+            lax.dot_general(x, g_ref[e], dims, preferred_element_type=F32) for e in range(per)
+        ]
+        copies[2 * side + 1].wait()
         for e in range(per):
-            copies[2 * side][e].wait()
-            gate = lax.dot_general(x, g_ref[e], dims, preferred_element_type=F32)
-            copies[2 * side + 1][e].wait()
+            gate = gates[e]
             up = lax.dot_general(x, u_ref[e], dims, preferred_element_type=F32)
             act = gate * jax.nn.sigmoid(1.702 * gate) * (up + 1.0)
             label = (first_ref[side] + e).astype(F32)
             share = jnp.sum(jnp.where(ids == label, expo, 0.0), axis=1, keepdims=True) / total
             acts.append((act * share).astype(BF16))
-    for i in (4, 5):
-        for e in range(per):
-            copies[i][e].wait()
+    copies[4].wait()
+    copies[5].wait()
     chunk = 768
     for start in range(0, width, chunk):
         stop = min(start + chunk, width)
@@ -295,7 +326,7 @@
         out_specs=vmem(),
         out_shape=jax.ShapeDtypeStruct((x.shape[0], width), BF16),
         scratch_shapes=[pltpu.VMEM(a.shape, BF16) for a in args]
-        + [pltpu.SemaphoreType.DMA((len(args), own[0].shape[0]))],
+        + [pltpu.SemaphoreType.DMA((len(args),))],
         compiler_params=params(32),
         name="experts",
     )(first, x, *stay(*args))
@@ -341,18 +372,15 @@
     attended = attend(
         prompt_lengths, queries, new_keys, new_values, key_cache, value_cache, nz
     )
-    ids = lax.dynamic_index_in_dim(expert_ids, d, 0, False).astype(F32)
-    logits = lax.dynamic_index_in_dim(top_logits, d, 0, False).astype(F32)
-    route = jnp.pad(jnp.concatenate([ids, logits], axis=1), ((0, 0), (0, 56)))
-    place = jnp.stack([z, c]).astype(jnp.int32)
+    place = jnp.stack([z, c, d]).astype(jnp.int32)
     first = jnp.stack([(2 * z + c) * per, (2 * z + 1 - c) * per]).astype(jnp.int32)
-    gain = norm_gain[None]
-    attended, route, place, first, gain = lax.optimization_barrier(
-        (attended, route, place, first, gain)
-    )
+    attended, place, first = lax.optimization_barrier((attended, place, first))
     by_heads = exchange(attended, zaxis)
-    keep, sent = project(place, by_heads, hidden_in, route, out_rows, other_out)
+    ids, logits = expert_ids.transpose(1, 2, 0), top_logits.transpose(1, 2, 0)
+    keep, sent = project(place, by_heads, hidden_in, ids, logits, out_rows, other_out)
+    sent, gain = lax.optimization_barrier((sent, norm_gain))
     got = lax.ppermute(sent, "v", SWAP)
+    got, gain = lax.optimization_barrier((got, gain[None]))
     quads = pair(keep, got, nz // 2)
     parts = exchange(quads, "w")
     residual, copies = norm(place, parts, gain, ndp, steps)

time: 120 us -> 120 us (level)
  waiting for transfers between devices: 5.24 us -> 14.1 us
  local copies, waits for them, and re-layouts: 18.9 us -> 12.3 us
  Pallas kernels: 18.8 us -> 15.9 us
  blocking collectives: 64.7 us -> 66.1 us
    optimization_barrier x6 -> x2, local copies, waits for them, and re-layouts: 14.5 us -> 4.71 us  [on_device(): copies, *weights = lax.optimization_barrier((copies, *weights))]
    all_to_all x1, waiting for transfers between devices: 1.27 us -> 10.1 us  [exchange(): return lax.all_to_all(value, axis, split_axis=0, concat_axis=0, tiled=True)]
    transpose x0 -> x2, local copies, waits for them, and re-layouts: none -> 7.5 us  [on_device(): w.swapaxes(1, 2)]
    unnamed x10 -> x8, local copies, waits for them, and re-layouts: 3.69 us -> 0.02 us
    pallas_call x1, Pallas kernels: 11.5 us -> 8.54 us  [experts(): pl.pallas_call(experts_kernel, in_specs=[smem(), vmem()] + [hbm()] * 6, o...]
    all_to_all x4, blocking collectives: 64.7 us -> 66.1 us  [exchange(): return lax.all_to_all(value, axis, split_axis=0, concat_axis=0, tiled=True)]
  transfers between devices with their start and end apart: 6 -> 6, of which waited for: 2 -> 2; matrix products, arithmetic and copies ran while one was open for 14% -> 6% of each run, Pallas kernels for 6% -> 6%
where the time goes in v5:
time: 120 us; the launch traced here: 119 us
  blocking collectives  66.1 us (55%)
  Pallas kernels  15.9 us (13%)
  waiting for transfers between devices  14.1 us (12%)
  local copies, waits for them, and re-layouts  12.3 us (10%)
  starting transfers between devices  9.11 us (8%)
    all_to_all x4, blocking collectives, exchange(): return lax.all_to_all(value, axis, split_axis=0, concat_axis=0, tiled=True)  66.1 us
    all_to_all x1, waiting for transfers between devices, exchange(): return lax.all_to_all(value, axis, split_axis=0, concat_axis=0, tiled=True)  10.1 us
    pallas_call x1, Pallas kernels, experts(): pl.pallas_call(experts_kernel, in_specs=[smem(), vmem()] + [hbm()] * 6, o...  8.54 us
    transpose x2, local copies, waits for them, and re-layouts, on_device(): w.swapaxes(1, 2)  7.5 us
    all_to_all x1, starting transfers between devices, exchange(): return lax.all_to_all(value, axis, split_axis=0, concat_axis=0, tiled=True)  7.39 us
    optimization_barrier x2, local copies, waits for them, and re-layouts, on_device(): copies, *weights = lax.optimization_barrier((copies, *weights))  4.71 us
    ppermute x1, waiting for transfers between devices, on_device(): got = lax.ppermute(sent, 'v', SWAP)  3.94 us
    pallas_call x1, Pallas kernels, project(): pl.pallas_call(project_kernel, in_specs=[smem(), vmem()] + [hbm()] * 5, o...  3.27 us
  transfers between devices with their start and end apart: 6, of which 2 were waited for; matrix products, arithmetic and copies ran while one was open for 6% of the time, Pallas kernels for 6%

profile of v5, /device:TPU:8, one launch (start us, length us, event | category | flops | bytes accessed | tf_op | source)
XLA Modules:
  0.0 119.2 jit_solution(15885259805305265028)
XLA Ops:
  0.0 0.0 copy-start.3
  0.0 0.0 collective-permute-start
  0.0 0.5 collective-permute-start.2
  0.5 0.1 collective-permute-start.3
  0.6 0.4 collective-permute-start.4
  1.7 2.1 %attend.1 = bf16[8,2,512]{2,1,0:T(2,128)(2,1)S(1)} custom-call(s32[1]{0:T(128)S(6)} %copy.59.len_ref, bf16[1,2,4096]{2,1,0:T(2,128)(2,1)} %q_hbm.1, bf16[1,2,512]{2,1,0:T(2,128)(2,1)} %nk_hbm.1, bf16[1,2,512]{2,1,0:T(2,128)(2,1)} %nv_hbm.1, bf16[1,512,512]{2,1,0:T(8,128)(2,1)} %k_hbm.1, bf16[1,512,512]{2,1,0:T(8,128)(2,1)} %v_hbm.1), custom_call_target="tpu_custom_call" | custom-call | tf_op jit(solution)/shard_map/attend/pallas_call | solution.py:102
  3.7 0.1 pad_add_fusion.1.first_ref
  3.8 0.1 pad_add_fusion.place_ref
  3.9 16.0 %all_to_all.25.x_ref = bf16[8,2,512]{2,1,0:T(2,128)(2,1)S(1)} all-to-all(bf16[8,2,512]{2,1,0:T(2,128)(2,1)S(1)} %attend.1), channel_id=1, replica_groups=mesh['x'=4,'y'=4,'w'=4,'v'=2,'c'=2] {'w','v'}, dimensions={0} | all-to-all | bytes 32768 | tf_op jit(solution)/shard_map/all_to_all | solution.py:340
  19.9 0.0 collective-permute-done.other_hbm
  19.9 0.0 copy-start
  19.9 3.3 %project.1 = (f32[16,2944]{1,0:T(8,128)S(1)}, bf16[16,2944]{1,0:T(8,128)(2,1)S(1)}) custom-call(s32[3]{0:T(128)S(1)} %pad_add_fusion.place_ref, bf16[8,2,512]{2,1,0:T(2,128)(2,1)S(1)} %all_to_all.25.x_ref, bf16[1,2,2880]{2,1,0:T(2,128)(2,1)} %hid_hbm.1, s32[2,4,16]{2,1,0:T(4,128)} %bitcast.24, bf16[2,4,16]{2,1,0:T(4,128)(2,1)} %bitcast.25, ...), custom_call_target="tpu_custom_call" | custom-call | tf_op jit(solution)/shard_map/project/pallas_call | solution.py:195
  23.2 0.7 collective-permute-start.1
  23.9 0.0 copy-done.3
  23.9 3.9 %collective-permute-done.1.got_ref = bf16[16,2944]{1,0:T(8,128)(2,1)S(1)} collective-permute-done((bf16[16,2944]{1,0:T(8,128)(2,1)S(1)}, bf16[16,2944]{1,0:T(8,128)(2,1)S(1)}, u32[]{:S(2)}, u32[]{:S(2)}) %collective-permute-start.1) | collective-permute-done | bytes 94240 | tf_op jit(solution)/shard_map/ppermute | solution.py:382
  27.9 13.0 %all_to_all.26.part_ref = bf16[4,16,2944]{2,1,0:T(8,128)(2,1)S(1)} all-to-all(bf16[4,16,2944]{2,1,0:T(8,128)(2,1)S(1)} %pair.1), channel_id=1, replica_groups=mesh['x'=4,'y'=4,'w'=4,'v'=2,'c'=2] {'w'}, dimensions={0} | all-to-all | bytes 753664 | tf_op jit(solution)/shard_map/all_to_all | solution.py:340
  40.9 2.0 %norm.1 = (f32[2,2880]{1,0:T(2,128)S(1)}, bf16[16,16,2944]{2,1,0:T(8,128)(2,1)}) custom-call(s32[3]{0:T(128)S(1)} %pad_add_fusion.place_ref, bf16[4,16,2944]{2,1,0:T(8,128)(2,1)S(1)} %all_to_all.26.part_ref, f32[1,2880]{1,0:T(1,128)S(1)} %broadcast_in_dim.6.gain_ref), custom_call_target="tpu_custom_call" | custom-call | tf_op jit(solution)/shard_map/norm/pallas_call | solution.py:260
  42.9 0.0 collective-permute-done.2
  42.9 0.0 collective-permute-done.3
  42.9 0.0 collective-permute-done.4
  42.9 0.0 copy-done
  42.9 1.6 %copy.49.d0_hbm = bf16[2,180,2880]{2,1,0:T(8,128)(2,1)} copy(bf16[2,180,2880]{2,0,1:T(2,128)(2,1)S(1)} %copy-done) | data formatting | bytes 4147200 | tf_op jit(solution)/shard_map/optimization_barrier | solution.py:387
  44.5 3.2 %copy.52.d1_hbm = bf16[2,180,2880]{2,1,0:T(8,128)(2,1)} copy(bf16[2,180,2880]{2,0,1:T(2,128)(2,1)} %collective-permute-done.4) | data formatting | bytes 4147200 | tf_op jit(solution)/shard_map/optimization_barrier | solution.py:387
  47.6 7.4 %all-to-all-start.2 = ((bf16[16,16,2944]{2,1,0:T(8,128)(2,1)}), bf16[16,16,2944]{2,1,0:T(8,128)(2,1)S(1)}, u32[]{:S(2)}, u32[]{:S(2)}) async-start(bf16[16,16,2944]{2,1,0:T(8,128)(2,1)} %get-tuple-element.41), calls=%async_computation.2 | async-start | bytes 3014656 | tf_op jit(solution)/shard_map/all_to_all | solution.py:340
  55.0 0.0 copy-start.1
  55.0 0.0 copy-start.2
  55.0 4.9 %copy_bitcast_fusion = (bf16[2,180,2880]{2,1,0:T(8,128)(2,1)}, bf16[2,180,2880]{2,1,0:T(8,128)(2,1)}) fusion(bf16[2,2880,180]{1,0,2:T(2,128)(2,1)} %collective-permute-done.3, bf16[2,2880,180]{1,0,2:T(2,128)(2,1)} %collective-permute-done.2), kind=kLoop, calls=%fused_computation | loop fusion | bytes 8294400 | tf_op jit(solution)/shard_map/transpose | solution.py:390
  60.0 0.0 copy-done.1
  60.0 0.0 copy-done.2
  60.0 2.6 %copy_bitcast_fusion.2 = (bf16[2,180,2880]{2,1,0:T(8,128)(2,1)}, bf16[2,180,2880]{2,1,0:T(8,128)(2,1)}) fusion(bf16[2,2880,180]{1,0,2:T(2,128)(2,1)S(1)} %copy-done.1, bf16[2,2880,180]{1,0,2:T(2,128)(2,1)S(1)} %copy-done.2), kind=kLoop, calls=%fused_computation.2 | loop fusion | bytes 8294400 | tf_op jit(solution)/shard_map/transpose | solution.py:390
  62.5 10.1 %all-to-all-done.2 = bf16[16,16,2944]{2,1,0:T(8,128)(2,1)S(1)} async-done(((bf16[16,16,2944]{2,1,0:T(8,128)(2,1)}), bf16[16,16,2944]{2,1,0:T(8,128)(2,1)S(1)}, u32[]{:S(2)}, u32[]{:S(2)}) %all-to-all-start.2) | async-done | bytes 1507360 | tf_op jit(solution)/shard_map/all_to_all | solution.py:340
  72.7 8.5 %experts.1 = bf16[256,2880]{1,0:T(8,128)(2,1)S(1)} custom-call(s32[2]{0:T(128)S(1)} %pad_add_fusion.1.first_ref, bf16[256,2944]{1,0:T(8,128)(2,1)S(1)} %bitcast.20, bf16[2,180,2880]{2,1,0:T(8,128)(2,1)} %get-tuple-element.49.g0_hbm, bf16[2,180,2880]{2,1,0:T(8,128)(2,1)} %get-tuple-element.50.u0_hbm, bf16[2,180,2880]{2,1,0:T(8,128)(2,1)} %get-tuple-element.51.g1_hbm, ...), custom_call_target="tpu_custom_call" | custom-call | tf_op jit(solution)/shard_map/experts/pallas_call | solution.py:323
  81.2 23.1 %all_to_all.27 = bf16[16,16,2880]{2,1,0:T(8,128)(2,1)S(1)} all-to-all(bf16[16,16,2880]{2,1,0:T(8,128)(2,1)S(1)} %bitcast.21), channel_id=1, replica_groups=mesh['x'=4,'y'=4,'w'=4,'v'=2,'c'=2] {'x','y'}, dimensions={0} | all-to-all | bytes 2949120 | tf_op jit(solution)/shard_map/all_to_all | solution.py:340
  104.3 0.2 reduce_sum.21
  104.5 14.0 %all_to_all.28 = bf16[8,2,2880]{2,1,0:T(2,128)(2,1)S(1)} all-to-all(bf16[8,2,2880]{2,1,0:T(2,128)(2,1)S(1)} %reshape.11), channel_id=1, replica_groups=mesh['x'=4,'y'=4,'w'=4,'v'=2,'c'=2] {'w','v'}, dimensions={0} | all-to-all | bytes 184320 | tf_op jit(solution)/shard_map/all_to_all | solution.py:340
  118.5 0.1 convert_reduce_fusion
  118.6 0.6 fusion
  (3 shorter events, 0.1 us)
Async XLA Ops:
  0.0 23.9 %copy-start.3 = (f32[2880]{0:T(1024)S(1)}, f32[2880]{0:T(1024)}, u32[]{:S(2)}) copy-start(f32[2880]{0:T(1024)} %param.22) | copy-start | bytes 34564
  0.0 19.9 %collective-permute-start = (bf16[2880,256]{1,0:T(8,128)(2,1)}, bf16[2880,256]{1,0:T(8,128)(2,1)S(1)}, u32[]{:S(2)}, u32[]{:S(2)}) collective-permute-start(bf16[2880,256]{1,0:T(8,128)(2,1)} %bitcast.22), channel_id=1, source_target_pairs={{0,1},{1,0},{2,3},{3,2},{4,5},{5,4},{6,7},{7,6},{8,9},{9,8},{10,11... | collective-permute-start | bytes 4423688 | tf_op jit(solution)/shard_map/ppermute | solution.py:369
  0.0 42.9 %collective-permute-start.2 = (bf16[2,2880,180]{1,0,2:T(2,128)(2,1)}, bf16[2,2880,180]{1,0,2:T(2,128)(2,1)}, u32[]{:S(2)}, u32[]{:S(2)}) collective-permute-start(bf16[2,2880,180]{1,0,2:T(2,128)(2,1)} %param.25), channel_id=1, source_target_pairs={{0,1},{1,0},{2,3},{3,2},{4,5},{5,4},{6,7},{7,6},{8,9},{9,8},{10,11... | collective-permute-start | bytes 6220808 | tf_op jit(solution)/shard_map/ppermute | solution.py:371
  0.5 42.4 %collective-permute-start.3 = (bf16[2,2880,180]{1,0,2:T(2,128)(2,1)}, bf16[2,2880,180]{1,0,2:T(2,128)(2,1)}, u32[]{:S(2)}, u32[]{:S(2)}) collective-permute-start(bf16[2,2880,180]{1,0,2:T(2,128)(2,1)} %param.26), channel_id=1, source_target_pairs={{0,1},{1,0},{2,3},{3,2},{4,5},{5,4},{6,7},{7,6},{8,9},{9,8},{10,11... | collective-permute-start | bytes 6220808 | tf_op jit(solution)/shard_map/ppermute | solution.py:371
  0.6 42.3 %collective-permute-start.4 = (bf16[2,180,2880]{2,0,1:T(2,128)(2,1)}, bf16[2,180,2880]{2,0,1:T(2,128)(2,1)}, u32[]{:S(2)}, u32[]{:S(2)}) collective-permute-start(bf16[2,180,2880]{2,0,1:T(2,128)(2,1)} %param.27), channel_id=1, source_target_pairs={{0,1},{1,0},{2,3},{3,2},{4,5},{5,4},{6,7},{7,6},{8,9},{9,8},{10,11... | collective-permute-start | bytes 6220808 | tf_op jit(solution)/shard_map/ppermute | solution.py:371
  19.9 23.0 %copy-start = (bf16[2,180,2880]{2,0,1:T(2,128)(2,1)S(1)}, bf16[2,180,2880]{2,0,1:T(2,128)(2,1)}, u32[]{:S(2)}) copy-start(bf16[2,180,2880]{2,0,1:T(2,128)(2,1)} %param.27) | copy-start | bytes 6220804
  23.2 4.7 %collective-permute-start.1 = (bf16[16,2944]{1,0:T(8,128)(2,1)S(1)}, bf16[16,2944]{1,0:T(8,128)(2,1)S(1)}, u32[]{:S(2)}, u32[]{:S(2)}) collective-permute-start(bf16[16,2944]{1,0:T(8,128)(2,1)S(1)} %get-tuple-element.34), channel_id=1, source_target_pairs={{0,2},{2,0},{1,3},{3,1},{4,6},{6,4},{5,7},{7,5},{8,10},{10,8},{9,1... | collective-permute-start | bytes 282632 | tf_op jit(solution)/shard_map/ppermute | solution.py:382
  47.6 25.0 %all-to-all-start.2 = ((bf16[16,16,2944]{2,1,0:T(8,128)(2,1)}), bf16[16,16,2944]{2,1,0:T(8,128)(2,1)S(1)}, u32[]{:S(2)}, u32[]{:S(2)}) async-start(bf16[16,16,2944]{2,1,0:T(8,128)(2,1)} %get-tuple-element.41), calls=%async_computation.2 | async-start | bytes 3014656 | tf_op jit(solution)/shard_map/all_to_all | solution.py:340
  55.0 5.0 %copy-start.1 = (bf16[2,2880,180]{1,0,2:T(2,128)(2,1)S(1)}, bf16[2,2880,180]{1,0,2:T(2,128)(2,1)}, u32[]{:S(2)}) copy-start(bf16[2,2880,180]{1,0,2:T(2,128)(2,1)} %param.26) | copy-start | bytes 6220804
  55.0 5.0 %copy-start.2 = (bf16[2,2880,180]{1,0,2:T(2,128)(2,1)S(1)}, bf16[2,2880,180]{1,0,2:T(2,128)(2,1)}, u32[]{:S(2)}) copy-start(bf16[2,2880,180]{1,0,2:T(2,128)(2,1)} %param.25) | copy-start | bytes 6220804

commit v6 on v5

--- a/solution.py
+++ b/solution.py
@@ -36,11 +36,12 @@
 
 
 def attend_kernel(
-    len_ref, q_hbm, nk_hbm, nv_hbm, k_hbm, v_hbm, out_ref,
+    len_ref, q_hbm, nk_hbm, nv_hbm, k_hbm, v_hbm, w_hbm, out_ref, w_ref,
     q_ref, nk_ref, nv_ref, k_ref, v_ref, rows_ref, flat_ref, sems,
 ):
     pairs = (
         (k_hbm, k_ref), (q_hbm, q_ref), (nk_hbm, nk_ref), (nv_hbm, nv_ref), (v_hbm, v_ref),
+        (w_hbm, w_ref),
     )
     copies = [pltpu.make_async_copy(a, b, sems.at[i]) for i, (a, b) in enumerate(pairs)]
     for copy in copies:
@@ -95,29 +96,33 @@
     wide = HQ * HD // blocks
     for b in range(blocks):
         out_ref[b] = flat_ref[:, b * wide : (b + 1) * wide].astype(BF16)
-
-
-def attend(length, q, nk, nv, k, v, blocks):
+    copies[5].wait()
+
+
+def attend(length, q, nk, nv, k, v, w, blocks):
     steps = q.shape[1]
     return pl.pallas_call(
         attend_kernel,
-        in_specs=[smem()] + [hbm()] * 5,
-        out_specs=vmem(),
-        out_shape=jax.ShapeDtypeStruct((blocks, steps, HQ * HD // blocks), BF16),
+        in_specs=[smem()] + [hbm()] * 6,
+        out_specs=[vmem(), vmem()],
+        out_shape=[
+            jax.ShapeDtypeStruct((blocks, steps, HQ * HD // blocks), BF16),
+            jax.ShapeDtypeStruct(w.shape, BF16),
+        ],
         scratch_shapes=[pltpu.VMEM(a.shape, BF16) for a in (q, nk, nv, k, v)]
         + [
             pltpu.VMEM((HQ * steps, HD), F32),
             pltpu.VMEM((steps, HQ * HD), F32),
-            pltpu.SemaphoreType.DMA((5,)),
+            pltpu.SemaphoreType.DMA((6,)),
         ],
         compiler_params=params(12),
         name="attend",
-    )(length, *stay(q, nk, nv, k, v))
+    )(length, *stay(q, nk, nv, k, v, w))
 
 
 def project_kernel(
-    place_ref, x_ref, hid_hbm, ids_hbm, logits_hbm, own_hbm, other_hbm, keep_ref, send_ref,
-    rows_ref, hid_ref, ids_ref, logits_ref, own_ref, other_ref, sems,
+    place_ref, x_ref, own_ref, other_ref, hid_hbm, ids_hbm, logits_hbm, keep_ref, send_ref,
+    rows_ref, hid_ref, ids_ref, logits_ref, sems,
 ):
     width, feats = own_ref.shape
     chunk = 640
@@ -127,20 +132,8 @@
         pltpu.make_async_copy(ids_hbm, ids_ref, sems.at[1]),
         pltpu.make_async_copy(logits_hbm, logits_ref, sems.at[2]),
     ]
-    copies = []
-    for i, (start, stop) in enumerate(cuts):
-        span = pl.ds(start, stop - start)
-        copies.append(
-            (
-                pltpu.make_async_copy(own_hbm.at[span], own_ref.at[span], sems.at[2 * i + 3]),
-                pltpu.make_async_copy(other_hbm.at[span], other_ref.at[span], sems.at[2 * i + 4]),
-            )
-        )
     for copy in small:
         copy.start()
-    for pair_copies in copies:
-        pair_copies[0].start()
-        pair_copies[1].start()
     blocks, steps, _ = x_ref.shape
     for i in range(blocks):
         rows_ref[i * steps : (i + 1) * steps, :] = x_ref[i].astype(F32)
@@ -174,9 +167,7 @@
     block = lax.broadcasted_iota(jnp.int32, extra.shape, 0) // steps
     extra = jnp.where(block == place_ref[0], extra, 0.0)
     dims = (((1,), (1,)), ((), ()))
-    for (start, stop), (first_copy, second_copy) in zip(cuts, copies):
-        first_copy.wait()
-        second_copy.wait()
+    for start, stop in cuts:
         part = lax.dot_general(mine, own_ref[start:stop], dims, preferred_element_type=F32)
         part = part + lax.dot_general(
             theirs, other_ref[start:stop], dims, preferred_element_type=F32
@@ -194,7 +185,7 @@
     rows = blocks * steps
     return pl.pallas_call(
         project_kernel,
-        in_specs=[smem(), vmem()] + [hbm()] * 5,
+        in_specs=[smem(), vmem(), vmem(), vmem()] + [hbm()] * 3,
         out_specs=[vmem(), vmem()],
         out_shape=[
             jax.ShapeDtypeStruct((rows, wide), F32),
@@ -205,13 +196,11 @@
             pltpu.VMEM(hidden.shape, BF16),
             pltpu.VMEM(ids.shape, jnp.int32),
             pltpu.VMEM(logits.shape, BF16),
-            pltpu.VMEM(own.shape, BF16),
-            pltpu.VMEM(own.shape, BF16),
-            pltpu.SemaphoreType.DMA((2 * pl.cdiv(own.shape[0], 640) + 3,)),
+            pltpu.SemaphoreType.DMA((3,)),
         ],
         compiler_params=params(12),
         name="project",
-    )(place, x, *stay(hidden, ids, logits, own), other)
+    )(place, x, own, other, *stay(hidden, ids, logits))
 
 
 def pair_kernel(keep_ref, got_ref, out_ref):
@@ -367,31 +356,36 @@
     per = gate_weight.shape[0]
     out_rows = out_weight.T
     other_out = lax.ppermute(out_rows, "c", SWAP)
-    weights = [gate_weight, up_weight, down_weight]
-    weights += [lax.ppermute(w, "c", SWAP) for w in weights]
-    attended = attend(
-        prompt_lengths, queries, new_keys, new_values, key_cache, value_cache, nz
+    far_down, far_gate, far_up = (
+        lax.ppermute(w, "c", SWAP) for w in (down_weight, gate_weight, up_weight)
+    )
+    attended, own_out = attend(
+        prompt_lengths, queries, new_keys, new_values, key_cache, value_cache, out_rows, nz
     )
     place = jnp.stack([z, c, d]).astype(jnp.int32)
     first = jnp.stack([(2 * z + c) * per, (2 * z + 1 - c) * per]).astype(jnp.int32)
     attended, place, first = lax.optimization_barrier((attended, place, first))
     by_heads = exchange(attended, zaxis)
     ids, logits = expert_ids.transpose(1, 2, 0), top_logits.transpose(1, 2, 0)
-    keep, sent = project(place, by_heads, hidden_in, ids, logits, out_rows, other_out)
-    sent, gain = lax.optimization_barrier((sent, norm_gain))
+    keep, sent = project(place, by_heads, hidden_in, ids, logits, own_out, other_out)
+    sent, gain, down, far_down = lax.optimization_barrier(
+        (sent, norm_gain, down_weight, far_down)
+    )
     got = lax.ppermute(sent, "v", SWAP)
-    got, gain = lax.optimization_barrier((got, gain[None]))
+    got, gain, down, far_down = lax.optimization_barrier(
+        (got, gain[None], row_major(down), row_major(far_down))
+    )
     quads = pair(keep, got, nz // 2)
     parts = exchange(quads, "w")
     residual, copies = norm(place, parts, gain, ndp, steps)
-    copies, *weights = lax.optimization_barrier((copies, *weights))
+    copies, *weights = lax.optimization_barrier(
+        (copies, gate_weight, up_weight, far_gate, far_up)
+    )
     tokens = exchange(copies, dp)
-    relaid = [
-        row_major(w if i % 3 == 2 else w.swapaxes(1, 2)) for i, w in enumerate(weights)
-    ]
-    tokens, *relaid = lax.optimization_barrier((tokens, *relaid))
+    relaid = [row_major(w.swapaxes(1, 2)) for w in weights]
+    tokens, gate, up, far_gate, far_up = lax.optimization_barrier((tokens, *relaid))
     tokens = tokens.reshape(ndp * nz * steps, -1)
-    made = experts(first, tokens, relaid[:3], relaid[3:])
+    made = experts(first, tokens, (gate, up, down), (far_gate, far_up, far_down))
     back = exchange(made.reshape(ndp, nz * steps, width), dp)
     column_sum = jnp.sum(back.astype(F32), axis=0).astype(BF16)
     final = exchange(column_sum.reshape(nz, steps, width), zaxis)

time: 120 us -> 116 us (0.967)
  waiting for transfers between devices: 14.1 us -> 9.17 us
  blocking collectives: 66.1 us -> 68.7 us
    ppermute x1, waiting for transfers between devices: 3.94 us -> 0.01 us  [on_device(): got = lax.ppermute(sent, 'v', SWAP)]
    all_to_all x4, blocking collectives: 66.1 us -> 68.7 us  [exchange(): return lax.all_to_all(value, axis, split_axis=0, concat_axis=0, tiled=True)]
  transfers between devices with their start and end apart: 6 -> 6, of which waited for: 2 -> 1; matrix products, arithmetic and copies ran while one was open for 6% -> 11% of each run, Pallas kernels for 6% -> 5%
where the time goes in v6:
time: 116 us
  blocking collectives  68.7 us (59%)
  Pallas kernels  14.8 us (13%)
  local copies, waits for them, and re-layouts  12.3 us (11%)
  waiting for transfers between devices  9.17 us (8%)
  starting transfers between devices  9.13 us (8%)
    all_to_all x4, blocking collectives, exchange(): return lax.all_to_all(value, axis, split_axis=0, concat_axis=0, tiled=True)  68.7 us
    all_to_all x1, waiting for transfers between devices, exchange(): return lax.all_to_all(value, axis, split_axis=0, concat_axis=0, tiled=True)  9.16 us
    pallas_call x1, Pallas kernels, experts(): pl.pallas_call(experts_kernel, in_specs=[smem(), vmem()] + [hbm()] * 6, o...  8.55 us
    transpose x2, local copies, waits for them, and re-layouts, on_device(): relaid = [row_major(w.swapaxes(1, 2)) for w in weights]  7.53 us
    all_to_all x1, starting transfers between devices, exchange(): return lax.all_to_all(value, axis, split_axis=0, concat_axis=0, tiled=True)  7.41 us
    optimization_barrier x2, local copies, waits for them, and re-layouts, on_device(): lax.optimization_barrier((sent, norm_gain, down_weight, far_down))  4.73 us
  transfers between devices with their start and end apart: 6, of which 1 were waited for; matrix products, arithmetic and copies ran while one was open for 11% of the time, Pallas kernels for 5%

profile of v6, /device:TPU:8, one launch (start us, length us, event | category | flops | bytes accessed | tf_op | source)
XLA Modules:
  0.0 115.9 jit_solution(4647577753894222669)
XLA Ops:
  0.0 0.0 collective-permute-start.1
  0.0 0.5 collective-permute-start
  0.5 0.0 collective-permute-start.3
  0.5 0.5 collective-permute-start.4
  1.7 2.1 %attend.1 = (bf16[8,2,512]{2,1,0:T(2,128)(2,1)S(1)}, bf16[2880,256]{1,0:T(8,128)(2,1)S(1)}) custom-call(s32[1]{0:T(128)S(6)} %copy.59.len_ref, bf16[1,2,4096]{2,1,0:T(2,128)(2,1)} %q_hbm.1, bf16[1,2,512]{2,1,0:T(2,128)(2,1)} %nk_hbm.1, bf16[1,2,512]{2,1,0:T(2,128)(2,1)} %nv_hbm.1, bf16[1,512,512]{2,1,0:T(8,128)(2,1)} %k_hbm.1, bf16[1,512,512]{2,1,0:T(8,128)(2,1)} %v_hbm.1, ...), custom_call_target="tpu_custom_call" | custom-call | tf_op jit(solution)/shard_map/attend/pallas_call | solution.py:104
  3.7 0.0 copy-start
  3.8 0.1 pad_add_fusion.1.first_ref
  3.8 0.1 pad_add_fusion.place_ref
  3.9 16.2 %all_to_all.25.x_ref = bf16[8,2,512]{2,1,0:T(2,128)(2,1)S(1)} all-to-all(bf16[8,2,512]{2,1,0:T(2,128)(2,1)S(1)} %get-tuple-element.34), channel_id=1, replica_groups=mesh['x'=4,'y'=4,'w'=4,'v'=2,'c'=2] {'w','v'}, dimensions={0} | all-to-all | bytes 32768 | tf_op jit(solution)/shard_map/all_to_all | solution.py:329
  20.1 0.0 collective-permute-done.other_ref
  20.1 2.2 %project.1 = (f32[16,2944]{1,0:T(8,128)S(1)}, bf16[16,2944]{1,0:T(8,128)(2,1)S(1)}) custom-call(s32[3]{0:T(128)S(1)} %pad_add_fusion.place_ref, bf16[8,2,512]{2,1,0:T(2,128)(2,1)S(1)} %all_to_all.25.x_ref, bf16[2880,256]{1,0:T(8,128)(2,1)S(1)} %get-tuple-element.35.own_ref, bf16[2880,256]{1,0:T(8,128)(2,1)S(1)} %collective-permute-done.other_ref, ...), custom_call_target="tpu_custom_call" | custom-call | tf_op jit(solution)/shard_map/project/pallas_call | solution.py:186
  22.3 0.0 collective-permute-done.1
  22.3 0.7 collective-permute-start.2
  23.0 0.0 copy-done
  23.0 1.6 %copy.47.d0_hbm = bf16[2,180,2880]{2,1,0:T(8,128)(2,1)} copy(bf16[2,180,2880]{2,0,1:T(2,128)(2,1)S(1)} %copy-done) | data formatting | bytes 4147200 | tf_op jit(solution)/shard_map/optimization_barrier | solution.py:371
  24.5 0.0 copy-start.3
  24.6 3.2 %copy.48.d1_hbm = bf16[2,180,2880]{2,1,0:T(8,128)(2,1)} copy(bf16[2,180,2880]{2,0,1:T(2,128)(2,1)} %collective-permute-done.1) | data formatting | bytes 4147200 | tf_op jit(solution)/shard_map/optimization_barrier | solution.py:371
  27.7 0.0 copy-done.3
  27.7 0.0 collective-permute-done.2.got_ref
  27.8 15.1 %all_to_all.26.part_ref = bf16[4,16,2944]{2,1,0:T(8,128)(2,1)S(1)} all-to-all(bf16[4,16,2944]{2,1,0:T(8,128)(2,1)S(1)} %pair.1), channel_id=1, replica_groups=mesh['x'=4,'y'=4,'w'=4,'v'=2,'c'=2] {'w'}, dimensions={0} | all-to-all | bytes 753664 | tf_op jit(solution)/shard_map/all_to_all | solution.py:329
  42.9 2.0 %norm.1 = (f32[2,2880]{1,0:T(2,128)S(1)}, bf16[16,16,2944]{2,1,0:T(8,128)(2,1)}) custom-call(s32[3]{0:T(128)S(1)} %pad_add_fusion.place_ref, bf16[4,16,2944]{2,1,0:T(8,128)(2,1)S(1)} %all_to_all.26.part_ref, f32[1,2880]{1,0:T(1,128)S(1)} %broadcast_in_dim.6.gain_ref), custom_call_target="tpu_custom_call" | custom-call | tf_op jit(solution)/shard_map/norm/pallas_call | solution.py:249
  44.8 0.0 collective-permute-done.3
  44.9 0.0 collective-permute-done.4
  44.9 7.4 %all-to-all-start.2 = ((bf16[16,16,2944]{2,1,0:T(8,128)(2,1)}), bf16[16,16,2944]{2,1,0:T(8,128)(2,1)S(1)}, u32[]{:S(2)}, u32[]{:S(2)}) async-start(bf16[16,16,2944]{2,1,0:T(8,128)(2,1)} %get-tuple-element.47), calls=%async_computation.2 | async-start | bytes 3014656 | tf_op jit(solution)/shard_map/all_to_all | solution.py:329
  52.3 0.0 copy-start.1
  52.3 0.0 copy-start.2
  52.3 4.9 %copy_bitcast_fusion = (bf16[2,180,2880]{2,1,0:T(8,128)(2,1)}, bf16[2,180,2880]{2,1,0:T(8,128)(2,1)}) fusion(bf16[2,2880,180]{1,0,2:T(2,128)(2,1)} %collective-permute-done.4, bf16[2,2880,180]{1,0,2:T(2,128)(2,1)} %collective-permute-done.3), kind=kLoop, calls=%fused_computation | loop fusion | bytes 8294400 | tf_op jit(solution)/shard_map/transpose | solution.py:385
  57.2 0.0 copy-done.1
  57.2 0.0 copy-done.2
  57.2 2.6 %copy_bitcast_fusion.2 = (bf16[2,180,2880]{2,1,0:T(8,128)(2,1)}, bf16[2,180,2880]{2,1,0:T(8,128)(2,1)}) fusion(bf16[2,2880,180]{1,0,2:T(2,128)(2,1)S(1)} %copy-done.1, bf16[2,2880,180]{1,0,2:T(2,128)(2,1)S(1)} %copy-done.2), kind=kLoop, calls=%fused_computation.2 | loop fusion | bytes 8294400 | tf_op jit(solution)/shard_map/transpose | solution.py:385
  59.8 9.2 %all-to-all-done.2 = bf16[16,16,2944]{2,1,0:T(8,128)(2,1)S(1)} async-done(((bf16[16,16,2944]{2,1,0:T(8,128)(2,1)}), bf16[16,16,2944]{2,1,0:T(8,128)(2,1)S(1)}, u32[]{:S(2)}, u32[]{:S(2)}) %all-to-all-start.2) | async-done | bytes 1507360 | tf_op jit(solution)/shard_map/all_to_all | solution.py:329
  69.0 8.5 %experts.1 = bf16[256,2880]{1,0:T(8,128)(2,1)S(1)} custom-call(s32[2]{0:T(128)S(1)} %pad_add_fusion.1.first_ref, bf16[256,2944]{1,0:T(8,128)(2,1)S(1)} %bitcast.20, bf16[2,180,2880]{2,1,0:T(8,128)(2,1)} %get-tuple-element.53.g0_hbm, bf16[2,180,2880]{2,1,0:T(8,128)(2,1)} %get-tuple-element.54.u0_hbm, bf16[2,180,2880]{2,1,0:T(8,128)(2,1)} %get-tuple-element.55.g1_hbm, ...), custom_call_target="tpu_custom_call" | custom-call | tf_op jit(solution)/shard_map/experts/pallas_call | solution.py:312
  77.5 22.1 %all_to_all.27 = bf16[16,16,2880]{2,1,0:T(8,128)(2,1)S(1)} all-to-all(bf16[16,16,2880]{2,1,0:T(8,128)(2,1)S(1)} %bitcast.21), channel_id=1, replica_groups=mesh['x'=4,'y'=4,'w'=4,'v'=2,'c'=2] {'x','y'}, dimensions={0} | all-to-all | bytes 2949120 | tf_op jit(solution)/shard_map/all_to_all | solution.py:329
  99.7 0.2 reduce_sum.21
  99.9 15.3 %all_to_all.28 = bf16[8,2,2880]{2,1,0:T(2,128)(2,1)S(1)} all-to-all(bf16[8,2,2880]{2,1,0:T(2,128)(2,1)S(1)} %reshape.11), channel_id=1, replica_groups=mesh['x'=4,'y'=4,'w'=4,'v'=2,'c'=2] {'w','v'}, dimensions={0} | all-to-all | bytes 184320 | tf_op jit(solution)/shard_map/all_to_all | solution.py:329
  115.3 0.1 convert_reduce_fusion
  115.3 0.6 fusion
  (3 shorter events, 0.1 us)
Async XLA Ops:
  0.0 22.3 %collective-permute-start.1 = (bf16[2,180,2880]{2,0,1:T(2,128)(2,1)}, bf16[2,180,2880]{2,0,1:T(2,128)(2,1)}, u32[]{:S(2)}, u32[]{:S(2)}) collective-permute-start(bf16[2,180,2880]{2,0,1:T(2,128)(2,1)} %param.27), channel_id=1, source_target_pairs={{0,1},{1,0},{2,3},{3,2},{4,5},{5,4},{6,7},{7,6},{8,9},{9,8},{10,11... | collective-permute-start | bytes 6220808 | tf_op jit(solution)/shard_map/ppermute | solution.py:360
  0.0 20.1 %collective-permute-start = (bf16[2880,256]{1,0:T(8,128)(2,1)}, bf16[2880,256]{1,0:T(8,128)(2,1)S(1)}, u32[]{:S(2)}, u32[]{:S(2)}) collective-permute-start(bf16[2880,256]{1,0:T(8,128)(2,1)} %bitcast.22), channel_id=1, source_target_pairs={{0,1},{1,0},{2,3},{3,2},{4,5},{5,4},{6,7},{7,6},{8,9},{9,8},{10,11... | collective-permute-start | bytes 4423688 | tf_op jit(solution)/shard_map/ppermute | solution.py:358
  0.5 44.3 %collective-permute-start.3 = (bf16[2,2880,180]{1,0,2:T(2,128)(2,1)}, bf16[2,2880,180]{1,0,2:T(2,128)(2,1)}, u32[]{:S(2)}, u32[]{:S(2)}) collective-permute-start(bf16[2,2880,180]{1,0,2:T(2,128)(2,1)} %param.25), channel_id=1, source_target_pairs={{0,1},{1,0},{2,3},{3,2},{4,5},{5,4},{6,7},{7,6},{8,9},{9,8},{10,11... | collective-permute-start | bytes 6220808 | tf_op jit(solution)/shard_map/ppermute | solution.py:360
  0.5 44.3 %collective-permute-start.4 = (bf16[2,2880,180]{1,0,2:T(2,128)(2,1)}, bf16[2,2880,180]{1,0,2:T(2,128)(2,1)}, u32[]{:S(2)}, u32[]{:S(2)}) collective-permute-start(bf16[2,2880,180]{1,0,2:T(2,128)(2,1)} %param.26), channel_id=1, source_target_pairs={{0,1},{1,0},{2,3},{3,2},{4,5},{5,4},{6,7},{7,6},{8,9},{9,8},{10,11... | collective-permute-start | bytes 6220808 | tf_op jit(solution)/shard_map/ppermute | solution.py:360
  3.7 19.2 %copy-start = (bf16[2,180,2880]{2,0,1:T(2,128)(2,1)S(1)}, bf16[2,180,2880]{2,0,1:T(2,128)(2,1)}, u32[]{:S(2)}) copy-start(bf16[2,180,2880]{2,0,1:T(2,128)(2,1)} %param.27) | copy-start | bytes 6220804
  22.3 5.5 %collective-permute-start.2 = (bf16[16,2944]{1,0:T(8,128)(2,1)S(1)}, bf16[16,2944]{1,0:T(8,128)(2,1)S(1)}, u32[]{:S(2)}, u32[]{:S(2)}) collective-permute-start(bf16[16,2944]{1,0:T(8,128)(2,1)S(1)} %get-tuple-element.38), channel_id=1, source_target_pairs={{0,2},{2,0},{1,3},{3,1},{4,6},{6,4},{5,7},{7,5},{8,10},{10,8},{9,1... | collective-permute-start | bytes 282632 | tf_op jit(solution)/shard_map/ppermute | solution.py:374
  24.5 3.2 %copy-start.3 = (f32[2880]{0:T(1024)S(1)}, f32[2880]{0:T(1024)}, u32[]{:S(2)}) copy-start(f32[2880]{0:T(1024)} %param.22) | copy-start | bytes 34564
  44.9 24.1 %all-to-all-start.2 = ((bf16[16,16,2944]{2,1,0:T(8,128)(2,1)}), bf16[16,16,2944]{2,1,0:T(8,128)(2,1)S(1)}, u32[]{:S(2)}, u32[]{:S(2)}) async-start(bf16[16,16,2944]{2,1,0:T(8,128)(2,1)} %get-tuple-element.47), calls=%async_computation.2 | async-start | bytes 3014656 | tf_op jit(solution)/shard_map/all_to_all | solution.py:329
  52.3 5.0 %copy-start.1 = (bf16[2,2880,180]{1,0,2:T(2,128)(2,1)S(1)}, bf16[2,2880,180]{1,0,2:T(2,128)(2,1)}, u32[]{:S(2)}) copy-start(bf16[2,2880,180]{1,0,2:T(2,128)(2,1)} %param.26) | copy-start | bytes 6220804
  52.3 4.9 %copy-start.2 = (bf16[2,2880,180]{1,0,2:T(2,128)(2,1)S(1)}, bf16[2,2880,180]{1,0,2:T(2,128)(2,1)}, u32[]{:S(2)}) copy-start(bf16[2,2880,180]{1,0,2:T(2,128)(2,1)} %param.25) | copy-start | bytes 6220804

commit v7 on v6

--- a/solution.py
+++ b/solution.py
@@ -121,8 +121,8 @@
 
 
 def project_kernel(
-    place_ref, x_ref, own_ref, other_ref, hid_hbm, ids_hbm, logits_hbm, keep_ref, send_ref,
-    rows_ref, hid_ref, ids_ref, logits_ref, sems,
+    place_ref, x_ref, own_ref, other_ref, hid_hbm, ids_hbm, logits_hbm, out_hbm,
+    send_ref, rows_ref, hid_ref, ids_ref, logits_ref, sems,
 ):
     width, feats = own_ref.shape
     chunk = 640
@@ -144,7 +144,7 @@
     theirs = jnp.where(first, high, low)
     for copy in small:
         copy.wait()
-    spare = keep_ref.shape[1] - width
+    spare = send_ref.shape[1] - width
     lane = lax.broadcasted_iota(jnp.int32, (1, spare), 1)
     routes = []
     for ref in (ids_ref, logits_ref):
@@ -172,11 +172,15 @@
         part = part + lax.dot_general(
             theirs, other_ref[start:stop], dims, preferred_element_type=F32
         )
-        part = part + extra[:, start:stop]
-        keep_ref[:, start:stop] = part
-        send_ref[:, start:stop] = part.astype(BF16)
-    keep_ref[:, width:] = extra[:, width:]
+        send_ref[:, start:stop] = (part + extra[:, start:stop]).astype(BF16)
     send_ref[:, width:] = extra[:, width:].astype(BF16)
+    out = [
+        pltpu.make_async_copy(send_ref, out_hbm.at[i], sems.at[3 + i]) for i in range(blocks)
+    ]
+    for copy in out:
+        copy.start()
+    for copy in out:
+        copy.wait()
 
 
 def project(place, x, hidden, ids, logits, own, other):
@@ -186,38 +190,19 @@
     return pl.pallas_call(
         project_kernel,
         in_specs=[smem(), vmem(), vmem(), vmem()] + [hbm()] * 3,
-        out_specs=[vmem(), vmem()],
-        out_shape=[
-            jax.ShapeDtypeStruct((rows, wide), F32),
-            jax.ShapeDtypeStruct((rows, wide), BF16),
-        ],
+        out_specs=hbm(),
+        out_shape=jax.ShapeDtypeStruct((blocks, rows, wide), BF16),
         scratch_shapes=[
+            pltpu.VMEM((rows, wide), BF16),
             pltpu.VMEM((rows, feats), F32),
             pltpu.VMEM(hidden.shape, BF16),
             pltpu.VMEM(ids.shape, jnp.int32),
             pltpu.VMEM(logits.shape, BF16),
-            pltpu.SemaphoreType.DMA((3,)),
+            pltpu.SemaphoreType.DMA((3 + blocks,)),
         ],
         compiler_params=params(12),
         name="project",
     )(place, x, own, other, *stay(hidden, ids, logits))
-
-
-def pair_kernel(keep_ref, got_ref, out_ref):
-    total = (keep_ref[...] + got_ref[...].astype(F32)).astype(BF16)
-    for i in range(out_ref.shape[0]):
-        out_ref[i] = total
-
-
-def pair(keep, got, copies):
-    return pl.pallas_call(
-        pair_kernel,
-        in_specs=[vmem(), vmem()],
-        out_specs=vmem(),
-        out_shape=jax.ShapeDtypeStruct((copies,) + keep.shape, BF16),
-        compiler_params=params(12),
-        name="pair",
-    )(keep, got)
 
 
 def norm_kernel(place_ref, part_ref, gain_ref, res_ref, out_hbm, full_ref, sems):
@@ -356,9 +341,7 @@
     per = gate_weight.shape[0]
     out_rows = out_weight.T
     other_out = lax.ppermute(out_rows, "c", SWAP)
-    far_down, far_gate, far_up = (
-        lax.ppermute(w, "c", SWAP) for w in (down_weight, gate_weight, up_weight)
-    )
+    far_down = lax.ppermute(down_weight, "c", SWAP)
     attended, own_out = attend(
         prompt_lengths, queries, new_keys, new_values, key_cache, value_cache, out_rows, nz
     )
@@ -367,19 +350,18 @@
     attended, place, first = lax.optimization_barrier((attended, place, first))
     by_heads = exchange(attended, zaxis)
     ids, logits = expert_ids.transpose(1, 2, 0), top_logits.transpose(1, 2, 0)
-    keep, sent = project(place, by_heads, hidden_in, ids, logits, own_out, other_out)
-    sent, gain, down, far_down = lax.optimization_barrier(
-        (sent, norm_gain, down_weight, far_down)
-    )
-    got = lax.ppermute(sent, "v", SWAP)
-    got, gain, down, far_down = lax.optimization_barrier(
-        (got, gain[None], row_major(down), row_major(far_down))
-    )
-    quads = pair(keep, got, nz // 2)
-    parts = exchange(quads, "w")
+    sent = project(place, by_heads, hidden_in, ids, logits, own_out, other_out)
+    sent, gain, gate, up, down, far_down = lax.optimization_barrier(
+        (sent, norm_gain, gate_weight, up_weight, down_weight, far_down)
+    )
+    far_gate, far_up = lax.ppermute(gate, "c", SWAP), lax.ppermute(up, "c", SWAP)
+    parts = exchange(sent, zaxis)
+    parts, gain, down, far_down = lax.optimization_barrier(
+        (parts, gain[None], row_major(down), row_major(far_down))
+    )
     residual, copies = norm(place, parts, gain, ndp, steps)
     copies, *weights = lax.optimization_barrier(
-        (copies, gate_weight, up_weight, far_gate, far_up)
+        (copies, gate, up, far_gate, far_up)
     )
     tokens = exchange(copies, dp)
     relaid = [row_major(w.swapaxes(1, 2)) for w in weights]

time: 116 us -> 126 us (1.086)
  waiting for transfers between devices: 9.17 us -> 29 us
  blocking collectives: 68.7 us -> 50.7 us
  local copies, waits for them, and re-layouts: 12.3 us -> 15.9 us
  starting transfers between devices: 9.13 us -> 12 us
    all_to_all x1 -> x2, waiting for transfers between devices: 9.16 us -> 29 us  [exchange(): return lax.all_to_all(value, axis, split_axis=0, concat_axis=0, tiled=True)]
    all_to_all x4 -> x3, blocking collectives: 68.7 us -> 50.7 us  [exchange(): return lax.all_to_all(value, axis, split_axis=0, concat_axis=0, tiled=True)]
    all_to_all x1 -> x2, starting transfers between devices: 7.41 us -> 10.9 us  [exchange(): return lax.all_to_all(value, axis, split_axis=0, concat_axis=0, tiled=True)]
    transpose x2, local copies, waits for them, and re-layouts: 7.53 us -> 9.53 us  [on_device(): relaid = [row_major(w.swapaxes(1, 2)) for w in weights]]
    optimization_barrier x2, local copies, waits for them, and re-layouts: 4.73 us -> 6.34 us  [on_device(): lax.optimization_barrier((sent, norm_gain, gate_weight, up_weight, down_w...]
  transfers between devices with their start and end apart: 6 -> 6, of which waited for: 1 -> 2; matrix products, arithmetic and copies ran while one was open for 11% -> 13% of each run, Pallas kernels for 5% -> 6%
where the time goes in v7:
time: 126 us; the launch traced here: 125 us
  blocking collectives  50.7 us (40%)
  waiting for transfers between devices  29 us (23%)
  local copies, waits for them, and re-layouts  15.9 us (13%)
  Pallas kernels  15.8 us (13%)
  starting transfers between devices  12 us (10%)
    all_to_all x3, blocking collectives, exchange(): return lax.all_to_all(value, axis, split_axis=0, concat_axis=0, tiled=True)  50.7 us
    all_to_all x2, waiting for transfers between devices, exchange(): return lax.all_to_all(value, axis, split_axis=0, concat_axis=0, tiled=True)  29 us
    all_to_all x2, starting transfers between devices, exchange(): return lax.all_to_all(value, axis, split_axis=0, concat_axis=0, tiled=True)  10.9 us
    transpose x2, local copies, waits for them, and re-layouts, on_device(): relaid = [row_major(w.swapaxes(1, 2)) for w in weights]  9.53 us
    pallas_call x1, Pallas kernels, experts(): pl.pallas_call(experts_kernel, in_specs=[smem(), vmem()] + [hbm()] * 6, o...  8.55 us
    optimization_barrier x2, local copies, waits for them, and re-layouts, on_device(): lax.optimization_barrier((sent, norm_gain, gate_weight, up_weight, down_w...  6.34 us
    pallas_call x1, Pallas kernels, project(): pl.pallas_call(project_kernel, in_specs=[smem(), vmem(), vmem(), vmem()]...  3.14 us
  transfers between devices with their start and end apart: 6, of which 2 were waited for; matrix products, arithmetic and copies ran while one was open for 13% of the time, Pallas kernels for 6%

profile of v7, /device:TPU:8, one launch (start us, length us, event | category | flops | bytes accessed | tf_op | source)
XLA Modules:
  0.0 125.2 jit_solution(12509387991001735932)
XLA Ops:
  0.0 0.0 collective-permute-start.1
  0.0 0.5 collective-permute-start
  1.2 2.1 %attend.1 = (bf16[8,2,512]{2,1,0:T(2,128)(2,1)S(1)}, bf16[2880,256]{1,0:T(8,128)(2,1)S(1)}) custom-call(s32[1]{0:T(128)S(6)} %copy.59.len_ref, bf16[1,2,4096]{2,1,0:T(2,128)(2,1)} %q_hbm.1, bf16[1,2,512]{2,1,0:T(2,128)(2,1)} %nk_hbm.1, bf16[1,2,512]{2,1,0:T(2,128)(2,1)} %nv_hbm.1, bf16[1,512,512]{2,1,0:T(8,128)(2,1)} %k_hbm.1, bf16[1,512,512]{2,1,0:T(8,128)(2,1)} %v_hbm.1, ...), custom_call_target="tpu_custom_call" | custom-call | tf_op jit(solution)/shard_map/attend/pallas_call | solution.py:104
  3.2 0.1 pad_add_fusion.1.first_ref
  3.3 0.1 pad_add_fusion.place_ref
  3.4 16.0 %all_to_all.25.x_ref = bf16[8,2,512]{2,1,0:T(2,128)(2,1)S(1)} all-to-all(bf16[8,2,512]{2,1,0:T(2,128)(2,1)S(1)} %get-tuple-element.34), channel_id=1, replica_groups=mesh['x'=4,'y'=4,'w'=4,'v'=2,'c'=2] {'w','v'}, dimensions={0} | all-to-all | bytes 32768 | tf_op jit(solution)/shard_map/all_to_all | solution.py:314
  19.4 0.0 collective-permute-done.other_ref
  19.4 3.1 %project.1 = bf16[8,16,2944]{2,1,0:T(8,128)(2,1)} custom-call(s32[3]{0:T(128)S(1)} %pad_add_fusion.place_ref, bf16[8,2,512]{2,1,0:T(2,128)(2,1)S(1)} %all_to_all.25.x_ref, bf16[2880,256]{1,0:T(8,128)(2,1)S(1)} %get-tuple-element.35.own_ref, bf16[2880,256]{1,0:T(8,128)(2,1)S(1)} %collective-permute-done.other_ref, bf16[1,2,2880]{2,1,0:T(2,128)(2,1)} %hid_hbm.1, ...), custom_call_target="tpu_custom_call" | custom-call | tf_op jit(solution)/shard_map/project/pallas_call | solution.py:190
  22.6 0.0 collective-permute-done.1
  22.6 0.1 collective-permute-start.2
  22.7 0.5 collective-permute-start.3
  23.2 3.5 %all-to-all-start.1 = ((bf16[8,16,2944]{2,1,0:T(8,128)(2,1)}), bf16[8,16,2944]{2,1,0:T(8,128)(2,1)S(1)}, u32[]{:S(2)}, u32[]{:S(2)}) async-start(bf16[8,16,2944]{2,1,0:T(8,128)(2,1)} %project.1), calls=%async_computation.1 | async-start | bytes 1507328 | tf_op jit(solution)/shard_map/all_to_all | solution.py:314
  26.7 3.2 %copy.47.d0_hbm = bf16[2,180,2880]{2,1,0:T(8,128)(2,1)} copy(bf16[2,180,2880]{2,0,1:T(2,128)(2,1)} %param.27) | data formatting | bytes 4147200 | tf_op jit(solution)/shard_map/optimization_barrier | solution.py:354
  29.9 0.0 copy-start
  29.9 3.2 %copy.48.d1_hbm = bf16[2,180,2880]{2,1,0:T(8,128)(2,1)} copy(bf16[2,180,2880]{2,0,1:T(2,128)(2,1)} %collective-permute-done.1) | data formatting | bytes 4147200 | tf_op jit(solution)/shard_map/optimization_barrier | solution.py:354
  33.1 0.0 copy-done
  33.1 16.6 %all-to-all-done.1.part_ref = bf16[8,16,2944]{2,1,0:T(8,128)(2,1)S(1)} async-done(((bf16[8,16,2944]{2,1,0:T(8,128)(2,1)}), bf16[8,16,2944]{2,1,0:T(8,128)(2,1)S(1)}, u32[]{:S(2)}, u32[]{:S(2)}) %all-to-all-start.1) | async-done | bytes 753696 | tf_op jit(solution)/shard_map/all_to_all | solution.py:314
  49.6 2.0 %norm.1 = (f32[2,2880]{1,0:T(2,128)S(1)}, bf16[16,16,2944]{2,1,0:T(8,128)(2,1)}) custom-call(s32[3]{0:T(128)S(1)} %pad_add_fusion.place_ref, bf16[8,16,2944]{2,1,0:T(8,128)(2,1)S(1)} %all-to-all-done.1.part_ref, f32[1,2880]{1,0:T(1,128)S(1)} %broadcast_in_dim.6.gain_ref), custom_call_target="tpu_custom_call" | custom-call | tf_op jit(solution)/shard_map/norm/pallas_call | solution.py:234
  51.7 0.0 collective-permute-done.2
  51.7 0.0 collective-permute-done.3
  51.7 7.4 %all-to-all-start.2 = ((bf16[16,16,2944]{2,1,0:T(8,128)(2,1)}), bf16[16,16,2944]{2,1,0:T(8,128)(2,1)S(1)}, u32[]{:S(2)}, u32[]{:S(2)}) async-start(bf16[16,16,2944]{2,1,0:T(8,128)(2,1)} %get-tuple-element.47), calls=%async_computation.2 | async-start | bytes 3014656 | tf_op jit(solution)/shard_map/all_to_all | solution.py:314
  59.1 4.8 %copy_bitcast_fusion = (bf16[2,180,2880]{2,1,0:T(8,128)(2,1)}, bf16[2,180,2880]{2,1,0:T(8,128)(2,1)}) fusion(bf16[2,2880,180]{1,0,2:T(2,128)(2,1)} %collective-permute-done.3, bf16[2,2880,180]{1,0,2:T(2,128)(2,1)} %collective-permute-done.2), kind=kLoop, calls=%fused_computation | loop fusion | bytes 8294400 | tf_op jit(solution)/shard_map/transpose | solution.py:367
  63.9 4.8 %copy_bitcast_fusion.2 = (bf16[2,180,2880]{2,1,0:T(8,128)(2,1)}, bf16[2,180,2880]{2,1,0:T(8,128)(2,1)}) fusion(bf16[2,2880,180]{1,0,2:T(2,128)(2,1)} %param.26, bf16[2,2880,180]{1,0,2:T(2,128)(2,1)} %param.25), kind=kLoop, calls=%fused_computation.2 | loop fusion | bytes 8294400 | tf_op jit(solution)/shard_map/transpose | solution.py:367
  68.6 12.4 %all-to-all-done.2 = bf16[16,16,2944]{2,1,0:T(8,128)(2,1)S(1)} async-done(((bf16[16,16,2944]{2,1,0:T(8,128)(2,1)}), bf16[16,16,2944]{2,1,0:T(8,128)(2,1)S(1)}, u32[]{:S(2)}, u32[]{:S(2)}) %all-to-all-start.2) | async-done | bytes 1507360 | tf_op jit(solution)/shard_map/all_to_all | solution.py:314
  81.0 8.5 %experts.1 = bf16[256,2880]{1,0:T(8,128)(2,1)S(1)} custom-call(s32[2]{0:T(128)S(1)} %pad_add_fusion.1.first_ref, bf16[256,2944]{1,0:T(8,128)(2,1)S(1)} %bitcast.20, bf16[2,180,2880]{2,1,0:T(8,128)(2,1)} %get-tuple-element.53.g0_hbm, bf16[2,180,2880]{2,1,0:T(8,128)(2,1)} %get-tuple-element.54.u0_hbm, bf16[2,180,2880]{2,1,0:T(8,128)(2,1)} %get-tuple-element.55.g1_hbm, ...), custom_call_target="tpu_custom_call" | custom-call | tf_op jit(solution)/shard_map/experts/pallas_call | solution.py:297
  89.6 23.6 %all_to_all.26 = bf16[16,16,2880]{2,1,0:T(8,128)(2,1)S(1)} all-to-all(bf16[16,16,2880]{2,1,0:T(8,128)(2,1)S(1)} %bitcast.21), channel_id=1, replica_groups=mesh['x'=4,'y'=4,'w'=4,'v'=2,'c'=2] {'x','y'}, dimensions={0} | all-to-all | bytes 2949120 | tf_op jit(solution)/shard_map/all_to_all | solution.py:314
  113.2 0.2 reduce_sum.21
  113.5 11.1 %all_to_all.27 = bf16[8,2,2880]{2,1,0:T(2,128)(2,1)S(1)} all-to-all(bf16[8,2,2880]{2,1,0:T(2,128)(2,1)S(1)} %reshape.11), channel_id=1, replica_groups=mesh['x'=4,'y'=4,'w'=4,'v'=2,'c'=2] {'w','v'}, dimensions={0} | all-to-all | bytes 184320 | tf_op jit(solution)/shard_map/all_to_all | solution.py:314
  124.5 0.1 convert_reduce_fusion
  124.6 0.6 fusion
  (2 shorter events, 0.0 us)
Async XLA Ops:
  0.0 22.6 %collective-permute-start.1 = (bf16[2,180,2880]{2,0,1:T(2,128)(2,1)}, bf16[2,180,2880]{2,0,1:T(2,128)(2,1)}, u32[]{:S(2)}, u32[]{:S(2)}) collective-permute-start(bf16[2,180,2880]{2,0,1:T(2,128)(2,1)} %param.27), channel_id=1, source_target_pairs={{0,1},{1,0},{2,3},{3,2},{4,5},{5,4},{6,7},{7,6},{8,9},{9,8},{10,11... | collective-permute-start | bytes 6220808 | tf_op jit(solution)/shard_map/ppermute | solution.py:344
  0.0 19.4 %collective-permute-start = (bf16[2880,256]{1,0:T(8,128)(2,1)}, bf16[2880,256]{1,0:T(8,128)(2,1)S(1)}, u32[]{:S(2)}, u32[]{:S(2)}) collective-permute-start(bf16[2880,256]{1,0:T(8,128)(2,1)} %bitcast.22), channel_id=1, source_target_pairs={{0,1},{1,0},{2,3},{3,2},{4,5},{5,4},{6,7},{7,6},{8,9},{9,8},{10,11... | collective-permute-start | bytes 4423688 | tf_op jit(solution)/shard_map/ppermute | solution.py:343
  22.6 29.1 %collective-permute-start.2 = (bf16[2,2880,180]{1,0,2:T(2,128)(2,1)}, bf16[2,2880,180]{1,0,2:T(2,128)(2,1)}, u32[]{:S(2)}, u32[]{:S(2)}) collective-permute-start(bf16[2,2880,180]{1,0,2:T(2,128)(2,1)} %param.25), channel_id=1, source_target_pairs={{0,1},{1,0},{2,3},{3,2},{4,5},{5,4},{6,7},{7,6},{8,9},{9,8},{10,11... | collective-permute-start | bytes 6220808 | tf_op jit(solution)/shard_map/ppermute | solution.py:357
  22.7 29.0 %collective-permute-start.3 = (bf16[2,2880,180]{1,0,2:T(2,128)(2,1)}, bf16[2,2880,180]{1,0,2:T(2,128)(2,1)}, u32[]{:S(2)}, u32[]{:S(2)}) collective-permute-start(bf16[2,2880,180]{1,0,2:T(2,128)(2,1)} %param.26), channel_id=1, source_target_pairs={{0,1},{1,0},{2,3},{3,2},{4,5},{5,4},{6,7},{7,6},{8,9},{9,8},{10,11... | collective-permute-start | bytes 6220808 | tf_op jit(solution)/shard_map/ppermute | solution.py:357
  23.2 26.5 %all-to-all-start.1 = ((bf16[8,16,2944]{2,1,0:T(8,128)(2,1)}), bf16[8,16,2944]{2,1,0:T(8,128)(2,1)S(1)}, u32[]{:S(2)}, u32[]{:S(2)}) async-start(bf16[8,16,2944]{2,1,0:T(8,128)(2,1)} %project.1), calls=%async_computation.1 | async-start | bytes 1507328 | tf_op jit(solution)/shard_map/all_to_all | solution.py:314
  29.9 3.2 %copy-start = (f32[2880]{0:T(1024)S(1)}, f32[2880]{0:T(1024)}, u32[]{:S(2)}) copy-start(f32[2880]{0:T(1024)} %param.22) | copy-start | bytes 34564
  51.7 29.3 %all-to-all-start.2 = ((bf16[16,16,2944]{2,1,0:T(8,128)(2,1)}), bf16[16,16,2944]{2,1,0:T(8,128)(2,1)S(1)}, u32[]{:S(2)}, u32[]{:S(2)}) async-start(bf16[16,16,2944]{2,1,0:T(8,128)(2,1)} %get-tuple-element.47), calls=%async_computation.2 | async-start | bytes 3014656 | tf_op jit(solution)/shard_map/all_to_all | solution.py:314

commit v8 on v6

--- a/solution.py
+++ b/solution.py
@@ -203,28 +203,29 @@
     )(place, x, own, other, *stay(hidden, ids, logits))
 
 
-def pair_kernel(keep_ref, got_ref, out_ref):
-    total = (keep_ref[...] + got_ref[...].astype(F32)).astype(BF16)
-    for i in range(out_ref.shape[0]):
-        out_ref[i] = total
-
-
-def pair(keep, got, copies):
+def join_kernel(keep_ref, got_ref, next_ref, send_ref):
+    total = keep_ref[...] + got_ref[...].astype(F32)
+    next_ref[...] = total
+    send_ref[...] = total.astype(BF16)
+
+
+def join(keep, got):
     return pl.pallas_call(
-        pair_kernel,
+        join_kernel,
         in_specs=[vmem(), vmem()],
-        out_specs=vmem(),
-        out_shape=jax.ShapeDtypeStruct((copies,) + keep.shape, BF16),
+        out_specs=[vmem(), vmem()],
+        out_shape=[
+            jax.ShapeDtypeStruct(keep.shape, F32),
+            jax.ShapeDtypeStruct(keep.shape, BF16),
+        ],
         compiler_params=params(12),
-        name="pair",
+        name="join",
     )(keep, got)
 
 
-def norm_kernel(place_ref, part_ref, gain_ref, res_ref, out_hbm, full_ref, sems):
+def norm_kernel(place_ref, keep_ref, got_ref, gain_ref, res_ref, out_hbm, full_ref, sems):
     steps, width = res_ref.shape
-    total = part_ref[0].astype(F32)
-    for i in range(1, part_ref.shape[0]):
-        total = total + part_ref[i].astype(F32)
+    total = keep_ref[...] + got_ref[...].astype(F32)
     res = total[:, :width]
     scale = lax.rsqrt(jnp.sum(res * res, axis=1, keepdims=True) / width + 1e-05)
     normed = (res * scale * gain_ref[...]).astype(BF16)
@@ -243,12 +244,12 @@
         copy.wait()
 
 
-def norm(place, parts, gain, copies, steps):
-    _, rows, wide = parts.shape
+def norm(place, keep, got, gain, copies, steps):
+    rows, wide = keep.shape
     width = gain.shape[1]
     return pl.pallas_call(
         norm_kernel,
-        in_specs=[smem(), vmem(), vmem()],
+        in_specs=[smem(), vmem(), vmem(), vmem()],
         out_specs=[vmem(), hbm()],
         out_shape=[
             jax.ShapeDtypeStruct((steps, width), F32),
@@ -257,7 +258,7 @@
         scratch_shapes=[pltpu.VMEM((rows, wide), BF16), pltpu.SemaphoreType.DMA((copies,))],
         compiler_params=params(12),
         name="norm",
-    )(place, parts, gain)
+    )(place, keep, got, gain)
 
 
 def experts_kernel(
@@ -356,9 +357,7 @@
     per = gate_weight.shape[0]
     out_rows = out_weight.T
     other_out = lax.ppermute(out_rows, "c", SWAP)
-    far_down, far_gate, far_up = (
-        lax.ppermute(w, "c", SWAP) for w in (down_weight, gate_weight, up_weight)
-    )
+    far_down = lax.ppermute(down_weight, "c", SWAP)
     attended, own_out = attend(
         prompt_lengths, queries, new_keys, new_values, key_cache, value_cache, out_rows, nz
     )
@@ -368,22 +367,28 @@
     by_heads = exchange(attended, zaxis)
     ids, logits = expert_ids.transpose(1, 2, 0), top_logits.transpose(1, 2, 0)
     keep, sent = project(place, by_heads, hidden_in, ids, logits, own_out, other_out)
-    sent, gain, down, far_down = lax.optimization_barrier(
-        (sent, norm_gain, down_weight, far_down)
+    sent, gain, down, gate, up = lax.optimization_barrier(
+        (sent, norm_gain, down_weight, gate_weight, up_weight)
     )
     got = lax.ppermute(sent, "v", SWAP)
-    got, gain, down, far_down = lax.optimization_barrier(
-        (got, gain[None], row_major(down), row_major(far_down))
-    )
-    quads = pair(keep, got, nz // 2)
-    parts = exchange(quads, "w")
-    residual, copies = norm(place, parts, gain, ndp, steps)
-    copies, *weights = lax.optimization_barrier(
-        (copies, gate_weight, up_weight, far_gate, far_up)
-    )
+    far_gate, far_up = lax.ppermute(gate, "c", SWAP), lax.ppermute(up, "c", SWAP)
+    got, gain, down = lax.optimization_barrier((got, gain[None], row_major(down)))
+    keep, sent = join(keep, got)
+    sent, far_down = lax.optimization_barrier((sent, far_down))
+    got = lax.ppermute(sent, "w", [(i, i ^ 1) for i in range(nz // 2)])
+    got, far_down = lax.optimization_barrier((got, row_major(far_down)))
+    keep, sent = join(keep, got)
+    sent, gate, up = lax.optimization_barrier((sent, gate, up))
+    got = lax.ppermute(sent, "w", [(i, i ^ 2) for i in range(nz // 2)])
+    got, gate, up = lax.optimization_barrier(
+        (got, row_major(gate.swapaxes(1, 2)), row_major(up.swapaxes(1, 2)))
+    )
+    residual, copies = norm(place, keep, got, gain, ndp, steps)
+    copies, far_gate, far_up = lax.optimization_barrier((copies, far_gate, far_up))
     tokens = exchange(copies, dp)
-    relaid = [row_major(w.swapaxes(1, 2)) for w in weights]
-    tokens, gate, up, far_gate, far_up = lax.optimization_barrier((tokens, *relaid))
+    tokens, far_gate, far_up = lax.optimization_barrier(
+        (tokens, row_major(far_gate.swapaxes(1, 2)), row_major(far_up.swapaxes(1, 2)))
+    )
     tokens = tokens.reshape(ndp * nz * steps, -1)
     made = experts(first, tokens, (gate, up, down), (far_gate, far_up, far_down))
     back = exchange(made.reshape(ndp, nz * steps, width), dp)

time: 116 us -> 118 us (1.017)
  blocking collectives: 68.7 us -> 50.2 us
  waiting for transfers between devices: 9.17 us -> 25.9 us
  local copies, waits for them, and re-layouts: 12.3 us -> 13.8 us
  starting transfers between devices: 9.13 us -> 10.5 us
    all_to_all x4 -> x3, blocking collectives: 68.7 us -> 50.2 us  [exchange(): return lax.all_to_all(value, axis, split_axis=0, concat_axis=0, tiled=True)]
    ppermute x3 -> x5, waiting for transfers between devices: 0.01 us -> 8.78 us  [the longest x1 5.68 us: on_device(): got = lax.ppermute(sent, 'w', [(i, i ^ 2) for i in range(nz // 2)])]
    optimization_barrier x2 -> x4, local copies, waits for them, and re-layouts: 4.73 us -> 11.1 us  [the longest x2 6.42 us: on_device(): lax.optimization_barrier((copies, far_gate, far_up))]
    all_to_all x1, waiting for transfers between devices: 9.16 us -> 14.6 us  [exchange(): return lax.all_to_all(value, axis, split_axis=0, concat_axis=0, tiled=True)]
    transpose x2 -> x1, local copies, waits for them, and re-layouts: 7.53 us -> 2.58 us  [on_device(): up.swapaxes(1, 2)]
    ppermute x1, waiting for transfers between devices: 0.01 us -> 2.5 us  [on_device(): got = lax.ppermute(sent, 'v', SWAP)]
    ppermute x3 -> x5, starting transfers between devices: 0.51 us -> 2.46 us  [the longest x1 0.71 us: on_device(): got = lax.ppermute(sent, 'w', [(i, i ^ 2) for i in range(nz // 2)])]
  transfers between devices with their start and end apart: 6 -> 8, of which waited for: 1 -> 4; matrix products, arithmetic and copies ran while one was open for 11% -> 12% of each run, Pallas kernels for 5% -> 5%
where the time goes in v8:
time: 118 us; the launch traced here: 117 us
  blocking collectives  50.2 us (43%)
  waiting for transfers between devices  25.9 us (22%)
  Pallas kernels  15 us (13%)
  local copies, waits for them, and re-layouts  13.8 us (12%)
  starting transfers between devices  10.5 us (9%)
    all_to_all x3, blocking collectives, exchange(): return lax.all_to_all(value, axis, split_axis=0, concat_axis=0, tiled=True)  50.2 us
    all_to_all x1, waiting for transfers between devices, exchange(): return lax.all_to_all(value, axis, split_axis=0, concat_axis=0, tiled=True)  14.6 us
    pallas_call x1, Pallas kernels, experts(): pl.pallas_call(experts_kernel, in_specs=[smem(), vmem()] + [hbm()] * 6, o...  8.55 us
    all_to_all x1, starting transfers between devices, exchange(): return lax.all_to_all(value, axis, split_axis=0, concat_axis=0, tiled=True)  7.4 us
    optimization_barrier x2, local copies, waits for them, and re-layouts, on_device(): lax.optimization_barrier((copies, far_gate, far_up))  6.42 us
    ppermute x1, waiting for transfers between devices, on_device(): got = lax.ppermute(sent, 'w', [(i, i ^ 2) for i in range(nz // 2)])  5.68 us
    optimization_barrier x1, local copies, waits for them, and re-layouts, on_device(): sent, far_down = lax.optimization_barrier((sent, far_down))  3.13 us
    ppermute x1, waiting for transfers between devices, on_device(): got = lax.ppermute(sent, 'w', [(i, i ^ 1) for i in range(nz // 2)])  3.09 us
  transfers between devices with their start and end apart: 8, of which 4 were waited for; matrix products, arithmetic and copies ran while one was open for 12% of the time, Pallas kernels for 5%

profile of v8, /device:TPU:8, one launch (start us, length us, event | category | flops | bytes accessed | tf_op | source)
XLA Modules:
  0.0 117.2 jit_solution(834109938477722381)
XLA Ops:
  0.0 0.0 collective-permute-start
  0.0 0.5 collective-permute-start.2
  1.2 0.0 copy-start.1
  1.2 2.2 %attend.1 = (bf16[8,2,512]{2,1,0:T(2,128)(2,1)S(1)}, bf16[2880,256]{1,0:T(8,128)(2,1)S(1)}) custom-call(s32[1]{0:T(128)S(6)} %copy.61.len_ref, bf16[1,2,4096]{2,1,0:T(2,128)(2,1)} %q_hbm.1, bf16[1,2,512]{2,1,0:T(2,128)(2,1)} %nk_hbm.1, bf16[1,2,512]{2,1,0:T(2,128)(2,1)} %nv_hbm.1, bf16[1,512,512]{2,1,0:T(8,128)(2,1)} %k_hbm.1, bf16[1,512,512]{2,1,0:T(8,128)(2,1)} %v_hbm.1, ...), custom_call_target="tpu_custom_call" | custom-call | tf_op jit(solution)/shard_map/attend/pallas_call | solution.py:104
  3.4 0.0 copy-start.3
  3.4 0.0 copy-start
  3.4 0.1 pad_add_fusion.1.first_ref
  3.5 0.1 pad_add_fusion.place_ref
  3.6 16.2 %all_to_all.20.x_ref = bf16[8,2,512]{2,1,0:T(2,128)(2,1)S(1)} all-to-all(bf16[8,2,512]{2,1,0:T(2,128)(2,1)S(1)} %get-tuple-element.44), channel_id=1, replica_groups=mesh['x'=4,'y'=4,'w'=4,'v'=2,'c'=2] {'w','v'}, dimensions={0} | all-to-all | bytes 32768 | tf_op jit(solution)/shard_map/all_to_all | solution.py:330
  19.7 0.0 collective-permute-done.other_ref
  19.7 2.2 %project.1 = (f32[16,2944]{1,0:T(8,128)S(1)}, bf16[16,2944]{1,0:T(8,128)(2,1)S(1)}) custom-call(s32[3]{0:T(128)S(1)} %pad_add_fusion.place_ref, bf16[8,2,512]{2,1,0:T(2,128)(2,1)S(1)} %all_to_all.20.x_ref, bf16[2880,256]{1,0:T(8,128)(2,1)S(1)} %get-tuple-element.45.own_ref, bf16[2880,256]{1,0:T(8,128)(2,1)S(1)} %collective-permute-done.other_ref, ...), custom_call_target="tpu_custom_call" | custom-call | tf_op jit(solution)/shard_map/project/pallas_call | solution.py:186
  21.9 0.0 copy-done.1
  21.9 0.1 collective-permute-start.5
  22.0 0.5 collective-permute-start.6
  22.5 0.6 collective-permute-start.1
  23.1 0.0 copy-done.3
  23.2 0.0 copy-done
  23.2 1.6 %copy.47.d0_hbm = bf16[2,180,2880]{2,1,0:T(8,128)(2,1)} copy(bf16[2,180,2880]{2,0,1:T(2,128)(2,1)S(1)} %copy-done) | data formatting | bytes 4147200 | tf_op jit(solution)/shard_map/optimization_barrier | solution.py:370
  24.7 2.5 %collective-permute-done.1.got_ref = bf16[16,2944]{1,0:T(8,128)(2,1)S(1)} collective-permute-done((bf16[16,2944]{1,0:T(8,128)(2,1)S(1)}, bf16[16,2944]{1,0:T(8,128)(2,1)S(1)}, u32[]{:S(2)}, u32[]{:S(2)}) %collective-permute-start.1) | collective-permute-done | bytes 94240 | tf_op jit(solution)/shard_map/ppermute | solution.py:373
  27.3 0.0 collective-permute-done.2
  27.3 0.0 copy-start.2
  27.3 0.7 collective-permute-start.3
  28.0 3.1 %copy.48.d1_hbm = bf16[2,180,2880]{2,1,0:T(8,128)(2,1)} copy(bf16[2,180,2880]{2,0,1:T(2,128)(2,1)} %collective-permute-done.2) | data formatting | bytes 4147200 | tf_op jit(solution)/shard_map/optimization_barrier | solution.py:377
  31.1 3.1 %collective-permute-done.3.got_ref = bf16[16,2944]{1,0:T(8,128)(2,1)S(1)} collective-permute-done((bf16[16,2944]{1,0:T(8,128)(2,1)S(1)}, bf16[16,2944]{1,0:T(8,128)(2,1)S(1)}, u32[]{:S(2)}, u32[]{:S(2)}) %collective-permute-start.3) | collective-permute-done | bytes 94240 | tf_op jit(solution)/shard_map/ppermute | solution.py:378
  34.2 0.7 collective-permute-start.4
  34.9 0.0 copy-done.2
  34.9 2.6 %copy_bitcast_fusion.2 = (bf16[2,180,2880]{2,1,0:T(8,128)(2,1)}, bf16[2,180,2880]{2,1,0:T(8,128)(2,1)}) fusion(bf16[2,2880,180]{1,0,2:T(2,128)(2,1)S(1)} %copy-done.2, bf16[2,2880,180]{1,0,2:T(2,128)(2,1)S(1)} %copy-done.1), kind=kLoop, calls=%fused_computation.2 | loop fusion | bytes 8294400 | tf_op jit(solution)/shard_map/transpose | solution.py:384
  37.5 5.7 %collective-permute-done.4.got_ref = bf16[16,2944]{1,0:T(8,128)(2,1)S(1)} collective-permute-done((bf16[16,2944]{1,0:T(8,128)(2,1)S(1)}, bf16[16,2944]{1,0:T(8,128)(2,1)S(1)}, u32[]{:S(2)}, u32[]{:S(2)}) %collective-permute-start.4) | collective-permute-done | bytes 94240 | tf_op jit(solution)/shard_map/ppermute | solution.py:382
  43.2 2.0 %norm.1 = (f32[2,2880]{1,0:T(2,128)S(1)}, bf16[16,16,2944]{2,1,0:T(8,128)(2,1)}) custom-call(s32[3]{0:T(128)S(1)} %pad_add_fusion.place_ref, f32[16,2944]{1,0:T(8,128)S(1)} %get-tuple-element.57.keep_ref, bf16[16,2944]{1,0:T(8,128)(2,1)S(1)} %collective-permute-done.4.got_ref, f32[1,2880]{1,0:T(1,128)S(1)} %broadcast_in_dim.6.gain_ref), custom_call_target="tpu_custom_call" | custom-call | tf_op jit(solution)/shard_map/norm/pallas_call | solution.py:250
  45.2 0.0 collective-permute-done.5
  45.2 0.0 collective-permute-done.6
  45.2 7.4 %all-to-all-start.1 = ((bf16[16,16,2944]{2,1,0:T(8,128)(2,1)}), bf16[16,16,2944]{2,1,0:T(8,128)(2,1)S(1)}, u32[]{:S(2)}, u32[]{:S(2)}) async-start(bf16[16,16,2944]{2,1,0:T(8,128)(2,1)} %get-tuple-element.69), calls=%async_computation.1 | async-start | bytes 3014656 | tf_op jit(solution)/shard_map/all_to_all | solution.py:330
  52.6 3.2 %copy.60 = bf16[2,2880,180]{1,2,0:T(8,128)(2,1)} copy(bf16[2,2880,180]{1,0,2:T(2,128)(2,1)} %collective-permute-done.5) | data formatting | bytes 4147200 | tf_op jit(solution)/shard_map/optimization_barrier | solution.py:387
  55.8 3.2 %copy.59 = bf16[2,2880,180]{1,2,0:T(8,128)(2,1)} copy(bf16[2,2880,180]{1,0,2:T(2,128)(2,1)} %collective-permute-done.6) | data formatting | bytes 4147200 | tf_op jit(solution)/shard_map/optimization_barrier | solution.py:387
  59.0 14.6 %all-to-all-done.1 = bf16[16,16,2944]{2,1,0:T(8,128)(2,1)S(1)} async-done(((bf16[16,16,2944]{2,1,0:T(8,128)(2,1)}), bf16[16,16,2944]{2,1,0:T(8,128)(2,1)S(1)}, u32[]{:S(2)}, u32[]{:S(2)}) %all-to-all-start.1) | async-done | bytes 1507360 | tf_op jit(solution)/shard_map/all_to_all | solution.py:330
  73.6 8.5 %experts.1 = bf16[256,2880]{1,0:T(8,128)(2,1)S(1)} custom-call(s32[2]{0:T(128)S(1)} %pad_add_fusion.1.first_ref, bf16[256,2944]{1,0:T(8,128)(2,1)S(1)} %bitcast.22, bf16[2,180,2880]{2,1,0:T(8,128)(2,1)} %get-tuple-element.73.g0_hbm, bf16[2,180,2880]{2,1,0:T(8,128)(2,1)} %get-tuple-element.74.u0_hbm, bf16[2,180,2880]{2,1,0:T(8,128)(2,1)} %bitcast.24, ...), custom_call_target="tpu_custom_call" | custom-call | tf_op jit(solution)/shard_map/experts/pallas_call | solution.py:313
  82.2 23.0 %all_to_all.21 = bf16[16,16,2880]{2,1,0:T(8,128)(2,1)S(1)} all-to-all(bf16[16,16,2880]{2,1,0:T(8,128)(2,1)S(1)} %bitcast.23), channel_id=1, replica_groups=mesh['x'=4,'y'=4,'w'=4,'v'=2,'c'=2] {'x','y'}, dimensions={0} | all-to-all | bytes 2949120 | tf_op jit(solution)/shard_map/all_to_all | solution.py:330
  105.2 0.2 reduce_sum.21
  105.4 11.1 %all_to_all.22 = bf16[8,2,2880]{2,1,0:T(2,128)(2,1)S(1)} all-to-all(bf16[8,2,2880]{2,1,0:T(2,128)(2,1)S(1)} %reshape.11), channel_id=1, replica_groups=mesh['x'=4,'y'=4,'w'=4,'v'=2,'c'=2] {'w','v'}, dimensions={0} | all-to-all | bytes 184320 | tf_op jit(solution)/shard_map/all_to_all | solution.py:330
  116.5 0.1 convert_reduce_fusion
  116.6 0.6 fusion
  (4 shorter events, 0.1 us)
Async XLA Ops:
  0.0 19.7 %collective-permute-start = (bf16[2880,256]{1,0:T(8,128)(2,1)}, bf16[2880,256]{1,0:T(8,128)(2,1)S(1)}, u32[]{:S(2)}, u32[]{:S(2)}) collective-permute-start(bf16[2880,256]{1,0:T(8,128)(2,1)} %bitcast.26), channel_id=1, source_target_pairs={{0,1},{1,0},{2,3},{3,2},{4,5},{5,4},{6,7},{7,6},{8,9},{9,8},{10,11... | collective-permute-start | bytes 4423688 | tf_op jit(solution)/shard_map/ppermute | solution.py:359
  0.0 27.3 %collective-permute-start.2 = (bf16[2,180,2880]{2,0,1:T(2,128)(2,1)}, bf16[2,180,2880]{2,0,1:T(2,128)(2,1)}, u32[]{:S(2)}, u32[]{:S(2)}) collective-permute-start(bf16[2,180,2880]{2,0,1:T(2,128)(2,1)} %param.27), channel_id=1, source_target_pairs={{0,1},{1,0},{2,3},{3,2},{4,5},{5,4},{6,7},{7,6},{8,9},{9,8},{10,11... | collective-permute-start | bytes 6220808 | tf_op jit(solution)/shard_map/ppermute | solution.py:360
  1.2 20.8 %copy-start.1 = (bf16[2,2880,180]{1,0,2:T(2,128)(2,1)S(1)}, bf16[2,2880,180]{1,0,2:T(2,128)(2,1)}, u32[]{:S(2)}) copy-start(bf16[2,2880,180]{1,0,2:T(2,128)(2,1)} %param.25) | copy-start | bytes 6220804
  3.4 19.7 %copy-start.3 = (f32[2880]{0:T(1024)S(1)}, f32[2880]{0:T(1024)}, u32[]{:S(2)}) copy-start(f32[2880]{0:T(1024)} %param.22) | copy-start | bytes 34564
  3.4 19.8 %copy-start = (bf16[2,180,2880]{2,0,1:T(2,128)(2,1)S(1)}, bf16[2,180,2880]{2,0,1:T(2,128)(2,1)}, u32[]{:S(2)}) copy-start(bf16[2,180,2880]{2,0,1:T(2,128)(2,1)} %param.27) | copy-start | bytes 6220804
  21.9 23.2 %collective-permute-start.5 = (bf16[2,2880,180]{1,0,2:T(2,128)(2,1)S(1)}, bf16[2,2880,180]{1,0,2:T(2,128)(2,1)}, u32[]{:S(2)}, u32[]{:S(2)}) collective-permute-start(bf16[2,2880,180]{1,0,2:T(2,128)(2,1)S(1)} %copy-done.1), channel_id=1, source_target_pairs={{0,1},{1,0},{2,3},{3,2},{4,5},{5,4},{6,7},{7,6},{8,9},{9,8},{10,11... | collective-permute-start | bytes 6220808 | tf_op jit(solution)/shard_map/ppermute | solution.py:374
  22.0 23.2 %collective-permute-start.6 = (bf16[2,2880,180]{1,0,2:T(2,128)(2,1)}, bf16[2,2880,180]{1,0,2:T(2,128)(2,1)}, u32[]{:S(2)}, u32[]{:S(2)}) collective-permute-start(bf16[2,2880,180]{1,0,2:T(2,128)(2,1)} %param.26), channel_id=1, source_target_pairs={{0,1},{1,0},{2,3},{3,2},{4,5},{5,4},{6,7},{7,6},{8,9},{9,8},{10,11... | collective-permute-start | bytes 6220808 | tf_op jit(solution)/shard_map/ppermute | solution.py:374
  22.5 4.7 %collective-permute-start.1 = (bf16[16,2944]{1,0:T(8,128)(2,1)S(1)}, bf16[16,2944]{1,0:T(8,128)(2,1)S(1)}, u32[]{:S(2)}, u32[]{:S(2)}) collective-permute-start(bf16[16,2944]{1,0:T(8,128)(2,1)S(1)} %get-tuple-element.48), channel_id=1, source_target_pairs={{0,2},{2,0},{1,3},{3,1},{4,6},{6,4},{5,7},{7,5},{8,10},{10,8},{9,1... | collective-permute-start | bytes 282632 | tf_op jit(solution)/shard_map/ppermute | solution.py:373
  27.3 7.6 %copy-start.2 = (bf16[2,2880,180]{1,0,2:T(2,128)(2,1)S(1)}, bf16[2,2880,180]{1,0,2:T(2,128)(2,1)}, u32[]{:S(2)}) copy-start(bf16[2,2880,180]{1,0,2:T(2,128)(2,1)} %param.26) | copy-start | bytes 6220804
  27.3 6.9 %collective-permute-start.3 = (bf16[16,2944]{1,0:T(8,128)(2,1)S(1)}, bf16[16,2944]{1,0:T(8,128)(2,1)S(1)}, u32[]{:S(2)}, u32[]{:S(2)}) collective-permute-start(bf16[16,2944]{1,0:T(8,128)(2,1)S(1)} %get-tuple-element.54), channel_id=1, source_target_pairs={{0,4},{4,0},{8,12},{12,8},{1,5},{5,1},{9,13},{13,9},{2,6},{6,2},{1... | collective-permute-start | bytes 282632 | tf_op jit(solution)/shard_map/ppermute | solution.py:378
  34.2 9.0 %collective-permute-start.4 = (bf16[16,2944]{1,0:T(8,128)(2,1)S(1)}, bf16[16,2944]{1,0:T(8,128)(2,1)S(1)}, u32[]{:S(2)}, u32[]{:S(2)}) collective-permute-start(bf16[16,2944]{1,0:T(8,128)(2,1)S(1)} %get-tuple-element.61), channel_id=1, source_target_pairs={{0,8},{4,12},{8,0},{12,4},{1,9},{5,13},{9,1},{13,5},{2,10},{6,14},... | collective-permute-start | bytes 282632 | tf_op jit(solution)/shard_map/ppermute | solution.py:382
  45.2 28.5 %all-to-all-start.1 = ((bf16[16,16,2944]{2,1,0:T(8,128)(2,1)}), bf16[16,16,2944]{2,1,0:T(8,128)(2,1)S(1)}, u32[]{:S(2)}, u32[]{:S(2)}) async-start(bf16[16,16,2944]{2,1,0:T(8,128)(2,1)} %get-tuple-element.69), calls=%async_computation.1 | async-start | bytes 3014656 | tf_op jit(solution)/shard_map/all_to_all | solution.py:330

commit v9 on v8

--- a/solution.py
+++ b/solution.py
@@ -223,9 +223,13 @@
     )(keep, got)
 
 
-def norm_kernel(place_ref, keep_ref, got_ref, gain_ref, res_ref, out_hbm, full_ref, sems):
+def norm_kernel(
+    place_ref, keep_ref, near_ref, back_ref, far_ref, gain_ref, res_ref, out_hbm, full_ref, sems
+):
     steps, width = res_ref.shape
-    total = keep_ref[...] + got_ref[...].astype(F32)
+    total = keep_ref[...]
+    for ref in (near_ref, back_ref, far_ref):
+        total = total + ref[...].astype(F32)
     res = total[:, :width]
     scale = lax.rsqrt(jnp.sum(res * res, axis=1, keepdims=True) / width + 1e-05)
     normed = (res * scale * gain_ref[...]).astype(BF16)
@@ -249,7 +253,7 @@
     width = gain.shape[1]
     return pl.pallas_call(
         norm_kernel,
-        in_specs=[smem(), vmem(), vmem(), vmem()],
+        in_specs=[smem()] + [vmem()] * 5,
         out_specs=[vmem(), hbm()],
         out_shape=[
             jax.ShapeDtypeStruct((steps, width), F32),
@@ -258,7 +262,7 @@
         scratch_shapes=[pltpu.VMEM((rows, wide), BF16), pltpu.SemaphoreType.DMA((copies,))],
         compiler_params=params(12),
         name="norm",
-    )(place, keep, got, gain)
+    )(place, keep, *got, gain)
 
 
 def experts_kernel(
@@ -374,15 +378,18 @@
     far_gate, far_up = lax.ppermute(gate, "c", SWAP), lax.ppermute(up, "c", SWAP)
     got, gain, down = lax.optimization_barrier((got, gain[None], row_major(down)))
     keep, sent = join(keep, got)
-    sent, far_down = lax.optimization_barrier((sent, far_down))
-    got = lax.ppermute(sent, "w", [(i, i ^ 1) for i in range(nz // 2)])
-    got, far_down = lax.optimization_barrier((got, row_major(far_down)))
-    keep, sent = join(keep, got)
-    sent, gate, up = lax.optimization_barrier((sent, gate, up))
-    got = lax.ppermute(sent, "w", [(i, i ^ 2) for i in range(nz // 2)])
-    got, gate, up = lax.optimization_barrier(
-        (got, row_major(gate.swapaxes(1, 2)), row_major(up.swapaxes(1, 2)))
-    )
+    sent, far_down, gate, up = lax.optimization_barrier((sent, far_down, gate, up))
+    quarter = nz // 2
+    got = [
+        lax.ppermute(sent, "w", [(i, (i + k) % quarter) for i in range(quarter)])
+        for k in range(1, quarter)
+    ]
+    far_down, gate, up = (
+        row_major(far_down),
+        row_major(gate.swapaxes(1, 2)),
+        row_major(up.swapaxes(1, 2)),
+    )
+    far_down, gate, up, *got = lax.optimization_barrier((far_down, gate, up, *got))
     residual, copies = norm(place, keep, got, gain, ndp, steps)
     copies, far_gate, far_up = lax.optimization_barrier((copies, far_gate, far_up))
     tokens = exchange(copies, dp)

time: 118 us -> 119 us (level)
  waiting for transfers between devices: 25.9 us -> 18.9 us
  blocking collectives: 50.2 us -> 55.4 us
  starting transfers between devices: 10.5 us -> 13.3 us
    ppermute x2 -> x3, waiting for transfers between devices: 8.77 us -> 2.42 us  [on_device(): lax.ppermute(sent, 'w', [(i, (i + k) % quarter) for i in range(quarter)])]
    all_to_all x3, blocking collectives: 50.2 us -> 55.4 us  [exchange(): return lax.all_to_all(value, axis, split_axis=0, concat_axis=0, tiled=True)]
    ppermute x2 -> x3, starting transfers between devices: 1.37 us -> 4.23 us  [on_device(): lax.ppermute(sent, 'w', [(i, (i + k) % quarter) for i in range(quarter)])]
  transfers between devices with their start and end apart: 8 -> 9, of which waited for: 4 -> 5; matrix products, arithmetic and copies ran while one was open for 12% -> 12% of each run, Pallas kernels for 5% -> 5%
where the time goes in v9:
time: 119 us; the launch traced here: 118 us
  blocking collectives  55.4 us (47%)
  waiting for transfers between devices  18.9 us (16%)
  Pallas kernels  15 us (13%)
  local copies, waits for them, and re-layouts  13.8 us (12%)
  starting transfers between devices  13.3 us (11%)
    all_to_all x3, blocking collectives, exchange(): return lax.all_to_all(value, axis, split_axis=0, concat_axis=0, tiled=True)  55.4 us
    all_to_all x1, waiting for transfers between devices, exchange(): return lax.all_to_all(value, axis, split_axis=0, concat_axis=0, tiled=True)  14 us
    pallas_call x1, Pallas kernels, experts(): pl.pallas_call(experts_kernel, in_specs=[smem(), vmem()] + [hbm()] * 6, o...  8.55 us
    all_to_all x1, starting transfers between devices, exchange(): return lax.all_to_all(value, axis, split_axis=0, concat_axis=0, tiled=True)  7.41 us
    optimization_barrier x2, local copies, waits for them, and re-layouts, on_device(): lax.optimization_barrier((copies, far_gate, far_up))  6.42 us
    ppermute x3, starting transfers between devices, on_device(): lax.ppermute(sent, 'w', [(i, (i + k) % quarter) for i in range(quarter)])  4.23 us
    optimization_barrier x1, local copies, waits for them, and re-layouts, on_device(): lax.optimization_barrier((sent, far_down, gate, up))  3.22 us
    transpose x1, local copies, waits for them, and re-layouts, on_device(): up.swapaxes(1, 2)  2.51 us
  transfers between devices with their start and end apart: 9, of which 5 were waited for; matrix products, arithmetic and copies ran while one was open for 12% of the time, Pallas kernels for 5%

profile of v9, /device:TPU:8, one launch (start us, length us, event | category | flops | bytes accessed | tf_op | source)
XLA Modules:
  0.0 118.2 jit_solution(9923721564099925567)
XLA Ops:
  0.0 0.0 collective-permute-start
  0.0 0.5 collective-permute-start.2
  1.2 0.0 copy-start.1
  1.2 2.2 %attend.1 = (bf16[8,2,512]{2,1,0:T(2,128)(2,1)S(1)}, bf16[2880,256]{1,0:T(8,128)(2,1)S(1)}) custom-call(s32[1]{0:T(128)S(6)} %copy.61.len_ref, bf16[1,2,4096]{2,1,0:T(2,128)(2,1)} %q_hbm.1, bf16[1,2,512]{2,1,0:T(2,128)(2,1)} %nk_hbm.1, bf16[1,2,512]{2,1,0:T(2,128)(2,1)} %nv_hbm.1, bf16[1,512,512]{2,1,0:T(8,128)(2,1)} %k_hbm.1, bf16[1,512,512]{2,1,0:T(8,128)(2,1)} %v_hbm.1, ...), custom_call_target="tpu_custom_call" | custom-call | tf_op jit(solution)/shard_map/attend/pallas_call | solution.py:104
  3.4 0.0 copy-start.3
  3.4 0.0 copy-start
  3.4 0.1 pad_add_fusion.1.first_ref
  3.5 0.1 pad_add_fusion.place_ref
  3.6 16.2 %all_to_all.20.x_ref = bf16[8,2,512]{2,1,0:T(2,128)(2,1)S(1)} all-to-all(bf16[8,2,512]{2,1,0:T(2,128)(2,1)S(1)} %get-tuple-element.42), channel_id=1, replica_groups=mesh['x'=4,'y'=4,'w'=4,'v'=2,'c'=2] {'w','v'}, dimensions={0} | all-to-all | bytes 32768 | tf_op jit(solution)/shard_map/all_to_all | solution.py:334
  19.7 0.0 collective-permute-done.other_ref
  19.7 2.2 %project.1 = (f32[16,2944]{1,0:T(8,128)S(1)}, bf16[16,2944]{1,0:T(8,128)(2,1)S(1)}) custom-call(s32[3]{0:T(128)S(1)} %pad_add_fusion.place_ref, bf16[8,2,512]{2,1,0:T(2,128)(2,1)S(1)} %all_to_all.20.x_ref, bf16[2880,256]{1,0:T(8,128)(2,1)S(1)} %get-tuple-element.43.own_ref, bf16[2880,256]{1,0:T(8,128)(2,1)S(1)} %collective-permute-done.other_ref, ...), custom_call_target="tpu_custom_call" | custom-call | tf_op jit(solution)/shard_map/project/pallas_call | solution.py:186
  21.9 0.0 copy-done.1
  21.9 0.1 collective-permute-start.6
  22.0 0.5 collective-permute-start.7
  22.5 0.6 collective-permute-start.1
  23.1 0.0 copy-done.3
  23.2 0.0 copy-done
  23.2 0.0 copy-start.2
  23.2 1.6 %copy.47.d0_hbm = bf16[2,180,2880]{2,1,0:T(8,128)(2,1)} copy(bf16[2,180,2880]{2,0,1:T(2,128)(2,1)S(1)} %copy-done) | data formatting | bytes 4147200 | tf_op jit(solution)/shard_map/optimization_barrier | solution.py:374
  24.8 2.5 %collective-permute-done.1.got_ref = bf16[16,2944]{1,0:T(8,128)(2,1)S(1)} collective-permute-done((bf16[16,2944]{1,0:T(8,128)(2,1)S(1)}, bf16[16,2944]{1,0:T(8,128)(2,1)S(1)}, u32[]{:S(2)}, u32[]{:S(2)}) %collective-permute-start.1) | collective-permute-done | bytes 94240 | tf_op jit(solution)/shard_map/ppermute | solution.py:377
  27.3 0.0 collective-permute-done.2
  27.3 0.7 collective-permute-start.5
  28.0 3.5 %collective-permute-start.4 = (bf16[16,2944]{1,0:T(8,128)(2,1)S(1)}, bf16[16,2944]{1,0:T(8,128)(2,1)S(1)}, u32[]{:S(2)}, u32[]{:S(2)}) collective-permute-start(bf16[16,2944]{1,0:T(8,128)(2,1)S(1)} %get-tuple-element.57), channel_id=1, source_target_pairs={{0,8},{4,12},{8,0},{12,4},{1,9},{5,13},{9,1},{13,5},{2,10},{6,14},... | collective-permute-start | bytes 282632 | tf_op jit(solution)/shard_map/ppermute | solution.py:384
  31.5 0.0 collective-permute-start.3
  31.5 0.0 copy-done.2
  31.5 2.5 %copy_bitcast_fusion.2 = (bf16[2,180,2880]{2,1,0:T(8,128)(2,1)}, bf16[2,180,2880]{2,1,0:T(8,128)(2,1)}) fusion(bf16[2,2880,180]{1,0,2:T(2,128)(2,1)S(1)} %copy-done.2, bf16[2,2880,180]{1,0,2:T(2,128)(2,1)S(1)} %copy-done.1), kind=kLoop, calls=%fused_computation.2 | loop fusion | bytes 8294400 | tf_op jit(solution)/shard_map/transpose | solution.py:390
  34.0 3.2 %copy.48.d1_hbm = bf16[2,180,2880]{2,1,0:T(8,128)(2,1)} copy(bf16[2,180,2880]{2,0,1:T(2,128)(2,1)} %collective-permute-done.2) | data formatting | bytes 4147200 | tf_op jit(solution)/shard_map/optimization_barrier | solution.py:381
  37.2 0.7 collective-permute-done.5.far_ref
  37.9 0.1 collective-permute-done.4.back_ref
  38.0 1.6 %collective-permute-done.3.near_ref = bf16[16,2944]{1,0:T(8,128)(2,1)S(1)} collective-permute-done((bf16[16,2944]{1,0:T(8,128)(2,1)S(1)}, bf16[16,2944]{1,0:T(8,128)(2,1)S(1)}, u32[]{:S(2)}, u32[]{:S(2)}) %collective-permute-start.3) | collective-permute-done | bytes 94240 | tf_op jit(solution)/shard_map/ppermute | solution.py:384
  39.7 2.0 %norm.1 = (f32[2,2880]{1,0:T(2,128)S(1)}, bf16[16,16,2944]{2,1,0:T(8,128)(2,1)}) custom-call(s32[3]{0:T(128)S(1)} %pad_add_fusion.place_ref, f32[16,2944]{1,0:T(8,128)S(1)} %get-tuple-element.50.keep_ref, bf16[16,2944]{1,0:T(8,128)(2,1)S(1)} %collective-permute-done.3.near_ref, bf16[16,2944]{1,0:T(8,128)(2,1)S(1)} %collective-permute-done.4.back_ref, ...), custom_call_target="tpu_custom_call" | custom-call | tf_op jit(solution)/shard_map/norm/pallas_call | solution.py:254
  41.7 0.0 collective-permute-done.6
  41.7 0.0 collective-permute-done.7
  41.7 7.4 %all-to-all-start.1 = ((bf16[16,16,2944]{2,1,0:T(8,128)(2,1)}), bf16[16,16,2944]{2,1,0:T(8,128)(2,1)S(1)}, u32[]{:S(2)}, u32[]{:S(2)}) async-start(bf16[16,16,2944]{2,1,0:T(8,128)(2,1)} %get-tuple-element.65), calls=%async_computation.1 | async-start | bytes 3014656 | tf_op jit(solution)/shard_map/all_to_all | solution.py:334
  49.1 3.2 %copy.60 = bf16[2,2880,180]{1,2,0:T(8,128)(2,1)} copy(bf16[2,2880,180]{1,0,2:T(2,128)(2,1)} %collective-permute-done.6) | data formatting | bytes 4147200 | tf_op jit(solution)/shard_map/optimization_barrier | solution.py:394
  52.3 3.2 %copy.59 = bf16[2,2880,180]{1,2,0:T(8,128)(2,1)} copy(bf16[2,2880,180]{1,0,2:T(2,128)(2,1)} %collective-permute-done.7) | data formatting | bytes 4147200 | tf_op jit(solution)/shard_map/optimization_barrier | solution.py:394
  55.5 14.0 %all-to-all-done.1 = bf16[16,16,2944]{2,1,0:T(8,128)(2,1)S(1)} async-done(((bf16[16,16,2944]{2,1,0:T(8,128)(2,1)}), bf16[16,16,2944]{2,1,0:T(8,128)(2,1)S(1)}, u32[]{:S(2)}, u32[]{:S(2)}) %all-to-all-start.1) | async-done | bytes 1507360 | tf_op jit(solution)/shard_map/all_to_all | solution.py:334
  69.5 8.5 %experts.1 = bf16[256,2880]{1,0:T(8,128)(2,1)S(1)} custom-call(s32[2]{0:T(128)S(1)} %pad_add_fusion.1.first_ref, bf16[256,2944]{1,0:T(8,128)(2,1)S(1)} %bitcast.22, bf16[2,180,2880]{2,1,0:T(8,128)(2,1)} %get-tuple-element.69.g0_hbm, bf16[2,180,2880]{2,1,0:T(8,128)(2,1)} %get-tuple-element.70.u0_hbm, bf16[2,180,2880]{2,1,0:T(8,128)(2,1)} %bitcast.24, ...), custom_call_target="tpu_custom_call" | custom-call | tf_op jit(solution)/shard_map/experts/pallas_call | solution.py:317
  78.1 23.2 %all_to_all.21 = bf16[16,16,2880]{2,1,0:T(8,128)(2,1)S(1)} all-to-all(bf16[16,16,2880]{2,1,0:T(8,128)(2,1)S(1)} %bitcast.23), channel_id=1, replica_groups=mesh['x'=4,'y'=4,'w'=4,'v'=2,'c'=2] {'x','y'}, dimensions={0} | all-to-all | bytes 2949120 | tf_op jit(solution)/shard_map/all_to_all | solution.py:334
  101.3 0.2 reduce_sum.21
  101.5 16.0 %all_to_all.22 = bf16[8,2,2880]{2,1,0:T(2,128)(2,1)S(1)} all-to-all(bf16[8,2,2880]{2,1,0:T(2,128)(2,1)S(1)} %reshape.11), channel_id=1, replica_groups=mesh['x'=4,'y'=4,'w'=4,'v'=2,'c'=2] {'w','v'}, dimensions={0} | all-to-all | bytes 184320 | tf_op jit(solution)/shard_map/all_to_all | solution.py:334
  117.5 0.1 convert_reduce_fusion
  117.6 0.6 fusion
  (3 shorter events, 0.1 us)
Async XLA Ops:
  0.0 19.7 %collective-permute-start = (bf16[2880,256]{1,0:T(8,128)(2,1)}, bf16[2880,256]{1,0:T(8,128)(2,1)S(1)}, u32[]{:S(2)}, u32[]{:S(2)}) collective-permute-start(bf16[2880,256]{1,0:T(8,128)(2,1)} %bitcast.26), channel_id=1, source_target_pairs={{0,1},{1,0},{2,3},{3,2},{4,5},{5,4},{6,7},{7,6},{8,9},{9,8},{10,11... | collective-permute-start | bytes 4423688 | tf_op jit(solution)/shard_map/ppermute | solution.py:363
  0.0 27.3 %collective-permute-start.2 = (bf16[2,180,2880]{2,0,1:T(2,128)(2,1)}, bf16[2,180,2880]{2,0,1:T(2,128)(2,1)}, u32[]{:S(2)}, u32[]{:S(2)}) collective-permute-start(bf16[2,180,2880]{2,0,1:T(2,128)(2,1)} %param.27), channel_id=1, source_target_pairs={{0,1},{1,0},{2,3},{3,2},{4,5},{5,4},{6,7},{7,6},{8,9},{9,8},{10,11... | collective-permute-start | bytes 6220808 | tf_op jit(solution)/shard_map/ppermute | solution.py:364
  1.2 20.8 %copy-start.1 = (bf16[2,2880,180]{1,0,2:T(2,128)(2,1)S(1)}, bf16[2,2880,180]{1,0,2:T(2,128)(2,1)}, u32[]{:S(2)}) copy-start(bf16[2,2880,180]{1,0,2:T(2,128)(2,1)} %param.25) | copy-start | bytes 6220804
  3.4 19.7 %copy-start.3 = (f32[2880]{0:T(1024)S(1)}, f32[2880]{0:T(1024)}, u32[]{:S(2)}) copy-start(f32[2880]{0:T(1024)} %param.22) | copy-start | bytes 34564
  3.4 19.7 %copy-start = (bf16[2,180,2880]{2,0,1:T(2,128)(2,1)S(1)}, bf16[2,180,2880]{2,0,1:T(2,128)(2,1)}, u32[]{:S(2)}) copy-start(bf16[2,180,2880]{2,0,1:T(2,128)(2,1)} %param.27) | copy-start | bytes 6220804
  21.9 19.8 %collective-permute-start.6 = (bf16[2,2880,180]{1,0,2:T(2,128)(2,1)S(1)}, bf16[2,2880,180]{1,0,2:T(2,128)(2,1)}, u32[]{:S(2)}, u32[]{:S(2)}) collective-permute-start(bf16[2,2880,180]{1,0,2:T(2,128)(2,1)S(1)} %copy-done.1), channel_id=1, source_target_pairs={{0,1},{1,0},{2,3},{3,2},{4,5},{5,4},{6,7},{7,6},{8,9},{9,8},{10,11... | collective-permute-start | bytes 6220808 | tf_op jit(solution)/shard_map/ppermute | solution.py:378
  22.0 19.7 %collective-permute-start.7 = (bf16[2,2880,180]{1,0,2:T(2,128)(2,1)}, bf16[2,2880,180]{1,0,2:T(2,128)(2,1)}, u32[]{:S(2)}, u32[]{:S(2)}) collective-permute-start(bf16[2,2880,180]{1,0,2:T(2,128)(2,1)} %param.26), channel_id=1, source_target_pairs={{0,1},{1,0},{2,3},{3,2},{4,5},{5,4},{6,7},{7,6},{8,9},{9,8},{10,11... | collective-permute-start | bytes 6220808 | tf_op jit(solution)/shard_map/ppermute | solution.py:378
  22.5 4.7 %collective-permute-start.1 = (bf16[16,2944]{1,0:T(8,128)(2,1)S(1)}, bf16[16,2944]{1,0:T(8,128)(2,1)S(1)}, u32[]{:S(2)}, u32[]{:S(2)}) collective-permute-start(bf16[16,2944]{1,0:T(8,128)(2,1)S(1)} %get-tuple-element.46), channel_id=1, source_target_pairs={{0,2},{2,0},{1,3},{3,1},{4,6},{6,4},{5,7},{7,5},{8,10},{10,8},{9,1... | collective-permute-start | bytes 282632 | tf_op jit(solution)/shard_map/ppermute | solution.py:377
  23.2 8.4 %copy-start.2 = (bf16[2,2880,180]{1,0,2:T(2,128)(2,1)S(1)}, bf16[2,2880,180]{1,0,2:T(2,128)(2,1)}, u32[]{:S(2)}) copy-start(bf16[2,2880,180]{1,0,2:T(2,128)(2,1)} %param.26) | copy-start | bytes 6220804
  27.3 10.6 %collective-permute-start.5 = (bf16[16,2944]{1,0:T(8,128)(2,1)S(1)}, bf16[16,2944]{1,0:T(8,128)(2,1)S(1)}, u32[]{:S(2)}, u32[]{:S(2)}) collective-permute-start(bf16[16,2944]{1,0:T(8,128)(2,1)S(1)} %get-tuple-element.57), channel_id=1, source_target_pairs={{0,12},{4,0},{8,4},{12,8},{1,13},{5,1},{9,5},{13,9},{2,14},{6,2},{... | collective-permute-start | bytes 282632 | tf_op jit(solution)/shard_map/ppermute | solution.py:384
  28.0 10.0 %collective-permute-start.4 = (bf16[16,2944]{1,0:T(8,128)(2,1)S(1)}, bf16[16,2944]{1,0:T(8,128)(2,1)S(1)}, u32[]{:S(2)}, u32[]{:S(2)}) collective-permute-start(bf16[16,2944]{1,0:T(8,128)(2,1)S(1)} %get-tuple-element.57), channel_id=1, source_target_pairs={{0,8},{4,12},{8,0},{12,4},{1,9},{5,13},{9,1},{13,5},{2,10},{6,14},... | collective-permute-start | bytes 282632 | tf_op jit(solution)/shard_map/ppermute | solution.py:384
  31.5 8.2 %collective-permute-start.3 = (bf16[16,2944]{1,0:T(8,128)(2,1)S(1)}, bf16[16,2944]{1,0:T(8,128)(2,1)S(1)}, u32[]{:S(2)}, u32[]{:S(2)}) collective-permute-start(bf16[16,2944]{1,0:T(8,128)(2,1)S(1)} %get-tuple-element.57), channel_id=1, source_target_pairs={{0,4},{4,8},{8,12},{12,0},{1,5},{5,9},{9,13},{13,1},{2,6},{6,10},{... | collective-permute-start | bytes 282632 | tf_op jit(solution)/shard_map/ppermute | solution.py:384
  41.7 27.8 %all-to-all-start.1 = ((bf16[16,16,2944]{2,1,0:T(8,128)(2,1)}), bf16[16,16,2944]{2,1,0:T(8,128)(2,1)S(1)}, u32[]{:S(2)}, u32[]{:S(2)}) async-start(bf16[16,16,2944]{2,1,0:T(8,128)(2,1)} %get-tuple-element.65), calls=%async_computation.1 | async-start | bytes 3014656 | tf_op jit(solution)/shard_map/all_to_all | solution.py:334

commit v10 on v9

--- a/solution.py
+++ b/solution.py
@@ -298,7 +298,7 @@
             acts.append((act * share).astype(BF16))
     copies[4].wait()
     copies[5].wait()
-    chunk = 768
+    chunk = 1536
     for start in range(0, width, chunk):
         stop = min(start + chunk, width)
         part = None
@@ -361,7 +361,9 @@
     per = gate_weight.shape[0]
     out_rows = out_weight.T
     other_out = lax.ppermute(out_rows, "c", SWAP)
-    far_down = lax.ppermute(down_weight, "c", SWAP)
+    far_down, far_gate, far_up = (
+        lax.ppermute(w, "c", SWAP) for w in (down_weight, gate_weight, up_weight)
+    )
     attended, own_out = attend(
         prompt_lengths, queries, new_keys, new_values, key_cache, value_cache, out_rows, nz
     )
@@ -371,31 +373,24 @@
     by_heads = exchange(attended, zaxis)
     ids, logits = expert_ids.transpose(1, 2, 0), top_logits.transpose(1, 2, 0)
     keep, sent = project(place, by_heads, hidden_in, ids, logits, own_out, other_out)
-    sent, gain, down, gate, up = lax.optimization_barrier(
-        (sent, norm_gain, down_weight, gate_weight, up_weight)
-    )
+    sent, gain, down = lax.optimization_barrier((sent, norm_gain, down_weight))
     got = lax.ppermute(sent, "v", SWAP)
-    far_gate, far_up = lax.ppermute(gate, "c", SWAP), lax.ppermute(up, "c", SWAP)
     got, gain, down = lax.optimization_barrier((got, gain[None], row_major(down)))
     keep, sent = join(keep, got)
-    sent, far_down, gate, up = lax.optimization_barrier((sent, far_down, gate, up))
+    sent, far_down = lax.optimization_barrier((sent, far_down))
     quarter = nz // 2
     got = [
         lax.ppermute(sent, "w", [(i, (i + k) % quarter) for i in range(quarter)])
         for k in range(1, quarter)
     ]
-    far_down, gate, up = (
-        row_major(far_down),
-        row_major(gate.swapaxes(1, 2)),
-        row_major(up.swapaxes(1, 2)),
-    )
-    far_down, gate, up, *got = lax.optimization_barrier((far_down, gate, up, *got))
+    far_down, *got = lax.optimization_barrier((row_major(far_down), *got))
     residual, copies = norm(place, keep, got, gain, ndp, steps)
-    copies, far_gate, far_up = lax.optimization_barrier((copies, far_gate, far_up))
+    copies, *weights = lax.optimization_barrier(
+        (copies, gate_weight, up_weight, far_gate, far_up)
+    )
     tokens = exchange(copies, dp)
-    tokens, far_gate, far_up = lax.optimization_barrier(
-        (tokens, row_major(far_gate.swapaxes(1, 2)), row_major(far_up.swapaxes(1, 2)))
-    )
+    relaid = [row_major(w.swapaxes(1, 2)) for w in weights]
+    tokens, gate, up, far_gate, far_up = lax.optimization_barrier((tokens, *relaid))
     tokens = tokens.reshape(ndp * nz * steps, -1)
     made = experts(first, tokens, (gate, up, down), (far_gate, far_up, far_down))
     back = exchange(made.reshape(ndp, nz * steps, width), dp)

time: 119 us -> 113 us (0.950)
  blocking collectives: 55.4 us -> 52.9 us
  local copies, waits for them, and re-layouts: 13.8 us -> 12.3 us
  waiting for transfers between devices: 18.9 us -> 17.7 us
    optimization_barrier x4 -> x2, local copies, waits for them, and re-layouts: 11.2 us -> 4.7 us  [the longest x1 3.13 us: on_device(): sent, far_down = lax.optimization_barrier((sent, far_down))]
    transpose x1 -> x2, local copies, waits for them, and re-layouts: 2.51 us -> 7.53 us  [on_device(): relaid = [row_major(w.swapaxes(1, 2)) for w in weights]]
    all_to_all x1, waiting for transfers between devices: 14 us -> 11 us  [exchange(): return lax.all_to_all(value, axis, split_axis=0, concat_axis=0, tiled=True)]
    all_to_all x3, blocking collectives: 55.4 us -> 52.9 us  [exchange(): return lax.all_to_all(value, axis, split_axis=0, concat_axis=0, tiled=True)]
    ppermute x3, waiting for transfers between devices: 2.42 us -> 4.4 us  [on_device(): lax.ppermute(sent, 'w', [(i, (i + k) % quarter) for i in range(quarter)])]
  transfers between devices with their start and end apart: 9 -> 9, of which waited for: 5 -> 5; matrix products, arithmetic and copies ran while one was open for 12% -> 11% of each run, Pallas kernels for 5% -> 6%
where the time goes in v10:
time: 113 us
  blocking collectives  52.9 us (47%)
  waiting for transfers between devices  17.7 us (16%)
  Pallas kernels  14.3 us (13%)
  starting transfers between devices  14 us (12%)
  local copies, waits for them, and re-layouts  12.3 us (11%)
    all_to_all x3, blocking collectives, exchange(): return lax.all_to_all(value, axis, split_axis=0, concat_axis=0, tiled=True)  52.9 us
    all_to_all x1, waiting for transfers between devices, exchange(): return lax.all_to_all(value, axis, split_axis=0, concat_axis=0, tiled=True)  11 us
    pallas_call x1, Pallas kernels, experts(): pl.pallas_call(experts_kernel, in_specs=[smem(), vmem()] + [hbm()] * 6, o...  8 us
    transpose x2, local copies, waits for them, and re-layouts, on_device(): relaid = [row_major(w.swapaxes(1, 2)) for w in weights]  7.53 us
    all_to_all x1, starting transfers between devices, exchange(): return lax.all_to_all(value, axis, split_axis=0, concat_axis=0, tiled=True)  7.41 us
    ppermute x3, starting transfers between devices, on_device(): lax.ppermute(sent, 'w', [(i, (i + k) % quarter) for i in range(quarter)])  4.83 us
    ppermute x3, waiting for transfers between devices, on_device(): lax.ppermute(sent, 'w', [(i, (i + k) % quarter) for i in range(quarter)])  4.4 us
    optimization_barrier x1, local copies, waits for them, and re-layouts, on_device(): sent, far_down = lax.optimization_barrier((sent, far_down))  3.13 us
  transfers between devices with their start and end apart: 9, of which 5 were waited for; matrix products, arithmetic and copies ran while one was open for 11% of the time, Pallas kernels for 6%

profile of v10, /device:TPU:8, one launch (start us, length us, event | category | flops | bytes accessed | tf_op | source)
XLA Modules:
  0.0 113.0 jit_solution(11917315333614286122)
XLA Ops:
  0.0 0.0 collective-permute-start.2
  0.0 0.5 collective-permute-start.6
  0.5 0.0 collective-permute-start.7
  0.5 0.5 collective-permute-start
  1.7 2.1 %attend.1 = (bf16[8,2,512]{2,1,0:T(2,128)(2,1)S(1)}, bf16[2880,256]{1,0:T(8,128)(2,1)S(1)}) custom-call(s32[1]{0:T(128)S(6)} %copy.59.len_ref, bf16[1,2,4096]{2,1,0:T(2,128)(2,1)} %q_hbm.1, bf16[1,2,512]{2,1,0:T(2,128)(2,1)} %nk_hbm.1, bf16[1,2,512]{2,1,0:T(2,128)(2,1)} %nv_hbm.1, bf16[1,512,512]{2,1,0:T(8,128)(2,1)} %k_hbm.1, bf16[1,512,512]{2,1,0:T(8,128)(2,1)} %v_hbm.1, ...), custom_call_target="tpu_custom_call" | custom-call | tf_op jit(solution)/shard_map/attend/pallas_call | solution.py:104
  3.7 0.0 copy-start
  3.8 0.1 pad_add_fusion.1.first_ref
  3.8 0.1 pad_add_fusion.place_ref
  3.9 16.2 %all_to_all.20.x_ref = bf16[8,2,512]{2,1,0:T(2,128)(2,1)S(1)} all-to-all(bf16[8,2,512]{2,1,0:T(2,128)(2,1)S(1)} %get-tuple-element.40), channel_id=1, replica_groups=mesh['x'=4,'y'=4,'w'=4,'v'=2,'c'=2] {'w','v'}, dimensions={0} | all-to-all | bytes 32768 | tf_op jit(solution)/shard_map/all_to_all | solution.py:334
  20.1 0.0 collective-permute-done.other_ref
  20.1 2.2 %project.1 = (f32[16,2944]{1,0:T(8,128)S(1)}, bf16[16,2944]{1,0:T(8,128)(2,1)S(1)}) custom-call(s32[3]{0:T(128)S(1)} %pad_add_fusion.place_ref, bf16[8,2,512]{2,1,0:T(2,128)(2,1)S(1)} %all_to_all.20.x_ref, bf16[2880,256]{1,0:T(8,128)(2,1)S(1)} %get-tuple-element.41.own_ref, bf16[2880,256]{1,0:T(8,128)(2,1)S(1)} %collective-permute-done.other_ref, ...), custom_call_target="tpu_custom_call" | custom-call | tf_op jit(solution)/shard_map/project/pallas_call | solution.py:186
  22.3 0.0 copy-start.3
  22.3 0.7 collective-permute-start.1
  23.0 0.0 copy-done
  23.0 1.6 %copy.47.d0_hbm = bf16[2,180,2880]{2,1,0:T(8,128)(2,1)} copy(bf16[2,180,2880]{2,0,1:T(2,128)(2,1)S(1)} %copy-done) | data formatting | bytes 4147200 | tf_op jit(solution)/shard_map/optimization_barrier | solution.py:376
  24.5 0.0 copy-done.3
  24.6 2.4 %collective-permute-done.1.got_ref = bf16[16,2944]{1,0:T(8,128)(2,1)S(1)} collective-permute-done((bf16[16,2944]{1,0:T(8,128)(2,1)S(1)}, bf16[16,2944]{1,0:T(8,128)(2,1)S(1)}, u32[]{:S(2)}, u32[]{:S(2)}) %collective-permute-start.1) | collective-permute-done | bytes 94240 | tf_op jit(solution)/shard_map/ppermute | solution.py:377
  27.0 0.0 collective-permute-done.2
  27.0 0.7 collective-permute-start.3
  27.6 2.4 %collective-permute-start.4 = (bf16[16,2944]{1,0:T(8,128)(2,1)S(1)}, bf16[16,2944]{1,0:T(8,128)(2,1)S(1)}, u32[]{:S(2)}, u32[]{:S(2)}) collective-permute-start(bf16[16,2944]{1,0:T(8,128)(2,1)S(1)} %get-tuple-element.51), channel_id=1, source_target_pairs={{0,8},{4,12},{8,0},{12,4},{1,9},{5,13},{9,1},{13,5},{2,10},{6,14},... | collective-permute-start | bytes 282632 | tf_op jit(solution)/shard_map/ppermute | solution.py:383
  30.1 1.8 %collective-permute-start.5 = (bf16[16,2944]{1,0:T(8,128)(2,1)S(1)}, bf16[16,2944]{1,0:T(8,128)(2,1)S(1)}, u32[]{:S(2)}, u32[]{:S(2)}) collective-permute-start(bf16[16,2944]{1,0:T(8,128)(2,1)S(1)} %get-tuple-element.51), channel_id=1, source_target_pairs={{0,12},{4,0},{8,4},{12,8},{1,13},{5,1},{9,5},{13,9},{2,14},{6,2},{... | collective-permute-start | bytes 282632 | tf_op jit(solution)/shard_map/ppermute | solution.py:383
  31.8 3.1 %copy.48.d1_hbm = bf16[2,180,2880]{2,1,0:T(8,128)(2,1)} copy(bf16[2,180,2880]{2,0,1:T(2,128)(2,1)} %collective-permute-done.2) | data formatting | bytes 4147200 | tf_op jit(solution)/shard_map/optimization_barrier | solution.py:380
  34.9 0.2 collective-permute-done.3.near_ref
  35.1 2.4 %collective-permute-done.4.back_ref = bf16[16,2944]{1,0:T(8,128)(2,1)S(1)} collective-permute-done((bf16[16,2944]{1,0:T(8,128)(2,1)S(1)}, bf16[16,2944]{1,0:T(8,128)(2,1)S(1)}, u32[]{:S(2)}, u32[]{:S(2)}) %collective-permute-start.4) | collective-permute-done | bytes 94240 | tf_op jit(solution)/shard_map/ppermute | solution.py:383
  37.5 1.9 %collective-permute-done.5.far_ref = bf16[16,2944]{1,0:T(8,128)(2,1)S(1)} collective-permute-done((bf16[16,2944]{1,0:T(8,128)(2,1)S(1)}, bf16[16,2944]{1,0:T(8,128)(2,1)S(1)}, u32[]{:S(2)}, u32[]{:S(2)}) %collective-permute-start.5) | collective-permute-done | bytes 94240 | tf_op jit(solution)/shard_map/ppermute | solution.py:383
  39.3 2.0 %norm.1 = (f32[2,2880]{1,0:T(2,128)S(1)}, bf16[16,16,2944]{2,1,0:T(8,128)(2,1)}) custom-call(s32[3]{0:T(128)S(1)} %pad_add_fusion.place_ref, f32[16,2944]{1,0:T(8,128)S(1)} %get-tuple-element.48.keep_ref, bf16[16,2944]{1,0:T(8,128)(2,1)S(1)} %collective-permute-done.3.near_ref, bf16[16,2944]{1,0:T(8,128)(2,1)S(1)} %collective-permute-done.4.back_ref, ...), custom_call_target="tpu_custom_call" | custom-call | tf_op jit(solution)/shard_map/norm/pallas_call | solution.py:254
  41.3 0.0 collective-permute-done.6
  41.4 0.0 collective-permute-done.7
  41.4 7.4 %all-to-all-start.1 = ((bf16[16,16,2944]{2,1,0:T(8,128)(2,1)}), bf16[16,16,2944]{2,1,0:T(8,128)(2,1)S(1)}, u32[]{:S(2)}, u32[]{:S(2)}) async-start(bf16[16,16,2944]{2,1,0:T(8,128)(2,1)} %get-tuple-element.59), calls=%async_computation.1 | async-start | bytes 3014656 | tf_op jit(solution)/shard_map/all_to_all | solution.py:334
  48.8 0.0 copy-start.1
  48.8 0.0 copy-start.2
  48.8 4.9 %copy_bitcast_fusion = (bf16[2,180,2880]{2,1,0:T(8,128)(2,1)}, bf16[2,180,2880]{2,1,0:T(8,128)(2,1)}) fusion(bf16[2,2880,180]{1,0,2:T(2,128)(2,1)} %collective-permute-done.7, bf16[2,2880,180]{1,0,2:T(2,128)(2,1)} %collective-permute-done.6), kind=kLoop, calls=%fused_computation | loop fusion | bytes 8294400 | tf_op jit(solution)/shard_map/transpose | solution.py:392
  53.7 0.0 copy-done.1
  53.7 0.0 copy-done.2
  53.7 2.6 %copy_bitcast_fusion.2 = (bf16[2,180,2880]{2,1,0:T(8,128)(2,1)}, bf16[2,180,2880]{2,1,0:T(8,128)(2,1)}) fusion(bf16[2,2880,180]{1,0,2:T(2,128)(2,1)S(1)} %copy-done.1, bf16[2,2880,180]{1,0,2:T(2,128)(2,1)S(1)} %copy-done.2), kind=kLoop, calls=%fused_computation.2 | loop fusion | bytes 8294400 | tf_op jit(solution)/shard_map/transpose | solution.py:392
  56.3 11.0 %all-to-all-done.1 = bf16[16,16,2944]{2,1,0:T(8,128)(2,1)S(1)} async-done(((bf16[16,16,2944]{2,1,0:T(8,128)(2,1)}), bf16[16,16,2944]{2,1,0:T(8,128)(2,1)S(1)}, u32[]{:S(2)}, u32[]{:S(2)}) %all-to-all-start.1) | async-done | bytes 1507360 | tf_op jit(solution)/shard_map/all_to_all | solution.py:334
  67.3 8.0 %experts.1 = bf16[256,2880]{1,0:T(8,128)(2,1)S(1)} custom-call(s32[2]{0:T(128)S(1)} %pad_add_fusion.1.first_ref, bf16[256,2944]{1,0:T(8,128)(2,1)S(1)} %bitcast.20, bf16[2,180,2880]{2,1,0:T(8,128)(2,1)} %get-tuple-element.65.g0_hbm, bf16[2,180,2880]{2,1,0:T(8,128)(2,1)} %get-tuple-element.66.u0_hbm, bf16[2,180,2880]{2,1,0:T(8,128)(2,1)} %get-tuple-element.67.g1_hbm, ...), custom_call_target="tpu_custom_call" | custom-call | tf_op jit(solution)/shard_map/experts/pallas_call | solution.py:317
  75.3 23.0 %all_to_all.21 = bf16[16,16,2880]{2,1,0:T(8,128)(2,1)S(1)} all-to-all(bf16[16,16,2880]{2,1,0:T(8,128)(2,1)S(1)} %bitcast.21), channel_id=1, replica_groups=mesh['x'=4,'y'=4,'w'=4,'v'=2,'c'=2] {'x','y'}, dimensions={0} | all-to-all | bytes 2949120 | tf_op jit(solution)/shard_map/all_to_all | solution.py:334
  98.3 0.2 reduce_sum.21
  98.5 13.8 %all_to_all.22 = bf16[8,2,2880]{2,1,0:T(2,128)(2,1)S(1)} all-to-all(bf16[8,2,2880]{2,1,0:T(2,128)(2,1)S(1)} %reshape.11), channel_id=1, replica_groups=mesh['x'=4,'y'=4,'w'=4,'v'=2,'c'=2] {'w','v'}, dimensions={0} | all-to-all | bytes 184320 | tf_op jit(solution)/shard_map/all_to_all | solution.py:334
  112.3 0.1 convert_reduce_fusion
  112.4 0.6 fusion
  (3 shorter events, 0.1 us)
Async XLA Ops:
  0.0 27.0 %collective-permute-start.2 = (bf16[2,180,2880]{2,0,1:T(2,128)(2,1)}, bf16[2,180,2880]{2,0,1:T(2,128)(2,1)}, u32[]{:S(2)}, u32[]{:S(2)}) collective-permute-start(bf16[2,180,2880]{2,0,1:T(2,128)(2,1)} %param.27), channel_id=1, source_target_pairs={{0,1},{1,0},{2,3},{3,2},{4,5},{5,4},{6,7},{7,6},{8,9},{9,8},{10,11... | collective-permute-start | bytes 6220808 | tf_op jit(solution)/shard_map/ppermute | solution.py:365
  0.0 41.3 %collective-permute-start.6 = (bf16[2,2880,180]{1,0,2:T(2,128)(2,1)}, bf16[2,2880,180]{1,0,2:T(2,128)(2,1)}, u32[]{:S(2)}, u32[]{:S(2)}) collective-permute-start(bf16[2,2880,180]{1,0,2:T(2,128)(2,1)} %param.25), channel_id=1, source_target_pairs={{0,1},{1,0},{2,3},{3,2},{4,5},{5,4},{6,7},{7,6},{8,9},{9,8},{10,11... | collective-permute-start | bytes 6220808 | tf_op jit(solution)/shard_map/ppermute | solution.py:365
  0.5 40.8 %collective-permute-start.7 = (bf16[2,2880,180]{1,0,2:T(2,128)(2,1)}, bf16[2,2880,180]{1,0,2:T(2,128)(2,1)}, u32[]{:S(2)}, u32[]{:S(2)}) collective-permute-start(bf16[2,2880,180]{1,0,2:T(2,128)(2,1)} %param.26), channel_id=1, source_target_pairs={{0,1},{1,0},{2,3},{3,2},{4,5},{5,4},{6,7},{7,6},{8,9},{9,8},{10,11... | collective-permute-start | bytes 6220808 | tf_op jit(solution)/shard_map/ppermute | solution.py:365
  0.5 19.6 %collective-permute-start = (bf16[2880,256]{1,0:T(8,128)(2,1)}, bf16[2880,256]{1,0:T(8,128)(2,1)S(1)}, u32[]{:S(2)}, u32[]{:S(2)}) collective-permute-start(bf16[2880,256]{1,0:T(8,128)(2,1)} %bitcast.22), channel_id=1, source_target_pairs={{0,1},{1,0},{2,3},{3,2},{4,5},{5,4},{6,7},{7,6},{8,9},{9,8},{10,11... | collective-permute-start | bytes 4423688 | tf_op jit(solution)/shard_map/ppermute | solution.py:363
  3.7 19.2 %copy-start = (bf16[2,180,2880]{2,0,1:T(2,128)(2,1)S(1)}, bf16[2,180,2880]{2,0,1:T(2,128)(2,1)}, u32[]{:S(2)}) copy-start(bf16[2,180,2880]{2,0,1:T(2,128)(2,1)} %param.27) | copy-start | bytes 6220804
  22.3 2.3 %copy-start.3 = (f32[2880]{0:T(1024)S(1)}, f32[2880]{0:T(1024)}, u32[]{:S(2)}) copy-start(f32[2880]{0:T(1024)} %param.22) | copy-start | bytes 34564
  22.3 4.7 %collective-permute-start.1 = (bf16[16,2944]{1,0:T(8,128)(2,1)S(1)}, bf16[16,2944]{1,0:T(8,128)(2,1)S(1)}, u32[]{:S(2)}, u32[]{:S(2)}) collective-permute-start(bf16[16,2944]{1,0:T(8,128)(2,1)S(1)} %get-tuple-element.44), channel_id=1, source_target_pairs={{0,2},{2,0},{1,3},{3,1},{4,6},{6,4},{5,7},{7,5},{8,10},{10,8},{9,1... | collective-permute-start | bytes 282632 | tf_op jit(solution)/shard_map/ppermute | solution.py:377
  27.0 8.1 %collective-permute-start.3 = (bf16[16,2944]{1,0:T(8,128)(2,1)S(1)}, bf16[16,2944]{1,0:T(8,128)(2,1)S(1)}, u32[]{:S(2)}, u32[]{:S(2)}) collective-permute-start(bf16[16,2944]{1,0:T(8,128)(2,1)S(1)} %get-tuple-element.51), channel_id=1, source_target_pairs={{0,4},{4,8},{8,12},{12,0},{1,5},{5,9},{9,13},{13,1},{2,6},{6,10},{... | collective-permute-start | bytes 282632 | tf_op jit(solution)/shard_map/ppermute | solution.py:383
  27.6 9.9 %collective-permute-start.4 = (bf16[16,2944]{1,0:T(8,128)(2,1)S(1)}, bf16[16,2944]{1,0:T(8,128)(2,1)S(1)}, u32[]{:S(2)}, u32[]{:S(2)}) collective-permute-start(bf16[16,2944]{1,0:T(8,128)(2,1)S(1)} %get-tuple-element.51), channel_id=1, source_target_pairs={{0,8},{4,12},{8,0},{12,4},{1,9},{5,13},{9,1},{13,5},{2,10},{6,14},... | collective-permute-start | bytes 282632 | tf_op jit(solution)/shard_map/ppermute | solution.py:383
  30.1 9.3 %collective-permute-start.5 = (bf16[16,2944]{1,0:T(8,128)(2,1)S(1)}, bf16[16,2944]{1,0:T(8,128)(2,1)S(1)}, u32[]{:S(2)}, u32[]{:S(2)}) collective-permute-start(bf16[16,2944]{1,0:T(8,128)(2,1)S(1)} %get-tuple-element.51), channel_id=1, source_target_pairs={{0,12},{4,0},{8,4},{12,8},{1,13},{5,1},{9,5},{13,9},{2,14},{6,2},{... | collective-permute-start | bytes 282632 | tf_op jit(solution)/shard_map/ppermute | solution.py:383
  41.4 25.9 %all-to-all-start.1 = ((bf16[16,16,2944]{2,1,0:T(8,128)(2,1)}), bf16[16,16,2944]{2,1,0:T(8,128)(2,1)S(1)}, u32[]{:S(2)}, u32[]{:S(2)}) async-start(bf16[16,16,2944]{2,1,0:T(8,128)(2,1)} %get-tuple-element.59), calls=%async_computation.1 | async-start | bytes 3014656 | tf_op jit(solution)/shard_map/all_to_all | solution.py:334
  48.8 5.0 %copy-start.1 = (bf16[2,2880,180]{1,0,2:T(2,128)(2,1)S(1)}, bf16[2,2880,180]{1,0,2:T(2,128)(2,1)}, u32[]{:S(2)}) copy-start(bf16[2,2880,180]{1,0,2:T(2,128)(2,1)} %param.26) | copy-start | bytes 6220804
  48.8 4.9 %copy-start.2 = (bf16[2,2880,180]{1,0,2:T(2,128)(2,1)S(1)}, bf16[2,2880,180]{1,0,2:T(2,128)(2,1)}, u32[]{:S(2)}) copy-start(bf16[2,2880,180]{1,0,2:T(2,128)(2,1)} %param.25) | copy-start | bytes 6220804

commit v11 on v10

--- a/solution.py
+++ b/solution.py
@@ -36,16 +36,16 @@
 
 
 def attend_kernel(
-    len_ref, q_hbm, nk_hbm, nv_hbm, k_hbm, v_hbm, w_hbm, out_ref, w_ref,
-    q_ref, nk_ref, nv_ref, k_ref, v_ref, rows_ref, flat_ref, sems,
+    len_ref, place_ref, q_hbm, nk_hbm, nv_hbm, k_hbm, v_hbm, w_hbm, hid_hbm, ids_hbm, logits_hbm,
+    out_ref, w_ref, extra_ref, hid_ref, ids_ref, logits_ref, q_ref, nk_ref, nv_ref, k_ref, v_ref, rows_ref, flat_ref, sems,
 ):
     pairs = (
         (k_hbm, k_ref), (q_hbm, q_ref), (nk_hbm, nk_ref), (nv_hbm, nv_ref), (v_hbm, v_ref),
-        (w_hbm, w_ref),
+        (w_hbm, w_ref), (hid_hbm, hid_ref), (ids_hbm, ids_ref), (logits_hbm, logits_ref),
     )
     copies = [pltpu.make_async_copy(a, b, sems.at[i]) for i, (a, b) in enumerate(pairs)]
-    for copy in copies:
-        copy.start()
+    for i in (1, 0, 6, 7, 8, 2, 3, 4, 5):
+        copies[i].start()
     steps = q_ref.shape[1]
     width = KVH * HD
     rows = HQ * steps
@@ -62,6 +62,27 @@
     in_group = row_id // per_group == col_id // HD
     q_wide = jnp.where(in_group, q_wide, 0.0)
     q_bf = q_wide.astype(BF16)
+    for i in (6, 7, 8):
+        copies[i].wait()
+    spare = extra_ref.shape[1] - hid_ref.shape[2]
+    lane = lax.broadcasted_iota(jnp.int32, (1, spare), 1)
+    routes = []
+    for ref in (ids_ref, logits_ref):
+        held = ref[...].astype(F32)
+        row = lax.broadcasted_iota(jnp.int32, held.shape, 2)
+        routes.append(
+            jnp.sum(jnp.where(row == place_ref[2], held, 0.0), axis=2, keepdims=True)
+        )
+    top = routes[0].shape[1]
+    lines = []
+    for s in range(steps):
+        line = jnp.zeros((1, spare), F32)
+        for i, values in enumerate(routes):
+            for k in range(top):
+                line = jnp.where(lane == i * top + k, values[s, k : k + 1, :], line)
+        lines.append(line)
+    route = jnp.concatenate(lines, axis=0)
+    extra_ref[...] = jnp.concatenate([hid_ref[0].astype(F32), route], axis=1)
     copies[0].wait()
     scores = lax.dot_general(
         q_bf, k_ref[0], (((1,), (1,)), ((), ())), preferred_element_type=F32
@@ -99,41 +120,36 @@
     copies[5].wait()
 
 
-def attend(length, q, nk, nv, k, v, w, blocks):
+def attend(length, place, q, nk, nv, k, v, w, hidden, ids, logits, blocks):
     steps = q.shape[1]
+    width = hidden.shape[2]
+    args = (q, nk, nv, k, v, w, hidden, ids, logits)
     return pl.pallas_call(
         attend_kernel,
-        in_specs=[smem()] + [hbm()] * 6,
-        out_specs=[vmem(), vmem()],
+        in_specs=[smem(), smem()] + [hbm()] * len(args),
+        out_specs=[vmem(), vmem(), vmem()],
         out_shape=[
             jax.ShapeDtypeStruct((blocks, steps, HQ * HD // blocks), BF16),
             jax.ShapeDtypeStruct(w.shape, BF16),
+            jax.ShapeDtypeStruct((steps, width + -width % 128), F32),
         ],
-        scratch_shapes=[pltpu.VMEM(a.shape, BF16) for a in (q, nk, nv, k, v)]
+        scratch_shapes=[pltpu.VMEM(a.shape, a.dtype) for a in (hidden, ids, logits)]
+        + [pltpu.VMEM(a.shape, BF16) for a in (q, nk, nv, k, v)]
         + [
             pltpu.VMEM((HQ * steps, HD), F32),
             pltpu.VMEM((steps, HQ * HD), F32),
-            pltpu.SemaphoreType.DMA((6,)),
+            pltpu.SemaphoreType.DMA((len(args),)),
         ],
         compiler_params=params(12),
         name="attend",
-    )(length, *stay(q, nk, nv, k, v, w))
+    )(length, place, *stay(*args))
 
 
 def project_kernel(
-    place_ref, x_ref, own_ref, other_ref, hid_hbm, ids_hbm, logits_hbm, keep_ref, send_ref,
-    rows_ref, hid_ref, ids_ref, logits_ref, sems,
+    place_ref, x_ref, line_ref, own_ref, other_ref, keep_ref, send_ref, rows_ref
 ):
     width, feats = own_ref.shape
     chunk = 640
-    cuts = [(start, min(start + chunk, width)) for start in range(0, width, chunk)]
-    small = [
-        pltpu.make_async_copy(hid_hbm, hid_ref, sems.at[0]),
-        pltpu.make_async_copy(ids_hbm, ids_ref, sems.at[1]),
-        pltpu.make_async_copy(logits_hbm, logits_ref, sems.at[2]),
-    ]
-    for copy in small:
-        copy.start()
     blocks, steps, _ = x_ref.shape
     for i in range(blocks):
         rows_ref[i * steps : (i + 1) * steps, :] = x_ref[i].astype(F32)
@@ -142,32 +158,12 @@
     first = place_ref[1] == 0
     mine = jnp.where(first, low, high)
     theirs = jnp.where(first, high, low)
-    for copy in small:
-        copy.wait()
-    spare = keep_ref.shape[1] - width
-    lane = lax.broadcasted_iota(jnp.int32, (1, spare), 1)
-    routes = []
-    for ref in (ids_ref, logits_ref):
-        held = ref[...].astype(F32)
-        row = lax.broadcasted_iota(jnp.int32, held.shape, 2)
-        routes.append(
-            jnp.sum(jnp.where(row == place_ref[2], held, 0.0), axis=2, keepdims=True)
-        )
-    top = routes[0].shape[1]
-    lines = []
-    for s in range(steps):
-        line = jnp.zeros((1, spare), F32)
-        for i, values in enumerate(routes):
-            for k in range(top):
-                line = jnp.where(lane == i * top + k, values[s, k : k + 1, :], line)
-        lines.append(line)
-    route = jnp.concatenate(lines, axis=0)
-    extra = jnp.concatenate([hid_ref[0].astype(F32), route], axis=1)
-    extra = jnp.concatenate([extra] * blocks, axis=0)
+    extra = jnp.concatenate([line_ref[...]] * blocks, axis=0)
     block = lax.broadcasted_iota(jnp.int32, extra.shape, 0) // steps
     extra = jnp.where(block == place_ref[0], extra, 0.0)
     dims = (((1,), (1,)), ((), ()))
-    for start, stop in cuts:
+    for start in range(0, width, chunk):
+        stop = min(start + chunk, width)
         part = lax.dot_general(mine, own_ref[start:stop], dims, preferred_element_type=F32)
         part = part + lax.dot_general(
             theirs, other_ref[start:stop], dims, preferred_element_type=F32
@@ -179,28 +175,21 @@
     send_ref[:, width:] = extra[:, width:].astype(BF16)
 
 
-def project(place, x, hidden, ids, logits, own, other):
+def project(place, x, line, own, other):
     blocks, steps, feats = x.shape
-    wide = own.shape[0] + -own.shape[0] % 128
     rows = blocks * steps
     return pl.pallas_call(
         project_kernel,
-        in_specs=[smem(), vmem(), vmem(), vmem()] + [hbm()] * 3,
+        in_specs=[smem()] + [vmem()] * 4,
         out_specs=[vmem(), vmem()],
         out_shape=[
-            jax.ShapeDtypeStruct((rows, wide), F32),
-            jax.ShapeDtypeStruct((rows, wide), BF16),
+            jax.ShapeDtypeStruct((rows, line.shape[1]), F32),
+            jax.ShapeDtypeStruct((rows, line.shape[1]), BF16),
         ],
-        scratch_shapes=[
-            pltpu.VMEM((rows, feats), F32),
-            pltpu.VMEM(hidden.shape, BF16),
-            pltpu.VMEM(ids.shape, jnp.int32),
-            pltpu.VMEM(logits.shape, BF16),
-            pltpu.SemaphoreType.DMA((3,)),
-        ],
+        scratch_shapes=[pltpu.VMEM((rows, feats), F32)],
         compiler_params=params(12),
         name="project",
-    )(place, x, own, other, *stay(hidden, ids, logits))
+    )(place, x, line, own, other)
 
 
 def join_kernel(keep_ref, got_ref, next_ref, send_ref):
@@ -298,17 +287,12 @@
             acts.append((act * share).astype(BF16))
     copies[4].wait()
     copies[5].wait()
-    chunk = 1536
-    for start in range(0, width, chunk):
-        stop = min(start + chunk, width)
-        part = None
-        for side, d_ref in enumerate((d0, d1)):
-            for e in range(per):
-                piece = jnp.dot(
-                    acts[side * per + e], d_ref[e, :, start:stop], preferred_element_type=F32
-                )
-                part = piece if part is None else part + piece
-        out_ref[:, start:stop] = part.astype(BF16)
+    part = None
+    for side, d_ref in enumerate((d0, d1)):
+        for e in range(per):
+            piece = jnp.dot(acts[side * per + e], d_ref[e], preferred_element_type=F32)
+            part = piece if part is None else part + piece
+    out_ref[...] = part.astype(BF16)
 
 
 def experts(first, x, own, other):
@@ -364,15 +348,16 @@
     far_down, far_gate, far_up = (
         lax.ppermute(w, "c", SWAP) for w in (down_weight, gate_weight, up_weight)
     )
-    attended, own_out = attend(
-        prompt_lengths, queries, new_keys, new_values, key_cache, value_cache, out_rows, nz
-    )
     place = jnp.stack([z, c, d]).astype(jnp.int32)
     first = jnp.stack([(2 * z + c) * per, (2 * z + 1 - c) * per]).astype(jnp.int32)
-    attended, place, first = lax.optimization_barrier((attended, place, first))
+    ids, logits = expert_ids.transpose(1, 2, 0), top_logits.transpose(1, 2, 0)
+    attended, own_out, line = attend(
+        prompt_lengths, place, queries, new_keys, new_values, key_cache, value_cache,
+        out_rows, hidden_in, ids, logits, nz,
+    )
+    attended, first = lax.optimization_barrier((attended, first))
     by_heads = exchange(attended, zaxis)
-    ids, logits = expert_ids.transpose(1, 2, 0), top_logits.transpose(1, 2, 0)
-    keep, sent = project(place, by_heads, hidden_in, ids, logits, own_out, other_out)
+    keep, sent = project(place, by_heads, line, own_out, other_out)
     sent, gain, down = lax.optimization_barrier((sent, norm_gain, down_weight))
     got = lax.ppermute(sent, "v", SWAP)
     got, gain, down = lax.optimization_barrier((got, gain[None], row_major(down)))

time: 113 us -> 113 us (level)
  transfers between devices with their start and end apart: 9 -> 9, of which waited for: 5 -> 5; matrix products, arithmetic and copies ran while one was open for 11% -> 11% of each run, Pallas kernels for 6% -> 5%
where the time goes in v11:
time: 113 us
  blocking collectives  52.9 us (47%)
  waiting for transfers between devices  17.7 us (16%)
  Pallas kernels  14.1 us (12%)
  starting transfers between devices  14 us (12%)
  local copies, waits for them, and re-layouts  12.3 us (11%)
    all_to_all x3, blocking collectives, exchange(): return lax.all_to_all(value, axis, split_axis=0, concat_axis=0, tiled=True)  52.9 us
    all_to_all x1, waiting for transfers between devices, exchange(): return lax.all_to_all(value, axis, split_axis=0, concat_axis=0, tiled=True)  11 us
    pallas_call x1, Pallas kernels, experts(): pl.pallas_call(experts_kernel, in_specs=[smem(), vmem()] + [hbm()] * 6, o...  8.01 us
    transpose x2, local copies, waits for them, and re-layouts, on_device(): relaid = [row_major(w.swapaxes(1, 2)) for w in weights]  7.53 us
    all_to_all x1, starting transfers between devices, exchange(): return lax.all_to_all(value, axis, split_axis=0, concat_axis=0, tiled=True)  7.41 us
    ppermute x3, starting transfers between devices, on_device(): lax.ppermute(sent, 'w', [(i, (i + k) % quarter) for i in range(quarter)])  4.83 us
    ppermute x3, waiting for transfers between devices, on_device(): lax.ppermute(sent, 'w', [(i, (i + k) % quarter) for i in range(quarter)])  4.4 us
    optimization_barrier x1, local copies, waits for them, and re-layouts, on_device(): sent, far_down = lax.optimization_barrier((sent, far_down))  3.13 us
  transfers between devices with their start and end apart: 9, of which 5 were waited for; matrix products, arithmetic and copies ran while one was open for 11% of the time, Pallas kernels for 5%

profile of v11, /device:TPU:8, one launch (start us, length us, event | category | flops | bytes accessed | tf_op | source)
XLA Modules:
  0.0 112.9 jit_solution(14383246275182752788)
XLA Ops:
  0.0 0.0 collective-permute-start.2
  0.0 0.5 collective-permute-start.6
  0.5 0.0 collective-permute-start.7
  0.5 0.5 collective-permute-start
  1.7 0.1 pad_add_fusion.place_ref
  1.8 2.7 %attend.1 = (bf16[8,2,512]{2,1,0:T(2,128)(2,1)S(1)}, bf16[2880,256]{1,0:T(8,128)(2,1)S(1)}, f32[2,2944]{1,0:T(2,128)S(1)}) custom-call(s32[1]{0:T(128)S(6)} %copy.59.len_ref, s32[3]{0:T(128)S(1)} %pad_add_fusion.place_ref, bf16[1,2,4096]{2,1,0:T(2,128)(2,1)} %q_hbm.1, bf16[1,2,512]{2,1,0:T(2,128)(2,1)} %nk_hbm.1, bf16[1,2,512]{2,1,0:T(2,128)(2,1)} %nv_hbm.1, ...), custom_call_target="tpu_custom_call" | custom-call | tf_op jit(solution)/shard_map/attend/pallas_call | solution.py:127
  4.4 0.0 copy-start
  4.4 0.1 pad_add_fusion.1.first_ref
  4.5 16.2 %all_to_all.20.x_ref = bf16[8,2,512]{2,1,0:T(2,128)(2,1)S(1)} all-to-all(bf16[8,2,512]{2,1,0:T(2,128)(2,1)S(1)} %get-tuple-element.39), channel_id=1, replica_groups=mesh['x'=4,'y'=4,'w'=4,'v'=2,'c'=2] {'w','v'}, dimensions={0} | all-to-all | bytes 32768 | tf_op jit(solution)/shard_map/all_to_all | solution.py:318
  20.7 0.0 collective-permute-done.other_ref
  20.7 1.4 %project.1 = (f32[16,2944]{1,0:T(8,128)S(1)}, bf16[16,2944]{1,0:T(8,128)(2,1)S(1)}) custom-call(s32[3]{0:T(128)S(1)} %pad_add_fusion.place_ref, bf16[8,2,512]{2,1,0:T(2,128)(2,1)S(1)} %all_to_all.20.x_ref, f32[2,2944]{1,0:T(2,128)S(1)} %get-tuple-element.40.line_ref, bf16[2880,256]{1,0:T(8,128)(2,1)S(1)} %get-tuple-element.41.own_ref, ...), custom_call_target="tpu_custom_call" | custom-call | tf_op jit(solution)/shard_map/project/pallas_call | solution.py:181
  22.1 0.0 copy-start.3
  22.1 0.7 collective-permute-start.1
  22.8 0.0 copy-done
  22.8 1.6 %copy.47.d0_hbm = bf16[2,180,2880]{2,1,0:T(8,128)(2,1)} copy(bf16[2,180,2880]{2,0,1:T(2,128)(2,1)S(1)} %copy-done) | data formatting | bytes 4147200 | tf_op jit(solution)/shard_map/optimization_barrier | solution.py:361
  24.4 0.0 copy-done.3
  24.4 2.4 %collective-permute-done.1.got_ref = bf16[16,2944]{1,0:T(8,128)(2,1)S(1)} collective-permute-done((bf16[16,2944]{1,0:T(8,128)(2,1)S(1)}, bf16[16,2944]{1,0:T(8,128)(2,1)S(1)}, u32[]{:S(2)}, u32[]{:S(2)}) %collective-permute-start.1) | collective-permute-done | bytes 94240 | tf_op jit(solution)/shard_map/ppermute | solution.py:362
  26.8 0.0 collective-permute-done.2
  26.8 0.7 collective-permute-start.3
  27.5 2.4 %collective-permute-start.4 = (bf16[16,2944]{1,0:T(8,128)(2,1)S(1)}, bf16[16,2944]{1,0:T(8,128)(2,1)S(1)}, u32[]{:S(2)}, u32[]{:S(2)}) collective-permute-start(bf16[16,2944]{1,0:T(8,128)(2,1)S(1)} %get-tuple-element.51), channel_id=1, source_target_pairs={{0,8},{4,12},{8,0},{12,4},{1,9},{5,13},{9,1},{13,5},{2,10},{6,14},... | collective-permute-start | bytes 282632 | tf_op jit(solution)/shard_map/ppermute | solution.py:368
  29.9 1.8 %collective-permute-start.5 = (bf16[16,2944]{1,0:T(8,128)(2,1)S(1)}, bf16[16,2944]{1,0:T(8,128)(2,1)S(1)}, u32[]{:S(2)}, u32[]{:S(2)}) collective-permute-start(bf16[16,2944]{1,0:T(8,128)(2,1)S(1)} %get-tuple-element.51), channel_id=1, source_target_pairs={{0,12},{4,0},{8,4},{12,8},{1,13},{5,1},{9,5},{13,9},{2,14},{6,2},{... | collective-permute-start | bytes 282632 | tf_op jit(solution)/shard_map/ppermute | solution.py:368
  31.7 3.1 %copy.48.d1_hbm = bf16[2,180,2880]{2,1,0:T(8,128)(2,1)} copy(bf16[2,180,2880]{2,0,1:T(2,128)(2,1)} %collective-permute-done.2) | data formatting | bytes 4147200 | tf_op jit(solution)/shard_map/optimization_barrier | solution.py:365
  34.8 0.2 collective-permute-done.3.near_ref
  35.0 2.4 %collective-permute-done.4.back_ref = bf16[16,2944]{1,0:T(8,128)(2,1)S(1)} collective-permute-done((bf16[16,2944]{1,0:T(8,128)(2,1)S(1)}, bf16[16,2944]{1,0:T(8,128)(2,1)S(1)}, u32[]{:S(2)}, u32[]{:S(2)}) %collective-permute-start.4) | collective-permute-done | bytes 94240 | tf_op jit(solution)/shard_map/ppermute | solution.py:368
  37.3 1.9 %collective-permute-done.5.far_ref = bf16[16,2944]{1,0:T(8,128)(2,1)S(1)} collective-permute-done((bf16[16,2944]{1,0:T(8,128)(2,1)S(1)}, bf16[16,2944]{1,0:T(8,128)(2,1)S(1)}, u32[]{:S(2)}, u32[]{:S(2)}) %collective-permute-start.5) | collective-permute-done | bytes 94240 | tf_op jit(solution)/shard_map/ppermute | solution.py:368
  39.2 2.0 %norm.1 = (f32[2,2880]{1,0:T(2,128)S(1)}, bf16[16,16,2944]{2,1,0:T(8,128)(2,1)}) custom-call(s32[3]{0:T(128)S(1)} %pad_add_fusion.place_ref, f32[16,2944]{1,0:T(8,128)S(1)} %get-tuple-element.48.keep_ref, bf16[16,2944]{1,0:T(8,128)(2,1)S(1)} %collective-permute-done.3.near_ref, bf16[16,2944]{1,0:T(8,128)(2,1)S(1)} %collective-permute-done.4.back_ref, ...), custom_call_target="tpu_custom_call" | custom-call | tf_op jit(solution)/shard_map/norm/pallas_call | solution.py:243
  41.2 0.0 collective-permute-done.6
  41.2 0.0 collective-permute-done.7
  41.2 7.4 %all-to-all-start.1 = ((bf16[16,16,2944]{2,1,0:T(8,128)(2,1)}), bf16[16,16,2944]{2,1,0:T(8,128)(2,1)S(1)}, u32[]{:S(2)}, u32[]{:S(2)}) async-start(bf16[16,16,2944]{2,1,0:T(8,128)(2,1)} %get-tuple-element.59), calls=%async_computation.1 | async-start | bytes 3014656 | tf_op jit(solution)/shard_map/all_to_all | solution.py:318
  48.6 0.0 copy-start.1
  48.6 0.0 copy-start.2
  48.7 4.9 %copy_bitcast_fusion = (bf16[2,180,2880]{2,1,0:T(8,128)(2,1)}, bf16[2,180,2880]{2,1,0:T(8,128)(2,1)}) fusion(bf16[2,2880,180]{1,0,2:T(2,128)(2,1)} %collective-permute-done.7, bf16[2,2880,180]{1,0,2:T(2,128)(2,1)} %collective-permute-done.6), kind=kLoop, calls=%fused_computation | loop fusion | bytes 8294400 | tf_op jit(solution)/shard_map/transpose | solution.py:377
  53.6 0.0 copy-done.1
  53.6 0.0 copy-done.2
  53.6 2.6 %copy_bitcast_fusion.2 = (bf16[2,180,2880]{2,1,0:T(8,128)(2,1)}, bf16[2,180,2880]{2,1,0:T(8,128)(2,1)}) fusion(bf16[2,2880,180]{1,0,2:T(2,128)(2,1)S(1)} %copy-done.1, bf16[2,2880,180]{1,0,2:T(2,128)(2,1)S(1)} %copy-done.2), kind=kLoop, calls=%fused_computation.2 | loop fusion | bytes 8294400 | tf_op jit(solution)/shard_map/transpose | solution.py:377
  56.2 11.0 %all-to-all-done.1 = bf16[16,16,2944]{2,1,0:T(8,128)(2,1)S(1)} async-done(((bf16[16,16,2944]{2,1,0:T(8,128)(2,1)}), bf16[16,16,2944]{2,1,0:T(8,128)(2,1)S(1)}, u32[]{:S(2)}, u32[]{:S(2)}) %all-to-all-start.1) | async-done | bytes 1507360 | tf_op jit(solution)/shard_map/all_to_all | solution.py:318
  67.2 8.0 %experts.1 = bf16[256,2880]{1,0:T(8,128)(2,1)S(1)} custom-call(s32[2]{0:T(128)S(1)} %pad_add_fusion.1.first_ref, bf16[256,2944]{1,0:T(8,128)(2,1)S(1)} %bitcast.20, bf16[2,180,2880]{2,1,0:T(8,128)(2,1)} %get-tuple-element.65.g0_hbm, bf16[2,180,2880]{2,1,0:T(8,128)(2,1)} %get-tuple-element.66.u0_hbm, bf16[2,180,2880]{2,1,0:T(8,128)(2,1)} %get-tuple-element.67.g1_hbm, ...), custom_call_target="tpu_custom_call" | custom-call | tf_op jit(solution)/shard_map/experts/pallas_call | solution.py:301
  75.2 23.0 %all_to_all.21 = bf16[16,16,2880]{2,1,0:T(8,128)(2,1)S(1)} all-to-all(bf16[16,16,2880]{2,1,0:T(8,128)(2,1)S(1)} %bitcast.21), channel_id=1, replica_groups=mesh['x'=4,'y'=4,'w'=4,'v'=2,'c'=2] {'x','y'}, dimensions={0} | all-to-all | bytes 2949120 | tf_op jit(solution)/shard_map/all_to_all | solution.py:318
  98.1 0.2 reduce_sum.21
  98.4 13.8 %all_to_all.22 = bf16[8,2,2880]{2,1,0:T(2,128)(2,1)S(1)} all-to-all(bf16[8,2,2880]{2,1,0:T(2,128)(2,1)S(1)} %reshape.11), channel_id=1, replica_groups=mesh['x'=4,'y'=4,'w'=4,'v'=2,'c'=2] {'w','v'}, dimensions={0} | all-to-all | bytes 184320 | tf_op jit(solution)/shard_map/all_to_all | solution.py:318
  112.2 0.1 convert_reduce_fusion
  112.3 0.6 fusion
  (3 shorter events, 0.1 us)
Async XLA Ops:
  0.0 26.8 %collective-permute-start.2 = (bf16[2,180,2880]{2,0,1:T(2,128)(2,1)}, bf16[2,180,2880]{2,0,1:T(2,128)(2,1)}, u32[]{:S(2)}, u32[]{:S(2)}) collective-permute-start(bf16[2,180,2880]{2,0,1:T(2,128)(2,1)} %param.27), channel_id=1, source_target_pairs={{0,1},{1,0},{2,3},{3,2},{4,5},{5,4},{6,7},{7,6},{8,9},{9,8},{10,11... | collective-permute-start | bytes 6220808 | tf_op jit(solution)/shard_map/ppermute | solution.py:349
  0.0 41.2 %collective-permute-start.6 = (bf16[2,2880,180]{1,0,2:T(2,128)(2,1)}, bf16[2,2880,180]{1,0,2:T(2,128)(2,1)}, u32[]{:S(2)}, u32[]{:S(2)}) collective-permute-start(bf16[2,2880,180]{1,0,2:T(2,128)(2,1)} %param.25), channel_id=1, source_target_pairs={{0,1},{1,0},{2,3},{3,2},{4,5},{5,4},{6,7},{7,6},{8,9},{9,8},{10,11... | collective-permute-start | bytes 6220808 | tf_op jit(solution)/shard_map/ppermute | solution.py:349
  0.5 40.7 %collective-permute-start.7 = (bf16[2,2880,180]{1,0,2:T(2,128)(2,1)}, bf16[2,2880,180]{1,0,2:T(2,128)(2,1)}, u32[]{:S(2)}, u32[]{:S(2)}) collective-permute-start(bf16[2,2880,180]{1,0,2:T(2,128)(2,1)} %param.26), channel_id=1, source_target_pairs={{0,1},{1,0},{2,3},{3,2},{4,5},{5,4},{6,7},{7,6},{8,9},{9,8},{10,11... | collective-permute-start | bytes 6220808 | tf_op jit(solution)/shard_map/ppermute | solution.py:349
  0.5 20.2 %collective-permute-start = (bf16[2880,256]{1,0:T(8,128)(2,1)}, bf16[2880,256]{1,0:T(8,128)(2,1)S(1)}, u32[]{:S(2)}, u32[]{:S(2)}) collective-permute-start(bf16[2880,256]{1,0:T(8,128)(2,1)} %bitcast.22), channel_id=1, source_target_pairs={{0,1},{1,0},{2,3},{3,2},{4,5},{5,4},{6,7},{7,6},{8,9},{9,8},{10,11... | collective-permute-start | bytes 4423688 | tf_op jit(solution)/shard_map/ppermute | solution.py:347
  4.4 18.4 %copy-start = (bf16[2,180,2880]{2,0,1:T(2,128)(2,1)S(1)}, bf16[2,180,2880]{2,0,1:T(2,128)(2,1)}, u32[]{:S(2)}) copy-start(bf16[2,180,2880]{2,0,1:T(2,128)(2,1)} %param.27) | copy-start | bytes 6220804
  22.1 2.3 %copy-start.3 = (f32[2880]{0:T(1024)S(1)}, f32[2880]{0:T(1024)}, u32[]{:S(2)}) copy-start(f32[2880]{0:T(1024)} %param.22) | copy-start | bytes 34564
  22.1 4.7 %collective-permute-start.1 = (bf16[16,2944]{1,0:T(8,128)(2,1)S(1)}, bf16[16,2944]{1,0:T(8,128)(2,1)S(1)}, u32[]{:S(2)}, u32[]{:S(2)}) collective-permute-start(bf16[16,2944]{1,0:T(8,128)(2,1)S(1)} %get-tuple-element.44), channel_id=1, source_target_pairs={{0,2},{2,0},{1,3},{3,1},{4,6},{6,4},{5,7},{7,5},{8,10},{10,8},{9,1... | collective-permute-start | bytes 282632 | tf_op jit(solution)/shard_map/ppermute | solution.py:362
  26.8 8.1 %collective-permute-start.3 = (bf16[16,2944]{1,0:T(8,128)(2,1)S(1)}, bf16[16,2944]{1,0:T(8,128)(2,1)S(1)}, u32[]{:S(2)}, u32[]{:S(2)}) collective-permute-start(bf16[16,2944]{1,0:T(8,128)(2,1)S(1)} %get-tuple-element.51), channel_id=1, source_target_pairs={{0,4},{4,8},{8,12},{12,0},{1,5},{5,9},{9,13},{13,1},{2,6},{6,10},{... | collective-permute-start | bytes 282632 | tf_op jit(solution)/shard_map/ppermute | solution.py:368
  27.5 9.9 %collective-permute-start.4 = (bf16[16,2944]{1,0:T(8,128)(2,1)S(1)}, bf16[16,2944]{1,0:T(8,128)(2,1)S(1)}, u32[]{:S(2)}, u32[]{:S(2)}) collective-permute-start(bf16[16,2944]{1,0:T(8,128)(2,1)S(1)} %get-tuple-element.51), channel_id=1, source_target_pairs={{0,8},{4,12},{8,0},{12,4},{1,9},{5,13},{9,1},{13,5},{2,10},{6,14},... | collective-permute-start | bytes 282632 | tf_op jit(solution)/shard_map/ppermute | solution.py:368
  29.9 9.3 %collective-permute-start.5 = (bf16[16,2944]{1,0:T(8,128)(2,1)S(1)}, bf16[16,2944]{1,0:T(8,128)(2,1)S(1)}, u32[]{:S(2)}, u32[]{:S(2)}) collective-permute-start(bf16[16,2944]{1,0:T(8,128)(2,1)S(1)} %get-tuple-element.51), channel_id=1, source_target_pairs={{0,12},{4,0},{8,4},{12,8},{1,13},{5,1},{9,5},{13,9},{2,14},{6,2},{... | collective-permute-start | bytes 282632 | tf_op jit(solution)/shard_map/ppermute | solution.py:368
  41.2 25.9 %all-to-all-start.1 = ((bf16[16,16,2944]{2,1,0:T(8,128)(2,1)}), bf16[16,16,2944]{2,1,0:T(8,128)(2,1)S(1)}, u32[]{:S(2)}, u32[]{:S(2)}) async-start(bf16[16,16,2944]{2,1,0:T(8,128)(2,1)} %get-tuple-element.59), calls=%async_computation.1 | async-start | bytes 3014656 | tf_op jit(solution)/shard_map/all_to_all | solution.py:318
  48.6 5.0 %copy-start.1 = (bf16[2,2880,180]{1,0,2:T(2,128)(2,1)S(1)}, bf16[2,2880,180]{1,0,2:T(2,128)(2,1)}, u32[]{:S(2)}) copy-start(bf16[2,2880,180]{1,0,2:T(2,128)(2,1)} %param.26) | copy-start | bytes 6220804
  48.6 4.9 %copy-start.2 = (bf16[2,2880,180]{1,0,2:T(2,128)(2,1)S(1)}, bf16[2,2880,180]{1,0,2:T(2,128)(2,1)}, u32[]{:S(2)}) copy-start(bf16[2,2880,180]{1,0,2:T(2,128)(2,1)} %param.25) | copy-start | bytes 6220804

commit v12 on v11

--- a/solution.py
+++ b/solution.py
@@ -62,27 +62,6 @@
     in_group = row_id // per_group == col_id // HD
     q_wide = jnp.where(in_group, q_wide, 0.0)
     q_bf = q_wide.astype(BF16)
-    for i in (6, 7, 8):
-        copies[i].wait()
-    spare = extra_ref.shape[1] - hid_ref.shape[2]
-    lane = lax.broadcasted_iota(jnp.int32, (1, spare), 1)
-    routes = []
-    for ref in (ids_ref, logits_ref):
-        held = ref[...].astype(F32)
-        row = lax.broadcasted_iota(jnp.int32, held.shape, 2)
-        routes.append(
-            jnp.sum(jnp.where(row == place_ref[2], held, 0.0), axis=2, keepdims=True)
-        )
-    top = routes[0].shape[1]
-    lines = []
-    for s in range(steps):
-        line = jnp.zeros((1, spare), F32)
-        for i, values in enumerate(routes):
-            for k in range(top):
-                line = jnp.where(lane == i * top + k, values[s, k : k + 1, :], line)
-        lines.append(line)
-    route = jnp.concatenate(lines, axis=0)
-    extra_ref[...] = jnp.concatenate([hid_ref[0].astype(F32), route], axis=1)
     copies[0].wait()
     scores = lax.dot_general(
         q_bf, k_ref[0], (((1,), (1,)), ((), ())), preferred_element_type=F32
@@ -117,6 +96,27 @@
     wide = HQ * HD // blocks
     for b in range(blocks):
         out_ref[b] = flat_ref[:, b * wide : (b + 1) * wide].astype(BF16)
+    for i in (6, 7, 8):
+        copies[i].wait()
+    spare = extra_ref.shape[1] - hid_ref.shape[2]
+    lane = lax.broadcasted_iota(jnp.int32, (1, spare), 1)
+    routes = []
+    for ref in (ids_ref, logits_ref):
+        held = ref[...].astype(F32)
+        row = lax.broadcasted_iota(jnp.int32, held.shape, 2)
+        routes.append(
+            jnp.sum(jnp.where(row == place_ref[2], held, 0.0), axis=2, keepdims=True)
+        )
+    top = routes[0].shape[1]
+    lines = []
+    for s in range(steps):
+        line = jnp.zeros((1, spare), F32)
+        for i, values in enumerate(routes):
+            for k in range(top):
+                line = jnp.where(lane == i * top + k, values[s, k : k + 1, :], line)
+        lines.append(line)
+    route = jnp.concatenate(lines, axis=0)
+    extra_ref[...] = jnp.concatenate([hid_ref[0].astype(F32), route], axis=1)
     copies[5].wait()
 
 
@@ -314,6 +314,24 @@
     return with_layout_constraint(value, Layout(major_to_minor=tuple(range(value.ndim))))
 
 
+def finish_kernel(res_ref, part_ref, out_ref):
+    total = res_ref[...]
+    for i in range(part_ref.shape[0]):
+        total = total + part_ref[i].astype(F32)
+    out_ref[0] = total.astype(BF16)
+
+
+def finish(residual, parts):
+    return pl.pallas_call(
+        finish_kernel,
+        in_specs=[vmem(), vmem()],
+        out_specs=vmem(),
+        out_shape=jax.ShapeDtypeStruct((1,) + residual.shape, BF16),
+        compiler_params=params(12),
+        name="finish",
+    )(residual, parts)
+
+
 def exchange(value, axis):
     return lax.all_to_all(value, axis, split_axis=0, concat_axis=0, tiled=True)
 
@@ -381,8 +399,7 @@
     back = exchange(made.reshape(ndp, nz * steps, width), dp)
     column_sum = jnp.sum(back.astype(F32), axis=0).astype(BF16)
     final = exchange(column_sum.reshape(nz, steps, width), zaxis)
-    out = residual + jnp.sum(final.astype(F32), axis=0)
-    return out.astype(BF16)[None]
+    return finish(residual, final)
 
 
 def solution(mesh):

time: 113 us -> 113 us (level)
  transfers between devices with their start and end apart: 9 -> 9, of which waited for: 5 -> 5; matrix products, arithmetic and copies ran while one was open for 11% -> 11% of each run, Pallas kernels for 5% -> 6%
where the time goes in v12:
time: 113 us
  blocking collectives  52.9 us (47%)
  waiting for transfers between devices  17.7 us (16%)
  Pallas kernels  14.9 us (13%)
  starting transfers between devices  14 us (12%)
  local copies, waits for them, and re-layouts  12.3 us (11%)
    all_to_all x3, blocking collectives, exchange(): return lax.all_to_all(value, axis, split_axis=0, concat_axis=0, tiled=True)  52.9 us
    all_to_all x1, waiting for transfers between devices, exchange(): return lax.all_to_all(value, axis, split_axis=0, concat_axis=0, tiled=True)  10.9 us
    pallas_call x1, Pallas kernels, experts(): pl.pallas_call(experts_kernel, in_specs=[smem(), vmem()] + [hbm()] * 6, o...  8 us
    transpose x2, local copies, waits for them, and re-layouts, on_device(): relaid = [row_major(w.swapaxes(1, 2)) for w in weights]  7.54 us
    all_to_all x1, starting transfers between devices, exchange(): return lax.all_to_all(value, axis, split_axis=0, concat_axis=0, tiled=True)  7.4 us
    ppermute x3, starting transfers between devices, on_device(): lax.ppermute(sent, 'w', [(i, (i + k) % quarter) for i in range(quarter)])  4.83 us
    ppermute x3, waiting for transfers between devices, on_device(): lax.ppermute(sent, 'w', [(i, (i + k) % quarter) for i in range(quarter)])  4.4 us
    optimization_barrier x1, local copies, waits for them, and re-layouts, on_device(): sent, far_down = lax.optimization_barrier((sent, far_down))  3.13 us
  transfers between devices with their start and end apart: 9, of which 5 were waited for; matrix products, arithmetic and copies ran while one was open for 11% of the time, Pallas kernels for 6%

profile of v12, /device:TPU:8, one launch (start us, length us, event | category | flops | bytes accessed | tf_op | source)
XLA Modules:
  0.0 112.9 jit_solution(11470039412866003807)
XLA Ops:
  0.0 0.0 collective-permute-start.2
  0.0 0.5 collective-permute-start.6
  0.5 0.0 collective-permute-start.7
  0.5 0.5 collective-permute-start
  1.7 0.1 pad_add_fusion.place_ref
  1.8 2.8 %attend.1 = (bf16[8,2,512]{2,1,0:T(2,128)(2,1)S(1)}, bf16[2880,256]{1,0:T(8,128)(2,1)S(1)}, f32[2,2944]{1,0:T(2,128)S(1)}) custom-call(s32[1]{0:T(128)S(6)} %copy.31.len_ref, s32[3]{0:T(128)S(1)} %pad_add_fusion.place_ref, bf16[1,2,4096]{2,1,0:T(2,128)(2,1)} %q_hbm.1, bf16[1,2,512]{2,1,0:T(2,128)(2,1)} %nk_hbm.1, bf16[1,2,512]{2,1,0:T(2,128)(2,1)} %nv_hbm.1, ...), custom_call_target="tpu_custom_call" | custom-call | tf_op jit(solution)/shard_map/attend/pallas_call | solution.py:127
  4.6 0.0 copy-start
  4.6 0.1 pad_add_fusion.1.first_ref
  4.6 16.2 %all_to_all.20.x_ref = bf16[8,2,512]{2,1,0:T(2,128)(2,1)S(1)} all-to-all(bf16[8,2,512]{2,1,0:T(2,128)(2,1)S(1)} %get-tuple-element.39), channel_id=1, replica_groups=mesh['x'=4,'y'=4,'w'=4,'v'=2,'c'=2] {'w','v'}, dimensions={0} | all-to-all | bytes 32768 | tf_op jit(solution)/shard_map/all_to_all | solution.py:336
  20.8 0.0 collective-permute-done.other_ref
  20.8 1.4 %project.1 = (f32[16,2944]{1,0:T(8,128)S(1)}, bf16[16,2944]{1,0:T(8,128)(2,1)S(1)}) custom-call(s32[3]{0:T(128)S(1)} %pad_add_fusion.place_ref, bf16[8,2,512]{2,1,0:T(2,128)(2,1)S(1)} %all_to_all.20.x_ref, f32[2,2944]{1,0:T(2,128)S(1)} %get-tuple-element.40.line_ref, bf16[2880,256]{1,0:T(8,128)(2,1)S(1)} %get-tuple-element.41.own_ref, ...), custom_call_target="tpu_custom_call" | custom-call | tf_op jit(solution)/shard_map/project/pallas_call | solution.py:181
  22.2 0.0 copy-start.3
  22.3 0.7 collective-permute-start.1
  23.0 0.0 copy-done
  23.0 1.6 %copy.21.d0_hbm = bf16[2,180,2880]{2,1,0:T(8,128)(2,1)} copy(bf16[2,180,2880]{2,0,1:T(2,128)(2,1)S(1)} %copy-done) | data formatting | bytes 4147200 | tf_op jit(solution)/shard_map/optimization_barrier | solution.py:379
  24.5 0.0 copy-done.3
  24.5 2.4 %collective-permute-done.1.got_ref = bf16[16,2944]{1,0:T(8,128)(2,1)S(1)} collective-permute-done((bf16[16,2944]{1,0:T(8,128)(2,1)S(1)}, bf16[16,2944]{1,0:T(8,128)(2,1)S(1)}, u32[]{:S(2)}, u32[]{:S(2)}) %collective-permute-start.1) | collective-permute-done | bytes 94240 | tf_op jit(solution)/shard_map/ppermute | solution.py:380
  26.9 0.0 collective-permute-done.2
  26.9 0.7 collective-permute-start.3
  27.6 2.4 %collective-permute-start.4 = (bf16[16,2944]{1,0:T(8,128)(2,1)S(1)}, bf16[16,2944]{1,0:T(8,128)(2,1)S(1)}, u32[]{:S(2)}, u32[]{:S(2)}) collective-permute-start(bf16[16,2944]{1,0:T(8,128)(2,1)S(1)} %get-tuple-element.51), channel_id=1, source_target_pairs={{0,8},{4,12},{8,0},{12,4},{1,9},{5,13},{9,1},{13,5},{2,10},{6,14},... | collective-permute-start | bytes 282632 | tf_op jit(solution)/shard_map/ppermute | solution.py:386
  30.0 1.8 %collective-permute-start.5 = (bf16[16,2944]{1,0:T(8,128)(2,1)S(1)}, bf16[16,2944]{1,0:T(8,128)(2,1)S(1)}, u32[]{:S(2)}, u32[]{:S(2)}) collective-permute-start(bf16[16,2944]{1,0:T(8,128)(2,1)S(1)} %get-tuple-element.51), channel_id=1, source_target_pairs={{0,12},{4,0},{8,4},{12,8},{1,13},{5,1},{9,5},{13,9},{2,14},{6,2},{... | collective-permute-start | bytes 282632 | tf_op jit(solution)/shard_map/ppermute | solution.py:386
  31.8 3.1 %copy.22.d1_hbm = bf16[2,180,2880]{2,1,0:T(8,128)(2,1)} copy(bf16[2,180,2880]{2,0,1:T(2,128)(2,1)} %collective-permute-done.2) | data formatting | bytes 4147200 | tf_op jit(solution)/shard_map/optimization_barrier | solution.py:383
  34.9 0.2 collective-permute-done.3.near_ref
  35.1 2.4 %collective-permute-done.4.back_ref = bf16[16,2944]{1,0:T(8,128)(2,1)S(1)} collective-permute-done((bf16[16,2944]{1,0:T(8,128)(2,1)S(1)}, bf16[16,2944]{1,0:T(8,128)(2,1)S(1)}, u32[]{:S(2)}, u32[]{:S(2)}) %collective-permute-start.4) | collective-permute-done | bytes 94240 | tf_op jit(solution)/shard_map/ppermute | solution.py:386
  37.5 1.9 %collective-permute-done.5.far_ref = bf16[16,2944]{1,0:T(8,128)(2,1)S(1)} collective-permute-done((bf16[16,2944]{1,0:T(8,128)(2,1)S(1)}, bf16[16,2944]{1,0:T(8,128)(2,1)S(1)}, u32[]{:S(2)}, u32[]{:S(2)}) %collective-permute-start.5) | collective-permute-done | bytes 94240 | tf_op jit(solution)/shard_map/ppermute | solution.py:386
  39.3 2.0 %norm.1 = (f32[2,2880]{1,0:T(2,128)S(1)}, bf16[16,16,2944]{2,1,0:T(8,128)(2,1)}) custom-call(s32[3]{0:T(128)S(1)} %pad_add_fusion.place_ref, f32[16,2944]{1,0:T(8,128)S(1)} %get-tuple-element.48.keep_ref, bf16[16,2944]{1,0:T(8,128)(2,1)S(1)} %collective-permute-done.3.near_ref, bf16[16,2944]{1,0:T(8,128)(2,1)S(1)} %collective-permute-done.4.back_ref, ...), custom_call_target="tpu_custom_call" | custom-call | tf_op jit(solution)/shard_map/norm/pallas_call | solution.py:243
  41.3 0.0 collective-permute-done.6
  41.4 0.0 collective-permute-done.7
  41.4 7.4 %all-to-all-start.1 = ((bf16[16,16,2944]{2,1,0:T(8,128)(2,1)}), bf16[16,16,2944]{2,1,0:T(8,128)(2,1)S(1)}, u32[]{:S(2)}, u32[]{:S(2)}) async-start(bf16[16,16,2944]{2,1,0:T(8,128)(2,1)} %get-tuple-element.59), calls=%async_computation.1 | async-start | bytes 3014656 | tf_op jit(solution)/shard_map/all_to_all | solution.py:336
  48.8 0.0 copy-start.1
  48.8 0.0 copy-start.2
  48.8 4.9 %copy_bitcast_fusion = (bf16[2,180,2880]{2,1,0:T(8,128)(2,1)}, bf16[2,180,2880]{2,1,0:T(8,128)(2,1)}) fusion(bf16[2,2880,180]{1,0,2:T(2,128)(2,1)} %collective-permute-done.7, bf16[2,2880,180]{1,0,2:T(2,128)(2,1)} %collective-permute-done.6), kind=kLoop, calls=%fused_computation | loop fusion | bytes 8294400 | tf_op jit(solution)/shard_map/transpose | solution.py:395
  53.7 0.0 copy-done.1
  53.7 0.0 copy-done.2
  53.7 2.6 %copy_bitcast_fusion.2 = (bf16[2,180,2880]{2,1,0:T(8,128)(2,1)}, bf16[2,180,2880]{2,1,0:T(8,128)(2,1)}) fusion(bf16[2,2880,180]{1,0,2:T(2,128)(2,1)S(1)} %copy-done.1, bf16[2,2880,180]{1,0,2:T(2,128)(2,1)S(1)} %copy-done.2), kind=kLoop, calls=%fused_computation.2 | loop fusion | bytes 8294400 | tf_op jit(solution)/shard_map/transpose | solution.py:395
  56.3 10.9 %all-to-all-done.1 = bf16[16,16,2944]{2,1,0:T(8,128)(2,1)S(1)} async-done(((bf16[16,16,2944]{2,1,0:T(8,128)(2,1)}), bf16[16,16,2944]{2,1,0:T(8,128)(2,1)S(1)}, u32[]{:S(2)}, u32[]{:S(2)}) %all-to-all-start.1) | async-done | bytes 1507360 | tf_op jit(solution)/shard_map/all_to_all | solution.py:336
  67.3 8.0 %experts.1 = bf16[256,2880]{1,0:T(8,128)(2,1)S(1)} custom-call(s32[2]{0:T(128)S(1)} %pad_add_fusion.1.first_ref, bf16[256,2944]{1,0:T(8,128)(2,1)S(1)} %bitcast.18, bf16[2,180,2880]{2,1,0:T(8,128)(2,1)} %get-tuple-element.65.g0_hbm, bf16[2,180,2880]{2,1,0:T(8,128)(2,1)} %get-tuple-element.66.u0_hbm, bf16[2,180,2880]{2,1,0:T(8,128)(2,1)} %get-tuple-element.67.g1_hbm, ...), custom_call_target="tpu_custom_call" | custom-call | tf_op jit(solution)/shard_map/experts/pallas_call | solution.py:301
  75.3 22.9 %all_to_all.21 = bf16[16,16,2880]{2,1,0:T(8,128)(2,1)S(1)} all-to-all(bf16[16,16,2880]{2,1,0:T(8,128)(2,1)S(1)} %bitcast.19), channel_id=1, replica_groups=mesh['x'=4,'y'=4,'w'=4,'v'=2,'c'=2] {'x','y'}, dimensions={0} | all-to-all | bytes 2949120 | tf_op jit(solution)/shard_map/all_to_all | solution.py:336
  98.2 0.2 reduce_sum.12
  98.5 13.8 %all_to_all.22.part_ref = bf16[8,2,2880]{2,1,0:T(2,128)(2,1)S(1)} all-to-all(bf16[8,2,2880]{2,1,0:T(2,128)(2,1)S(1)} %reshape.11), channel_id=1, replica_groups=mesh['x'=4,'y'=4,'w'=4,'v'=2,'c'=2] {'w','v'}, dimensions={0} | all-to-all | bytes 184320 | tf_op jit(solution)/shard_map/all_to_all | solution.py:336
  112.3 0.6 finish.1
  (3 shorter events, 0.1 us)
Async XLA Ops:
  0.0 26.9 %collective-permute-start.2 = (bf16[2,180,2880]{2,0,1:T(2,128)(2,1)}, bf16[2,180,2880]{2,0,1:T(2,128)(2,1)}, u32[]{:S(2)}, u32[]{:S(2)}) collective-permute-start(bf16[2,180,2880]{2,0,1:T(2,128)(2,1)} %param.27), channel_id=1, source_target_pairs={{0,1},{1,0},{2,3},{3,2},{4,5},{5,4},{6,7},{7,6},{8,9},{9,8},{10,11... | collective-permute-start | bytes 6220808 | tf_op jit(solution)/shard_map/ppermute | solution.py:367
  0.0 41.3 %collective-permute-start.6 = (bf16[2,2880,180]{1,0,2:T(2,128)(2,1)}, bf16[2,2880,180]{1,0,2:T(2,128)(2,1)}, u32[]{:S(2)}, u32[]{:S(2)}) collective-permute-start(bf16[2,2880,180]{1,0,2:T(2,128)(2,1)} %param.25), channel_id=1, source_target_pairs={{0,1},{1,0},{2,3},{3,2},{4,5},{5,4},{6,7},{7,6},{8,9},{9,8},{10,11... | collective-permute-start | bytes 6220808 | tf_op jit(solution)/shard_map/ppermute | solution.py:367
  0.5 40.8 %collective-permute-start.7 = (bf16[2,2880,180]{1,0,2:T(2,128)(2,1)}, bf16[2,2880,180]{1,0,2:T(2,128)(2,1)}, u32[]{:S(2)}, u32[]{:S(2)}) collective-permute-start(bf16[2,2880,180]{1,0,2:T(2,128)(2,1)} %param.26), channel_id=1, source_target_pairs={{0,1},{1,0},{2,3},{3,2},{4,5},{5,4},{6,7},{7,6},{8,9},{9,8},{10,11... | collective-permute-start | bytes 6220808 | tf_op jit(solution)/shard_map/ppermute | solution.py:367
  0.5 20.3 %collective-permute-start = (bf16[2880,256]{1,0:T(8,128)(2,1)}, bf16[2880,256]{1,0:T(8,128)(2,1)S(1)}, u32[]{:S(2)}, u32[]{:S(2)}) collective-permute-start(bf16[2880,256]{1,0:T(8,128)(2,1)} %bitcast.20), channel_id=1, source_target_pairs={{0,1},{1,0},{2,3},{3,2},{4,5},{5,4},{6,7},{7,6},{8,9},{9,8},{10,11... | collective-permute-start | bytes 4423688 | tf_op jit(solution)/shard_map/ppermute | solution.py:365
  4.6 18.4 %copy-start = (bf16[2,180,2880]{2,0,1:T(2,128)(2,1)S(1)}, bf16[2,180,2880]{2,0,1:T(2,128)(2,1)}, u32[]{:S(2)}) copy-start(bf16[2,180,2880]{2,0,1:T(2,128)(2,1)} %param.27) | copy-start | bytes 6220804
  22.2 2.3 %copy-start.3 = (f32[2880]{0:T(1024)S(1)}, f32[2880]{0:T(1024)}, u32[]{:S(2)}) copy-start(f32[2880]{0:T(1024)} %param.22) | copy-start | bytes 34564
  22.3 4.7 %collective-permute-start.1 = (bf16[16,2944]{1,0:T(8,128)(2,1)S(1)}, bf16[16,2944]{1,0:T(8,128)(2,1)S(1)}, u32[]{:S(2)}, u32[]{:S(2)}) collective-permute-start(bf16[16,2944]{1,0:T(8,128)(2,1)S(1)} %get-tuple-element.44), channel_id=1, source_target_pairs={{0,2},{2,0},{1,3},{3,1},{4,6},{6,4},{5,7},{7,5},{8,10},{10,8},{9,1... | collective-permute-start | bytes 282632 | tf_op jit(solution)/shard_map/ppermute | solution.py:380
  26.9 8.1 %collective-permute-start.3 = (bf16[16,2944]{1,0:T(8,128)(2,1)S(1)}, bf16[16,2944]{1,0:T(8,128)(2,1)S(1)}, u32[]{:S(2)}, u32[]{:S(2)}) collective-permute-start(bf16[16,2944]{1,0:T(8,128)(2,1)S(1)} %get-tuple-element.51), channel_id=1, source_target_pairs={{0,4},{4,8},{8,12},{12,0},{1,5},{5,9},{9,13},{13,1},{2,6},{6,10},{... | collective-permute-start | bytes 282632 | tf_op jit(solution)/shard_map/ppermute | solution.py:386
  27.6 9.8 %collective-permute-start.4 = (bf16[16,2944]{1,0:T(8,128)(2,1)S(1)}, bf16[16,2944]{1,0:T(8,128)(2,1)S(1)}, u32[]{:S(2)}, u32[]{:S(2)}) collective-permute-start(bf16[16,2944]{1,0:T(8,128)(2,1)S(1)} %get-tuple-element.51), channel_id=1, source_target_pairs={{0,8},{4,12},{8,0},{12,4},{1,9},{5,13},{9,1},{13,5},{2,10},{6,14},... | collective-permute-start | bytes 282632 | tf_op jit(solution)/shard_map/ppermute | solution.py:386
  30.0 9.3 %collective-permute-start.5 = (bf16[16,2944]{1,0:T(8,128)(2,1)S(1)}, bf16[16,2944]{1,0:T(8,128)(2,1)S(1)}, u32[]{:S(2)}, u32[]{:S(2)}) collective-permute-start(bf16[16,2944]{1,0:T(8,128)(2,1)S(1)} %get-tuple-element.51), channel_id=1, source_target_pairs={{0,12},{4,0},{8,4},{12,8},{1,13},{5,1},{9,5},{13,9},{2,14},{6,2},{... | collective-permute-start | bytes 282632 | tf_op jit(solution)/shard_map/ppermute | solution.py:386
  41.4 25.9 %all-to-all-start.1 = ((bf16[16,16,2944]{2,1,0:T(8,128)(2,1)}), bf16[16,16,2944]{2,1,0:T(8,128)(2,1)S(1)}, u32[]{:S(2)}, u32[]{:S(2)}) async-start(bf16[16,16,2944]{2,1,0:T(8,128)(2,1)} %get-tuple-element.59), calls=%async_computation.1 | async-start | bytes 3014656 | tf_op jit(solution)/shard_map/all_to_all | solution.py:336
  48.8 5.0 %copy-start.1 = (bf16[2,2880,180]{1,0,2:T(2,128)(2,1)S(1)}, bf16[2,2880,180]{1,0,2:T(2,128)(2,1)}, u32[]{:S(2)}) copy-start(bf16[2,2880,180]{1,0,2:T(2,128)(2,1)} %param.26) | copy-start | bytes 6220804
  48.8 5.0 %copy-start.2 = (bf16[2,2880,180]{1,0,2:T(2,128)(2,1)S(1)}, bf16[2,2880,180]{1,0,2:T(2,128)(2,1)}, u32[]{:S(2)}) copy-start(bf16[2,2880,180]{1,0,2:T(2,128)(2,1)} %param.25) | copy-start | bytes 6220804

commit v13 on v10

--- a/solution.py
+++ b/solution.py
@@ -388,12 +388,12 @@
     copies, *weights = lax.optimization_barrier(
         (copies, gate_weight, up_weight, far_gate, far_up)
     )
-    tokens = exchange(copies, dp)
+    tokens = exchange(copies, ("y", "x"))
     relaid = [row_major(w.swapaxes(1, 2)) for w in weights]
     tokens, gate, up, far_gate, far_up = lax.optimization_barrier((tokens, *relaid))
     tokens = tokens.reshape(ndp * nz * steps, -1)
     made = experts(first, tokens, (gate, up, down), (far_gate, far_up, far_down))
-    back = exchange(made.reshape(ndp, nz * steps, width), dp)
+    back = exchange(made.reshape(ndp, nz * steps, width), ("y", "x"))
     column_sum = jnp.sum(back.astype(F32), axis=0).astype(BF16)
     final = exchange(column_sum.reshape(nz, steps, width), zaxis)
     out = residual + jnp.sum(final.astype(F32), axis=0)

time: 113 us -> 114 us (level)
  no operation moved by 1% of the time
where the time goes in v13:
time: 114 us; the launch traced here: 113 us
  blocking collectives  53.8 us (47%)
  waiting for transfers between devices  16.9 us (15%)
  Pallas kernels  14.3 us (13%)
  starting transfers between devices  14 us (12%)
  local copies, waits for them, and re-layouts  12.3 us (11%)
    all_to_all x3, blocking collectives, exchange(): return lax.all_to_all(value, axis, split_axis=0, concat_axis=0, tiled=True)  53.8 us
    all_to_all x1, waiting for transfers between devices, exchange(): return lax.all_to_all(value, axis, split_axis=0, concat_axis=0, tiled=True)  10.2 us
    pallas_call x1, Pallas kernels, experts(): pl.pallas_call(experts_kernel, in_specs=[smem(), vmem()] + [hbm()] * 6, o...  8 us
    transpose x2, local copies, waits for them, and re-layouts, on_device(): relaid = [row_major(w.swapaxes(1, 2)) for w in weights]  7.53 us
    all_to_all x1, starting transfers between devices, exchange(): return lax.all_to_all(value, axis, split_axis=0, concat_axis=0, tiled=True)  7.41 us
    ppermute x3, starting transfers between devices, on_device(): lax.ppermute(sent, 'w', [(i, (i + k) % quarter) for i in range(quarter)])  4.83 us
    ppermute x3, waiting for transfers between devices, on_device(): lax.ppermute(sent, 'w', [(i, (i + k) % quarter) for i in range(quarter)])  4.4 us
    optimization_barrier x1, local copies, waits for them, and re-layouts, on_device(): sent, far_down = lax.optimization_barrier((sent, far_down))  3.13 us
  transfers between devices with their start and end apart: 9, of which 5 were waited for; matrix products, arithmetic and copies ran while one was open for 11% of the time, Pallas kernels for 6%

profile of v13, /device:TPU:8, one launch (start us, length us, event | category | flops | bytes accessed | tf_op | source)
XLA Modules:
  0.0 113.1 jit_solution(16263153956507860850)
XLA Ops:
  0.0 0.0 collective-permute-start.2
  0.0 0.5 collective-permute-start.6
  0.5 0.0 collective-permute-start.7
  0.5 0.5 collective-permute-start
  1.7 2.1 %attend.1 = (bf16[8,2,512]{2,1,0:T(2,128)(2,1)S(1)}, bf16[2880,256]{1,0:T(8,128)(2,1)S(1)}) custom-call(s32[1]{0:T(128)S(6)} %copy.59.len_ref, bf16[1,2,4096]{2,1,0:T(2,128)(2,1)} %q_hbm.1, bf16[1,2,512]{2,1,0:T(2,128)(2,1)} %nk_hbm.1, bf16[1,2,512]{2,1,0:T(2,128)(2,1)} %nv_hbm.1, bf16[1,512,512]{2,1,0:T(8,128)(2,1)} %k_hbm.1, bf16[1,512,512]{2,1,0:T(8,128)(2,1)} %v_hbm.1, ...), custom_call_target="tpu_custom_call" | custom-call | tf_op jit(solution)/shard_map/attend/pallas_call | solution.py:104
  3.7 0.0 copy-start
  3.8 0.1 pad_add_fusion.1.first_ref
  3.8 0.1 pad_add_fusion.place_ref
  3.9 16.2 %all_to_all.20.x_ref = bf16[8,2,512]{2,1,0:T(2,128)(2,1)S(1)} all-to-all(bf16[8,2,512]{2,1,0:T(2,128)(2,1)S(1)} %get-tuple-element.40), channel_id=1, replica_groups=mesh['x'=4,'y'=4,'w'=4,'v'=2,'c'=2] {'w','v'}, dimensions={0} | all-to-all | bytes 32768 | tf_op jit(solution)/shard_map/all_to_all | solution.py:334
  20.1 0.0 collective-permute-done.other_ref
  20.1 2.2 %project.1 = (f32[16,2944]{1,0:T(8,128)S(1)}, bf16[16,2944]{1,0:T(8,128)(2,1)S(1)}) custom-call(s32[3]{0:T(128)S(1)} %pad_add_fusion.place_ref, bf16[8,2,512]{2,1,0:T(2,128)(2,1)S(1)} %all_to_all.20.x_ref, bf16[2880,256]{1,0:T(8,128)(2,1)S(1)} %get-tuple-element.41.own_ref, bf16[2880,256]{1,0:T(8,128)(2,1)S(1)} %collective-permute-done.other_ref, ...), custom_call_target="tpu_custom_call" | custom-call | tf_op jit(solution)/shard_map/project/pallas_call | solution.py:186
  22.3 0.0 copy-start.3
  22.3 0.7 collective-permute-start.1
  23.0 0.0 copy-done
  23.0 1.6 %copy.47.d0_hbm = bf16[2,180,2880]{2,1,0:T(8,128)(2,1)} copy(bf16[2,180,2880]{2,0,1:T(2,128)(2,1)S(1)} %copy-done) | data formatting | bytes 4147200 | tf_op jit(solution)/shard_map/optimization_barrier | solution.py:376
  24.5 0.0 copy-done.3
  24.6 2.4 %collective-permute-done.1.got_ref = bf16[16,2944]{1,0:T(8,128)(2,1)S(1)} collective-permute-done((bf16[16,2944]{1,0:T(8,128)(2,1)S(1)}, bf16[16,2944]{1,0:T(8,128)(2,1)S(1)}, u32[]{:S(2)}, u32[]{:S(2)}) %collective-permute-start.1) | collective-permute-done | bytes 94240 | tf_op jit(solution)/shard_map/ppermute | solution.py:377
  27.0 0.0 collective-permute-done.2
  27.0 0.7 collective-permute-start.3
  27.6 2.4 %collective-permute-start.4 = (bf16[16,2944]{1,0:T(8,128)(2,1)S(1)}, bf16[16,2944]{1,0:T(8,128)(2,1)S(1)}, u32[]{:S(2)}, u32[]{:S(2)}) collective-permute-start(bf16[16,2944]{1,0:T(8,128)(2,1)S(1)} %get-tuple-element.51), channel_id=1, source_target_pairs={{0,8},{4,12},{8,0},{12,4},{1,9},{5,13},{9,1},{13,5},{2,10},{6,14},... | collective-permute-start | bytes 282632 | tf_op jit(solution)/shard_map/ppermute | solution.py:383
  30.1 1.8 %collective-permute-start.5 = (bf16[16,2944]{1,0:T(8,128)(2,1)S(1)}, bf16[16,2944]{1,0:T(8,128)(2,1)S(1)}, u32[]{:S(2)}, u32[]{:S(2)}) collective-permute-start(bf16[16,2944]{1,0:T(8,128)(2,1)S(1)} %get-tuple-element.51), channel_id=1, source_target_pairs={{0,12},{4,0},{8,4},{12,8},{1,13},{5,1},{9,5},{13,9},{2,14},{6,2},{... | collective-permute-start | bytes 282632 | tf_op jit(solution)/shard_map/ppermute | solution.py:383
  31.8 3.1 %copy.48.d1_hbm = bf16[2,180,2880]{2,1,0:T(8,128)(2,1)} copy(bf16[2,180,2880]{2,0,1:T(2,128)(2,1)} %collective-permute-done.2) | data formatting | bytes 4147200 | tf_op jit(solution)/shard_map/optimization_barrier | solution.py:380
  34.9 0.2 collective-permute-done.3.near_ref
  35.1 2.4 %collective-permute-done.4.back_ref = bf16[16,2944]{1,0:T(8,128)(2,1)S(1)} collective-permute-done((bf16[16,2944]{1,0:T(8,128)(2,1)S(1)}, bf16[16,2944]{1,0:T(8,128)(2,1)S(1)}, u32[]{:S(2)}, u32[]{:S(2)}) %collective-permute-start.4) | collective-permute-done | bytes 94240 | tf_op jit(solution)/shard_map/ppermute | solution.py:383
  37.5 1.9 %collective-permute-done.5.far_ref = bf16[16,2944]{1,0:T(8,128)(2,1)S(1)} collective-permute-done((bf16[16,2944]{1,0:T(8,128)(2,1)S(1)}, bf16[16,2944]{1,0:T(8,128)(2,1)S(1)}, u32[]{:S(2)}, u32[]{:S(2)}) %collective-permute-start.5) | collective-permute-done | bytes 94240 | tf_op jit(solution)/shard_map/ppermute | solution.py:383
  39.3 2.0 %norm.1 = (f32[2,2880]{1,0:T(2,128)S(1)}, bf16[16,16,2944]{2,1,0:T(8,128)(2,1)}) custom-call(s32[3]{0:T(128)S(1)} %pad_add_fusion.place_ref, f32[16,2944]{1,0:T(8,128)S(1)} %get-tuple-element.48.keep_ref, bf16[16,2944]{1,0:T(8,128)(2,1)S(1)} %collective-permute-done.3.near_ref, bf16[16,2944]{1,0:T(8,128)(2,1)S(1)} %collective-permute-done.4.back_ref, ...), custom_call_target="tpu_custom_call" | custom-call | tf_op jit(solution)/shard_map/norm/pallas_call | solution.py:254
  41.3 0.0 collective-permute-done.6
  41.4 0.0 collective-permute-done.7
  41.4 7.4 %all-to-all-start.1 = ((bf16[16,16,2944]{2,1,0:T(8,128)(2,1)}), bf16[16,16,2944]{2,1,0:T(8,128)(2,1)S(1)}, u32[]{:S(2)}, u32[]{:S(2)}) async-start(bf16[16,16,2944]{2,1,0:T(8,128)(2,1)} %get-tuple-element.59), calls=%async_computation.1 | async-start | bytes 3014656 | tf_op jit(solution)/shard_map/all_to_all | solution.py:334
  48.8 0.0 copy-start.1
  48.8 0.0 copy-start.2
  48.8 4.9 %copy_bitcast_fusion = (bf16[2,180,2880]{2,1,0:T(8,128)(2,1)}, bf16[2,180,2880]{2,1,0:T(8,128)(2,1)}) fusion(bf16[2,2880,180]{1,0,2:T(2,128)(2,1)} %collective-permute-done.7, bf16[2,2880,180]{1,0,2:T(2,128)(2,1)} %collective-permute-done.6), kind=kLoop, calls=%fused_computation | loop fusion | bytes 8294400 | tf_op jit(solution)/shard_map/transpose | solution.py:392
  53.7 0.0 copy-done.1
  53.7 0.0 copy-done.2
  53.7 2.6 %copy_bitcast_fusion.2 = (bf16[2,180,2880]{2,1,0:T(8,128)(2,1)}, bf16[2,180,2880]{2,1,0:T(8,128)(2,1)}) fusion(bf16[2,2880,180]{1,0,2:T(2,128)(2,1)S(1)} %copy-done.1, bf16[2,2880,180]{1,0,2:T(2,128)(2,1)S(1)} %copy-done.2), kind=kLoop, calls=%fused_computation.2 | loop fusion | bytes 8294400 | tf_op jit(solution)/shard_map/transpose | solution.py:392
  56.3 10.2 %all-to-all-done.1 = bf16[16,16,2944]{2,1,0:T(8,128)(2,1)S(1)} async-done(((bf16[16,16,2944]{2,1,0:T(8,128)(2,1)}), bf16[16,16,2944]{2,1,0:T(8,128)(2,1)S(1)}, u32[]{:S(2)}, u32[]{:S(2)}) %all-to-all-start.1) | async-done | bytes 1507360 | tf_op jit(solution)/shard_map/all_to_all | solution.py:334
  66.5 8.0 %experts.1 = bf16[256,2880]{1,0:T(8,128)(2,1)S(1)} custom-call(s32[2]{0:T(128)S(1)} %pad_add_fusion.1.first_ref, bf16[256,2944]{1,0:T(8,128)(2,1)S(1)} %bitcast.20, bf16[2,180,2880]{2,1,0:T(8,128)(2,1)} %get-tuple-element.65.g0_hbm, bf16[2,180,2880]{2,1,0:T(8,128)(2,1)} %get-tuple-element.66.u0_hbm, bf16[2,180,2880]{2,1,0:T(8,128)(2,1)} %get-tuple-element.67.g1_hbm, ...), custom_call_target="tpu_custom_call" | custom-call | tf_op jit(solution)/shard_map/experts/pallas_call | solution.py:317
  74.5 21.8 %all_to_all.21 = bf16[16,16,2880]{2,1,0:T(8,128)(2,1)S(1)} all-to-all(bf16[16,16,2880]{2,1,0:T(8,128)(2,1)S(1)} %bitcast.21), channel_id=1, replica_groups=mesh['x'=4,'y'=4,'w'=4,'v'=2,'c'=2] {'y','x'}, dimensions={0} | all-to-all | bytes 2949120 | tf_op jit(solution)/shard_map/all_to_all | solution.py:334
  96.3 0.2 reduce_sum.21
  96.5 15.9 %all_to_all.22 = bf16[8,2,2880]{2,1,0:T(2,128)(2,1)S(1)} all-to-all(bf16[8,2,2880]{2,1,0:T(2,128)(2,1)S(1)} %reshape.11), channel_id=1, replica_groups=mesh['x'=4,'y'=4,'w'=4,'v'=2,'c'=2] {'w','v'}, dimensions={0} | all-to-all | bytes 184320 | tf_op jit(solution)/shard_map/all_to_all | solution.py:334
  112.4 0.1 convert_reduce_fusion
  112.5 0.6 fusion
  (3 shorter events, 0.1 us)
Async XLA Ops:
  0.0 27.0 %collective-permute-start.2 = (bf16[2,180,2880]{2,0,1:T(2,128)(2,1)}, bf16[2,180,2880]{2,0,1:T(2,128)(2,1)}, u32[]{:S(2)}, u32[]{:S(2)}) collective-permute-start(bf16[2,180,2880]{2,0,1:T(2,128)(2,1)} %param.27), channel_id=1, source_target_pairs={{0,1},{1,0},{2,3},{3,2},{4,5},{5,4},{6,7},{7,6},{8,9},{9,8},{10,11... | collective-permute-start | bytes 6220808 | tf_op jit(solution)/shard_map/ppermute | solution.py:365
  0.0 41.3 %collective-permute-start.6 = (bf16[2,2880,180]{1,0,2:T(2,128)(2,1)}, bf16[2,2880,180]{1,0,2:T(2,128)(2,1)}, u32[]{:S(2)}, u32[]{:S(2)}) collective-permute-start(bf16[2,2880,180]{1,0,2:T(2,128)(2,1)} %param.25), channel_id=1, source_target_pairs={{0,1},{1,0},{2,3},{3,2},{4,5},{5,4},{6,7},{7,6},{8,9},{9,8},{10,11... | collective-permute-start | bytes 6220808 | tf_op jit(solution)/shard_map/ppermute | solution.py:365
  0.5 40.8 %collective-permute-start.7 = (bf16[2,2880,180]{1,0,2:T(2,128)(2,1)}, bf16[2,2880,180]{1,0,2:T(2,128)(2,1)}, u32[]{:S(2)}, u32[]{:S(2)}) collective-permute-start(bf16[2,2880,180]{1,0,2:T(2,128)(2,1)} %param.26), channel_id=1, source_target_pairs={{0,1},{1,0},{2,3},{3,2},{4,5},{5,4},{6,7},{7,6},{8,9},{9,8},{10,11... | collective-permute-start | bytes 6220808 | tf_op jit(solution)/shard_map/ppermute | solution.py:365
  0.5 19.6 %collective-permute-start = (bf16[2880,256]{1,0:T(8,128)(2,1)}, bf16[2880,256]{1,0:T(8,128)(2,1)S(1)}, u32[]{:S(2)}, u32[]{:S(2)}) collective-permute-start(bf16[2880,256]{1,0:T(8,128)(2,1)} %bitcast.22), channel_id=1, source_target_pairs={{0,1},{1,0},{2,3},{3,2},{4,5},{5,4},{6,7},{7,6},{8,9},{9,8},{10,11... | collective-permute-start | bytes 4423688 | tf_op jit(solution)/shard_map/ppermute | solution.py:363
  3.7 19.2 %copy-start = (bf16[2,180,2880]{2,0,1:T(2,128)(2,1)S(1)}, bf16[2,180,2880]{2,0,1:T(2,128)(2,1)}, u32[]{:S(2)}) copy-start(bf16[2,180,2880]{2,0,1:T(2,128)(2,1)} %param.27) | copy-start | bytes 6220804
  22.3 2.3 %copy-start.3 = (f32[2880]{0:T(1024)S(1)}, f32[2880]{0:T(1024)}, u32[]{:S(2)}) copy-start(f32[2880]{0:T(1024)} %param.22) | copy-start | bytes 34564
  22.3 4.7 %collective-permute-start.1 = (bf16[16,2944]{1,0:T(8,128)(2,1)S(1)}, bf16[16,2944]{1,0:T(8,128)(2,1)S(1)}, u32[]{:S(2)}, u32[]{:S(2)}) collective-permute-start(bf16[16,2944]{1,0:T(8,128)(2,1)S(1)} %get-tuple-element.44), channel_id=1, source_target_pairs={{0,2},{2,0},{1,3},{3,1},{4,6},{6,4},{5,7},{7,5},{8,10},{10,8},{9,1... | collective-permute-start | bytes 282632 | tf_op jit(solution)/shard_map/ppermute | solution.py:377
  27.0 8.1 %collective-permute-start.3 = (bf16[16,2944]{1,0:T(8,128)(2,1)S(1)}, bf16[16,2944]{1,0:T(8,128)(2,1)S(1)}, u32[]{:S(2)}, u32[]{:S(2)}) collective-permute-start(bf16[16,2944]{1,0:T(8,128)(2,1)S(1)} %get-tuple-element.51), channel_id=1, source_target_pairs={{0,4},{4,8},{8,12},{12,0},{1,5},{5,9},{9,13},{13,1},{2,6},{6,10},{... | collective-permute-start | bytes 282632 | tf_op jit(solution)/shard_map/ppermute | solution.py:383
  27.6 9.9 %collective-permute-start.4 = (bf16[16,2944]{1,0:T(8,128)(2,1)S(1)}, bf16[16,2944]{1,0:T(8,128)(2,1)S(1)}, u32[]{:S(2)}, u32[]{:S(2)}) collective-permute-start(bf16[16,2944]{1,0:T(8,128)(2,1)S(1)} %get-tuple-element.51), channel_id=1, source_target_pairs={{0,8},{4,12},{8,0},{12,4},{1,9},{5,13},{9,1},{13,5},{2,10},{6,14},... | collective-permute-start | bytes 282632 | tf_op jit(solution)/shard_map/ppermute | solution.py:383
  30.1 9.3 %collective-permute-start.5 = (bf16[16,2944]{1,0:T(8,128)(2,1)S(1)}, bf16[16,2944]{1,0:T(8,128)(2,1)S(1)}, u32[]{:S(2)}, u32[]{:S(2)}) collective-permute-start(bf16[16,2944]{1,0:T(8,128)(2,1)S(1)} %get-tuple-element.51), channel_id=1, source_target_pairs={{0,12},{4,0},{8,4},{12,8},{1,13},{5,1},{9,5},{13,9},{2,14},{6,2},{... | collective-permute-start | bytes 282632 | tf_op jit(solution)/shard_map/ppermute | solution.py:383
  41.4 25.1 %all-to-all-start.1 = ((bf16[16,16,2944]{2,1,0:T(8,128)(2,1)}), bf16[16,16,2944]{2,1,0:T(8,128)(2,1)S(1)}, u32[]{:S(2)}, u32[]{:S(2)}) async-start(bf16[16,16,2944]{2,1,0:T(8,128)(2,1)} %get-tuple-element.59), calls=%async_computation.1 | async-start | bytes 3014656 | tf_op jit(solution)/shard_map/all_to_all | solution.py:334
  48.8 5.0 %copy-start.1 = (bf16[2,2880,180]{1,0,2:T(2,128)(2,1)S(1)}, bf16[2,2880,180]{1,0,2:T(2,128)(2,1)}, u32[]{:S(2)}) copy-start(bf16[2,2880,180]{1,0,2:T(2,128)(2,1)} %param.26) | copy-start | bytes 6220804
  48.8 4.9 %copy-start.2 = (bf16[2,2880,180]{1,0,2:T(2,128)(2,1)S(1)}, bf16[2,2880,180]{1,0,2:T(2,128)(2,1)}, u32[]{:S(2)}) copy-start(bf16[2,2880,180]{1,0,2:T(2,128)(2,1)} %param.25) | copy-start | bytes 6220804
